TPU v7x, 32 devices: a whole 2x2x4 slice. The times are simulated.
32 devices in a mesh: ctx: 16 (over z, x, core), fsdp: 2 (over y).
Axes of the slice: x: 2, y: 2, z: 4, core: 2. Of those that a mesh axis runs over, the one named last changes fastest.
Arguments:
- tokens: bfloat16 [2, 4096, 768], P('fsdp', 'ctx'), may hold values from -6 to 6
- cotangent: bfloat16 [2, 4096, 768], P('fsdp', 'ctx'), may hold values from -6 to 6
- lengths: int32 [2, 3], P('fsdp'), may hold values from 1 to 2048, 4096 in all within a row
- deal: int32 [2, 32], P('fsdp'), may hold values from 0 to 31, each once within a row
- joint_projection: bfloat16 [768, 2304], P('fsdp'), may hold values from -0.21875 to 0.21875
- output_projection: bfloat16 [768, 768], P('fsdp'), may hold values from -3 to 3
- expand_weight: bfloat16 [768, 2304], P('fsdp'), may hold values from -0.21875 to 0.21875
- contract_weight: bfloat16 [1152, 768], P('fsdp'), may hold values from -0.1875 to 0.1875
- gain_first: bfloat16 [768], P('fsdp'), may hold values from 0.099609375 to 1.8984375
- gain_second: bfloat16 [768], P('fsdp'), may hold values from 0.099609375 to 1.8984375
Outputs:
- output: bfloat16 [2, 4096, 768], P('fsdp', 'ctx')
- input_grad: bfloat16 [2, 4096, 768], P('fsdp', 'ctx')
- joint_grad: float32 [768, 2304], P('ctx')
- output_grad: float32 [768, 768], P('ctx')
- expand_grad: float32 [768, 2304], P('ctx')
- contract_grad: float32 [1152, 768], P('ctx')
- gain_first_grad: float32 [768], P('ctx')
- gain_second_grad: float32 [768], P('ctx')
Inputs may be any that keep to these rules, and one draw needn't show every extreme that they name: Each row of 3 lengths sums to 4096, and its longest is exactly 2048. Each row deal[g, :] is a permutation of the 32 blocks of a group.
All inputs are finite; a program needn't handle non-finite values.
Results may differ from a plain program's by a relative error of at most 0.029.
Values may be sent and summed in bfloat16 or wider, within the bound.
A program may use at most 192 MiB of HBM per device.

v0:
```python
import functools

import jax
import jax.numpy as jnp
from jax import lax
from jax.experimental import pallas as pl
from jax.experimental.pallas import tpu as pltpu
from jax.sharding import PartitionSpec as P

FF = 1152
HEADS = 12
HEAD_DIM = 64
BLOCK = 128
PLANES = 4
HD = HEAD_DIM
HALF = HEAD_DIM // 2
HP = HEADS // PLANES
QW = HP * HEAD_DIM
rope_base = 160000.0
norm_eps = 1e-05
MASKED = -1e30


def ends_of(lengths_ref, count):
    ends, total = [], 0
    for i in range(count):
        total = total + lengths_ref[0, i]
        ends.append(total)
    return ends


def span_of(index, ends):
    begin, end = jnp.zeros_like(index), jnp.full_like(index, ends[0])
    for before, after in zip(ends[:-1], ends[1:]):
        begin = jnp.where(index >= before, before, begin)
        end = jnp.where(index >= before, after, end)
    return begin, end


def head_rows(x, head):
    rows = lax.broadcasted_iota(jnp.int32, x.shape, 0)
    return jnp.where((rows >= head * HD) & (rows < (head + 1) * HD), x, jnp.zeros_like(x))


def query_block(n, b, T, ends):
    S = n // PLANES
    me = lax.axis_index("ctx")
    base = (lax.rem(me // S + PLANES - b, PLANES) * S + lax.rem(me, S)) * T
    low_begin, low_end = span_of(base, ends)
    high_begin, high_end = span_of(base + T - 1, ends)
    low, high = low_begin // T, (high_end + T - 1) // T
    full_low = jnp.clip((high_begin + T - 1) // T, low, high)
    full_high = jnp.clip(low_end // T, full_low, high)
    begin, end = span_of(base + lax.broadcasted_iota(jnp.int32, (8, T), 1), ends)
    return (low, full_low, full_high, high), begin[0:1], end[0:1]


def over_units(bounds, step):
    low, full_low, full_high, high = bounds

    def run(begin, end, masked):
        def body(u, carry):
            step(u, masked)
            return carry

        lax.fori_loop(begin, end, body, 0)

    run(low, full_low, True)
    in_pairs(full_low, full_high, lambda u: step(u, False))
    run(full_high, high, True)


def in_pairs(begin, end, step):
    pairs = (end - begin) // 2

    def two(i, carry):
        step(begin + 2 * i)
        step(begin + 2 * i + 1)
        return carry

    def one(u, carry):
        step(u)
        return carry

    lax.fori_loop(0, pairs, two, 0)
    lax.fori_loop(begin + 2 * pairs, end, one, 0)


def fwd_kernel(n, count, lengths_ref, qt_ref, kv_ref, ot_ref, lowt_ref, lse_ref, values, scores, top, total, acc):
    units, T, _ = kv_ref.shape
    ends = ends_of(lengths_ref, count)

    def flip(u, carry):
        values[u] = kv_ref[u, :, 128:].T
        return carry

    lax.fori_loop(0, units, flip, 0, unroll=4)

    def one_query_block(b, carry):
        qt = qt_ref[b]
        qheads = [head_rows(qt, h) for h in range(HP)]
        bounds, q_start, q_end = query_block(n, b, T, ends)
        top[...] = jnp.full_like(top, MASKED)
        total[...] = jnp.zeros_like(total)
        acc[...] = jnp.zeros_like(acc)

        def score(u, masked):
            k = kv_ref[u, :, :QW]
            st = [jnp.dot(k, qheads[h], preferred_element_type=jnp.float32) for h in range(HP)]
            if masked:
                at = u * T + lax.broadcasted_iota(jnp.int32, (T, T), 0)
                allowed = (at >= q_start) & (at < q_end)
                st = [jnp.where(allowed, s, MASKED) for s in st]
            for h in range(HP):
                scores[u, h] = st[h]
                top[h] = jnp.maximum(top[h], jnp.max(st[h].reshape(T // 8, 8, T), axis=0))

        over_units(bounds, score)
        m = [jnp.max(top[h], axis=0, keepdims=True) for h in range(HP)]

        def gather(u):
            p = [jnp.exp(scores[u, h] - m[h]) for h in range(HP)]
            for h in range(HP):
                total[h] += jnp.sum(p[h].reshape(T // 8, 8, T), axis=0)
                rows = pl.ds(h * HD, HD)
                acc[rows, :] += jnp.dot(
                    values[u, pl.ds(HD + h * HD, HD), :], p[h].astype(jnp.bfloat16), preferred_element_type=jnp.float32
                )

        in_pairs(bounds[0], bounds[3], gather)
        for h in range(HP):
            rows = pl.ds(h * HD, HD)
            l = jnp.sum(total[h], axis=0, keepdims=True)
            o = acc[rows, :] / l
            ot_ref[b, rows, :] = o
            lowt_ref[b, rows, :] = o.astype(jnp.bfloat16)
            lse_ref[b, h : h + 1, :] = m[h] + jnp.log(l)
        return carry

    lax.fori_loop(0, qt_ref.shape[0], one_query_block, 0)


def attn_fwd(n, lengths, qt, kv):
    B, _, T = qt.shape
    U = kv.shape[0]
    sm, vm = pl.BlockSpec(memory_space=pltpu.SMEM), pl.BlockSpec(memory_space=pltpu.VMEM)
    return pl.pallas_call(
        functools.partial(fwd_kernel, n, lengths.shape[1]),
        out_shape=(
            jax.ShapeDtypeStruct((B, QW, T), jnp.float32),
            jax.ShapeDtypeStruct((B, QW, T), jnp.bfloat16),
            jax.ShapeDtypeStruct((B, 8, T), jnp.float32),
        ),
        in_specs=[sm, vm, vm],
        out_specs=(vm, vm, vm),
        scratch_shapes=[
            pltpu.VMEM((U, 256, T), jnp.bfloat16),
            pltpu.VMEM((U, HP, T, T), jnp.float32),
            pltpu.VMEM((HP, 8, T), jnp.float32),
            pltpu.VMEM((HP, 8, T), jnp.float32),
            pltpu.VMEM((QW, T), jnp.float32),
        ],
        compiler_params=pltpu.CompilerParams(vmem_limit_bytes=60 << 20),
    )(lengths, qt, kv)


def bwd_kernel(n, count, lengths_ref, qt_ref, kv_ref, ot_ref, lse_ref, gt_ref, dqt_ref, dkv_ref, keys, dk, dv, dq):
    units, T, _ = kv_ref.shape
    ends = ends_of(lengths_ref, count)

    def flip(u, carry):
        keys[u] = kv_ref[u, :, :256].T
        dk[u] = jnp.zeros_like(dk[u])
        dv[u] = jnp.zeros_like(dv[u])
        return carry

    lax.fori_loop(0, units, flip, 0, unroll=4)

    def one_query_block(b, carry):
        qt, gt = qt_ref[b], gt_ref[b]
        zero = jnp.zeros((HD, T), jnp.bfloat16)
        qheads = [head_rows(qt, h) for h in range(HP)]
        gheads = [head_rows(gt, h) for h in range(HP)]
        gpad = [jnp.concatenate([zero, x], axis=0) for x in gheads]
        q = jnp.concatenate([jnp.concatenate([x, zero], axis=0).T for x in qheads], axis=0)
        g = jnp.concatenate([x.T for x in gpad], axis=0)
        bounds, q_start, q_end = query_block(n, b, T, ends)
        prod = gt.astype(jnp.float32) * ot_ref[b]
        delta = [jnp.sum(prod[h * HD : (h + 1) * HD], axis=0, keepdims=True) for h in range(HP)]
        lse = [lse_ref[b, h : h + 1, :] for h in range(HP)]
        dq[...] = jnp.zeros_like(dq)

        def one_unit(u, masked):
            k, v = kv_ref[u, :, :QW], kv_ref[u, :, 128:]
            st = [jnp.dot(k, qheads[h], preferred_element_type=jnp.float32) for h in range(HP)]
            dp = [jnp.dot(v, gpad[h], preferred_element_type=jnp.float32) for h in range(HP)]
            st = [st[h] - lse[h] for h in range(HP)]
            if masked:
                at = u * T + lax.broadcasted_iota(jnp.int32, (T, T), 0)
                allowed = (at >= q_start) & (at < q_end)
                st = [jnp.where(allowed, s, MASKED) for s in st]
            p = [jnp.exp(s) for s in st]
            ds = [(p[h] * (dp[h] - delta[h])).astype(jnp.bfloat16) for h in range(HP)]
            p = [x.astype(jnp.bfloat16) for x in p]
            dv[u] += jnp.dot(jnp.concatenate(p, axis=1), g, preferred_element_type=jnp.float32)
            dk[u] += jnp.dot(jnp.concatenate(ds, axis=1), q, preferred_element_type=jnp.float32)
            for h in range(HP):
                rows = pl.ds(h * HD, HD)
                dq[rows, :] += jnp.dot(keys[u, rows, :], ds[h], preferred_element_type=jnp.float32)

        over_units(bounds, one_unit)
        dqt_ref[b] = dq[...] * (HD**-0.5)
        return carry

    lax.fori_loop(0, qt_ref.shape[0], one_query_block, 0)

    def out(u, carry):
        dkv_ref[u, :, :128] = dk[u, :, :128].astype(jnp.bfloat16)
        dkv_ref[u, :, 128:256] = (dk[u, :, 128:] + dv[u, :, :128]).astype(jnp.bfloat16)
        dkv_ref[u, :, 256:] = dv[u, :, 128:].astype(jnp.bfloat16)
        return carry

    lax.fori_loop(0, units, out, 0, unroll=2)


def attn_bwd(n, lengths, qt, kv, ot, lse, gt):
    B, _, T = qt.shape
    U = kv.shape[0]
    sm, vm = pl.BlockSpec(memory_space=pltpu.SMEM), pl.BlockSpec(memory_space=pltpu.VMEM)
    return pl.pallas_call(
        functools.partial(bwd_kernel, n, lengths.shape[1]),
        out_shape=(jax.ShapeDtypeStruct((B, QW, T), jnp.float32), jax.ShapeDtypeStruct((U, T, 2 * QW), jnp.bfloat16)),
        in_specs=[sm] + [vm] * 5,
        out_specs=(vm, vm),
        scratch_shapes=[
            pltpu.VMEM((U, 256, T), jnp.bfloat16),
            pltpu.VMEM((U, T, 256), jnp.float32),
            pltpu.VMEM((U, T, 256), jnp.float32),
            pltpu.VMEM((QW, T), jnp.float32),
        ],
        compiler_params=pltpu.CompilerParams(vmem_limit_bytes=60 << 20),
    )(lengths, qt, kv, ot, lse, gt)
def front_kernel(
    n,
    groups,
    count,
    lengths_ref,
    tokens_ref,
    joint_ref,
    gain_one_ref,
    gain_two_ref,
    freq_ref,
    out_hbm,
    exp_hbm,
    con_hbm,
    first_ref,
    qt_ref,
    kv_ref,
    joint_t_out,
    turn_ref,
    gains_ref,
    out_all,
    exp_all,
    con_all,
    held,
    t_sems,
    cols,
    cols_all,
    gain_held,
    g_sems,
    kv_own,
    kv_sems,
    own_sems,
    w_sems,
    w_local,
    joint_rows,
    out_held,
    exp_held,
    con_held,
):
    bf, f32 = jnp.bfloat16, jnp.float32
    S = n // PLANES
    S2 = S // 2
    T, D = tokens_ref.shape
    me, group = lax.axis_index("ctx"), lax.axis_index("fsdp")
    plane, side = me // S, lax.rem(me, S)
    s2, core = side // 2, lax.rem(side, 2)

    def at(p, a, c, g):
        return (p * S + a * 2 + c, g)

    def side_peer(k):
        return at(plane, lax.rem(s2 + k, S2), core, group)

    def group_peer(k):
        return at(plane, s2, core, lax.rem(group + k, groups))

    core_peer = at(plane, s2, 1 - core, group)

    def remote(source, target, sems, index, device):
        return pltpu.make_async_remote_copy(
            src_ref=source,
            dst_ref=target,
            send_sem=sems.at[0, index],
            recv_sem=sems.at[1, index],
            device_id=device,
            device_id_type=pl.DeviceIdType.MESH,
        )

    barrier = pltpu.get_barrier_semaphore()

    def greet(device):
        pl.semaphore_signal(barrier, inc=1, device_id=device, device_id_type=pl.DeviceIdType.MESH)

    for k in range(1, PLANES):
        greet(at(lax.rem(plane + k, PLANES), s2, core, group))
    for k in range(1, S2):
        greet(side_peer(k))
    for k in range(1, groups):
        greet(group_peer(k))
    greet(core_peer)
    pl.semaphore_wait(barrier, PLANES - 1 + S2 - 1 + groups - 1 + 1)

    def up(p):
        return remote(held.at[p], held.at[p], t_sems, p, at(plane + 1, s2, core, group))

    def down(p):
        return remote(held.at[p], held.at[p], t_sems, PLANES + p, at(plane - 1, s2, core, group))

    held[plane] = tokens_ref[...]

    @pl.when(plane < PLANES - 1)
    def _():
        up(plane).start()

    @pl.when(plane > 0)
    def _():
        down(plane).start()

    pair = 2 * QW
    for part in range(3):
        window = joint_ref[:, pl.ds(pl.multiple_of(part * D + plane // 2 * pair, 128), pair)].T
        chosen = jnp.where(lax.rem(plane, 2) == 0, window[:QW].astype(f32), window[QW:].astype(f32))
        half = 3 * QW // 2
        low, high = part * QW, (part + 1) * QW
        for c in range(2):
            begin, end = max(low, c * half), min(high, (c + 1) * half)
            if begin < end:
                cols[c, begin - c * half : end - c * half] = chosen[begin - low : end - low].astype(bf)
    gain_held[group] = jnp.zeros_like(gain_held[group])
    gain_held[group, 0:1] = gain_one_ref[...].astype(f32)
    gain_held[group, 1:2] = gain_two_ref[...].astype(f32)
    col_moves = [
        remote(cols.at[core], cols_all.at[group, core], g_sems, k - 1, group_peer(k)) for k in range(1, groups)
    ]
    col_hands = []
    for k in range(1, groups):
        came = cols_all.at[lax.rem(group + groups - k, groups), core]
        col_hands.append(remote(came, came, g_sems, 2 * (groups - 1) + k - 1, core_peer))
    gain_moves = [
        remote(gain_held.at[group], gain_held.at[group], g_sems, groups - 1 + k - 1, group_peer(k))
        for k in range(1, groups)
    ]
    for copy in gain_moves + col_moves:
        copy.start()
    cols_all[group] = cols[...]

    weights = [(out_hbm, out_all, out_held), (exp_hbm, exp_all, exp_held), (con_hbm, con_all, con_held)]
    w_in, w_own, w_first, w_second = [], [], [], []
    for i, (source, target, bounce) in enumerate(weights):
        w_in.append(pltpu.make_async_copy(source, bounce, w_local.at[0, i]))
        w_own.append(pltpu.make_async_copy(bounce, target.at[group], w_local.at[1, i]))
        for k in range(1, groups):
            index = (i * (groups - 1) + k - 1) * 2
            w_first.append(remote(source.at[core], target.at[group, core], w_sems, index, group_peer(k)))
            came = lax.rem(group + groups - k, groups)
            w_second.append(remote(target.at[came, core], target.at[came, core], w_sems, index + 1, core_peer))
    for copy in w_in:
        copy.start()

    ends = ends_of(lengths_ref, count)
    for j in range(PLANES):
        base = (lax.rem(plane + PLANES - j, PLANES) * S + side) * T
        index = base + lax.broadcasted_iota(jnp.int32, (8, T), 1)
        begin, _ = span_of(index, ends)
        angles = (index - begin)[0:1].astype(f32) * freq_ref[...]
        turn_ref[j, :HALF] = jnp.cos(angles)
        turn_ref[j, HALF:] = jnp.sin(angles)

    strip = 64

    def kv_unit(p, a, c):
        return p * S + a * 2 + c

    def side_kv(j, k):
        p = lax.rem(plane + PLANES - j, PLANES)
        return remote(kv_own.at[j], kv_ref.at[kv_unit(p, s2, core)], kv_sems, j * (2 * S2 - 1) + k - 1, side_peer(k))

    def core_kv(j, k):
        p = lax.rem(plane + PLANES - j, PLANES)
        unit = kv_unit(p, lax.rem(s2 + S2 - k, S2), core)
        source = kv_own.at[j] if k == 0 else kv_ref.at[unit]
        return remote(source, kv_ref.at[unit], kv_sems, j * (2 * S2 - 1) + S2 - 1 + k, core_peer)

    def own_kv(j):
        p = lax.rem(plane + PLANES - j, PLANES)
        return pltpu.make_async_copy(kv_own.at[j], kv_ref.at[kv_unit(p, s2, core)], own_sems.at[j])

    def process(p):
        j = lax.rem(plane + PLANES - p, PLANES)

        def norm(i, carry):
            rows = pl.ds(pl.multiple_of(i * strip, strip), strip)
            values = held[p, rows].astype(f32)
            centred = values - jnp.mean(values, axis=-1, keepdims=True)
            spread = jnp.mean(centred * centred, axis=-1, keepdims=True)
            first_ref[j, rows] = (centred * lax.rsqrt(spread + norm_eps) * gains_ref[0:1]).astype(bf)
            return carry

        lax.fori_loop(0, T // strip, norm, 0)
        mixed = lax.dot_general(
            joint_t_out[: 3 * QW], first_ref[j], (((1,), (1,)), ((), ())), preferred_element_type=f32
        )
        cos, sin = turn_ref[j, :HALF], turn_ref[j, HALF:]
        turned = []
        for h in range(2 * HP):
            upper, lower = mixed[h * HD : h * HD + HALF], mixed[h * HD + HALF : (h + 1) * HD]
            turned += [upper * cos - lower * sin, lower * cos + upper * sin]
        q = jnp.concatenate(turned[: 2 * HP], axis=0).astype(bf)
        qt_ref[j] = (q.astype(f32) * HEAD_DIM**-0.5).astype(bf)
        kv_own[j] = jnp.concatenate(turned[2 * HP :] + [mixed[2 * QW :]], axis=0).T.astype(bf)
        for k in range(1, S2):
            side_kv(j, k).start()
        core_kv(j, 0).start()
        own_kv(j).start()

    def hand_on(t):
        @pl.when(plane >= t)
        def _():
            up(plane - t).wait_recv()

            @pl.when(plane < PLANES - 1)
            def _():
                up(plane - t).start()

        @pl.when(plane + t < PLANES)
        def _():
            down(plane + t).wait_recv()

            @pl.when(plane > 0)
            def _():
                down(plane + t).start()

    def process_arrived(t):
        below = jnp.where(plane >= t, 1, 0)
        above = jnp.where(plane + t < PLANES, 1, 0)

        def arrived(i, carry):
            process(jnp.where(i < below, plane - t, plane + t))
            return carry

        lax.fori_loop(0, below + above, arrived, 0)

    hand_on(1)
    for copy in gain_moves:
        copy.wait()
    share = D // groups
    total = jnp.zeros((8, D), f32)
    for g in range(groups):
        rows = lax.broadcasted_iota(jnp.int32, (share, D), 0)
        lanes = lax.broadcasted_iota(jnp.int32, (share, D), 1)
        place = jnp.where(lanes == rows + g * share, 1.0, 0.0).astype(bf)
        total = total + jnp.dot(gain_held[g].astype(bf), place, preferred_element_type=f32)
    gains_ref[...] = total
    for copy, hand in zip(col_moves, col_hands):
        copy.wait()
        hand.start()
    for copy in w_first:
        copy.start()
    for copy in w_in:
        copy.wait()
    for copy in w_own:
        copy.start()
    for copy in col_hands:
        copy.wait()
    width = joint_t_out.shape[0]
    for g in range(groups):
        whole = jnp.concatenate([cols_all[g, 0], cols_all[g, 1], jnp.zeros((width - 3 * QW, share), bf)], axis=0)
        if share % 128 == 0:
            joint_t_out[:, g * share : (g + 1) * share] = whole
        else:
            joint_rows[g * share : (g + 1) * share] = whole.T
    if share % 128:
        for i in range(D // 128):
            joint_t_out[:, i * 128 : (i + 1) * 128] = joint_rows[i * 128 : (i + 1) * 128].T

    process(plane)
    hand_on(2)
    process_arrived(1)
    hand_on(3)
    process_arrived(2)
    process_arrived(3)

    for j in range(PLANES):
        for k in range(1, S2):
            side_kv(j, k).wait_recv()
            core_kv(j, k).start()
    for first_move, second_move in zip(w_first, w_second):
        first_move.wait_recv()
        second_move.start()

    for j in range(PLANES):
        own_kv(j).wait()
        for k in range(1, S2):
            side_kv(j, k).wait_send()
        for k in range(S2):
            core_kv(j, k).wait()
    for p in range(PLANES):

        @pl.when((plane < PLANES - 1) & (plane >= p))
        def _(p=p):
            up(p).wait_send()

        @pl.when((plane > 0) & (plane <= p))
        def _(p=p):
            down(p).wait_send()

    for copy in w_own:
        copy.wait()
    for first_move, second_move in zip(w_first, w_second):
        first_move.wait_send()
        second_move.wait()


def front(n, groups, lengths, tokens, joint_shard, gain_first, gain_second, out_w, exp_w, con_w):
    bf, f32 = jnp.bfloat16, jnp.float32
    S2 = n // PLANES // 2
    T, D = tokens.shape
    width = 3 * QW + 64
    share = D // groups
    any_, vm, sm = (pl.BlockSpec(memory_space=m) for m in (pl.ANY, pltpu.VMEM, pltpu.SMEM))
    sems = lambda count: pltpu.SemaphoreType.DMA((2, count))
    halves = lambda w: w.reshape(2, w.shape[0] // 2, w.shape[1])
    frequencies = rope_base ** (-jnp.arange(0, HEAD_DIM, 2).astype(f32) / HEAD_DIM)
    weights = [halves(w) for w in (out_w, exp_w, con_w)]
    return pl.pallas_call(
        functools.partial(front_kernel, n, groups, lengths.shape[1]),
        out_shape=(
            jax.ShapeDtypeStruct((PLANES, T, D), bf),
            jax.ShapeDtypeStruct((PLANES, QW, T), bf),
            jax.ShapeDtypeStruct((n, T, 2 * QW), bf),
            jax.ShapeDtypeStruct((width, D), bf),
            jax.ShapeDtypeStruct((PLANES, 2 * HALF, T), f32),
            jax.ShapeDtypeStruct((8, D), f32),
            *[jax.ShapeDtypeStruct((groups, *w.shape), bf) for w in weights],
        ),
        in_specs=[sm, vm, vm, vm, vm, vm, any_, any_, any_],
        out_specs=(vm, vm, any_, vm, vm, vm, any_, any_, any_),
        scratch_shapes=[
            pltpu.VMEM((PLANES, T, D), bf),
            sems(2 * PLANES),
            pltpu.VMEM((2, 3 * QW // 2, share), bf),
            pltpu.VMEM((groups, 2, 3 * QW // 2, share), bf),
            pltpu.VMEM((groups, 8, share), f32),
            sems(3 * (groups - 1)),
            pltpu.VMEM((PLANES, T, 2 * QW), bf),
            sems(PLANES * (2 * S2 - 1)),
            pltpu.SemaphoreType.DMA((PLANES,)),
            sems(2 * len(weights) * (groups - 1)),
            pltpu.SemaphoreType.DMA((2, len(weights))),
            pltpu.VMEM((D, width), bf),
            *[pltpu.VMEM(w.shape, bf) for w in weights],
        ],
        compiler_params=pltpu.CompilerParams(collective_id=1, has_side_effects=True, vmem_limit_bytes=60 << 20),
    )(
        lengths,
        tokens,
        joint_shard,
        gain_first[None],
        gain_second[None],
        frequencies[:, None],
        *weights,
    )


def tail_kernel(
    n,
    groups,
    deal_ref,
    dq_ref,
    dkv_ref,
    turn_ref,
    joint_t_hbm,
    first_hbm,
    tokens_hbm,
    grad_hidden_hbm,
    gain_ref,
    packed_hbm,
    dealt_ref,
    shard_ref,
    joint_out_ref,
    joint_t,
    first,
    tokens,
    grad_hidden,
    w_own,
    local_sems,
    kv_near,
    kv_send,
    kv_far,
    kv_sems,
    mixed,
    z_send,
    z_got,
    z_sems,
    jg_t,
    jg,
    j_core,
    j_side,
    j_plane,
    j_group,
    j_sems,
    w_core,
    w_y1,
    w_x1,
    w_x2,
    w_y2,
    w_plane,
    w_z,
    w_all,
    w_sems,
    d_send,
    d_mid,
    d_back,
    d_got,
    d_sems,
):
    bf, f32 = jnp.bfloat16, jnp.float32
    S = n // PLANES
    S2 = S // 2
    T, D = tokens.shape
    me, group = lax.axis_index("ctx"), lax.axis_index("fsdp")
    plane, side = me // S, lax.rem(me, S)
    s2, core = side // 2, lax.rem(side, 2)

    def at(p, a, c, g):
        return (p * S + a * 2 + c, g)

    def plane_peer(k):
        return at(lax.rem(plane + k, PLANES), s2, core, group)

    def side_peer(k):
        return at(plane, lax.rem(s2 + k, S2), core, group)

    def group_peer(k):
        return at(plane, s2, core, lax.rem(group + k, groups))

    core_peer = at(plane, s2, 1 - core, group)

    def remote(source, target, sems, index, device):
        return pltpu.make_async_remote_copy(
            src_ref=source,
            dst_ref=target,
            send_sem=sems.at[0, index],
            recv_sem=sems.at[1, index],
            device_id=device,
            device_id_type=pl.DeviceIdType.MESH,
        )

    barrier = pltpu.get_barrier_semaphore()

    def greet(k, carry):
        pl.semaphore_signal(
            barrier, inc=1, device_id=(lax.rem(me + k, n), group), device_id_type=pl.DeviceIdType.MESH
        )
        return carry

    lax.fori_loop(1, n, greet, 0)
    for k in range(1, groups):
        pl.semaphore_signal(barrier, inc=1, device_id=group_peer(k), device_id_type=pl.DeviceIdType.MESH)
    pl.semaphore_wait(barrier, n - 1 + groups - 1)

    order = [*range(1, PLANES), 0]
    planes = [lax.rem(plane + PLANES - j, PLANES) for j in range(PLANES)]
    core_kv = [remote(dkv_ref.at[planes[j], :, 1 - core], kv_near.at[j], kv_sems, j, core_peer) for j in range(PLANES)]
    for j in order:
        core_kv[j].start()
    local = [
        pltpu.make_async_copy(source, target, local_sems.at[i])
        for i, (source, target) in enumerate(
            [
                (joint_t_hbm, joint_t),
                (first_hbm, first),
                (packed_hbm.at[:, :, core], w_own),
                (tokens_hbm, tokens),
                (grad_hidden_hbm, grad_hidden),
            ]
        )
    ]
    for copy in local:
        copy.start()
    half = PLANES // 2
    core_w = [
        remote(
            packed_hbm.at[pl.ds(i * half, half), :, 1 - core],
            w_core.at[pl.ds(i * half, half)],
            w_sems,
            i,
            core_peer,
        )
        for i in range(2)
    ]
    for copy in core_w:
        copy.start()

    side_kv = {}
    for j in order:
        core_kv[j].wait()
        for k in range(S2):
            total = dkv_ref[planes[j], k, core].astype(f32) + kv_near[j, k].astype(f32)
            kv_send[j, k] = total.astype(bf)
        for k in range(1, S2):
            side_kv[j, k] = remote(
                kv_send.at[j, lax.rem(s2 + S2 - k, S2)],
                kv_far.at[j, k - 1],
                kv_sems,
                PLANES + j * (S2 - 1) + k - 1,
                side_peer(S2 - k),
            )
            side_kv[j, k].start()

    w_moves = []

    def w_copy(source, target, device):
        copy = remote(source, target, w_sems, 2 + len(w_moves), device)
        w_moves.append(copy)
        copy.start()
        return copy

    def add_core(i):
        core_w[i].wait()
        if i == 0:
            local[2].wait()

        def body(step, carry):
            p, a, g = i * half + step // (S2 * groups), lax.rem(step // groups, S2), lax.rem(step, groups)
            w_core[p, a, g] = (w_own[p, a, g].astype(f32) + w_core[p, a, g].astype(f32)).astype(bf)
            return carry

        lax.fori_loop(0, half * S2 * groups, body, 0)

    plane_parts = {}
    local[0].wait()
    for j in order:
        dk = kv_send[j, s2].astype(f32)
        for k in range(1, S2):
            side_kv[j, k].wait()
            dk = dk + kv_far[j, k - 1].astype(f32)
        dk = dk.T
        cos, sin = turn_ref[j, :HALF], turn_ref[j, HALF:]
        rows = []
        for part in (dq_ref[j], dk[:QW]):
            for h in range(HP):
                upper, lower = part[h * HD : h * HD + HALF], part[h * HD + HALF : (h + 1) * HD]
                rows += [upper * cos + lower * sin, lower * cos - upper * sin]
        rows += [dk[QW:], jnp.zeros((mixed.shape[1] - 3 * QW, T), f32)]
        turned = jnp.concatenate(rows, axis=0)
        mixed[j] = turned.astype(bf)
        part = jnp.dot(turned.T.astype(bf), joint_t[...], preferred_element_type=f32)
        z_send[j] = part.astype(bf)
        if j:
            plane_parts[j] = remote(z_send.at[j], z_got.at[j - 1], z_sems, j - 1, plane_peer(PLANES - j))
            plane_parts[j].start()
        if j == order[0]:
            add_core(0)
            y1 = [
                w_copy(w_core.at[pl.ds(0, half), :, lax.rem(group + k, groups)], w_y1.at[k - 1], group_peer(k))
                for k in range(1, groups)
            ]
        elif j == order[1]:
            add_core(1)
            x2 = [
                w_copy(w_core.at[pl.ds(half, half), lax.rem(s2 + k, S2)], w_x2.at[k - 1], side_peer(k))
                for k in range(1, S2)
            ]

    local[1].wait()
    jg_t[...] = jnp.dot(mixed[0], first[0], preferred_element_type=f32)
    for j in range(1, PLANES):
        jg_t[...] += jnp.dot(mixed[j], first[j], preferred_element_type=f32)
    width = jg_t.shape[0]
    shard_rows = jg.shape[3]
    per = 128
    for i in range(D // per):
        block = jg_t[:, i * per : (i + 1) * per]
        gain_part = jnp.sum(block * joint_t[:, i * per : (i + 1) * per].astype(f32), axis=0, keepdims=True)
        whole = jnp.concatenate([block, jnp.broadcast_to(gain_part, (per, per))], axis=0).T.astype(bf)
        j_rows = whole.astype(f32)
        first_row = i * per
        row = first_row
        while row < first_row + per:
            shard, offset = divmod(row, shard_rows)
            count = min(shard_rows - offset, first_row + per - row)
            jg[shard // S, shard % S // 2, shard % 2, offset : offset + count] = j_rows[
                row - first_row : row - first_row + count
            ].astype(bf)
            row += count
    j_moves = []

    def j_copy(source, target, device):
        copy = remote(source, target, j_sems, len(j_moves), device)
        j_moves.append(copy)
        copy.start()
        return copy

    j_first = j_copy(jg.at[:, :, 1 - core], j_core, core_peer)

    def sum_into(target, terms):
        total = terms[0].astype(f32)
        for term in terms[1:]:
            total = total + term.astype(f32)
        return total.astype(target)

    for copy in y1:
        copy.wait()
    for p in range(half):
        for a in range(S2):
            w_y1[0, p, a] = sum_into(bf, [w_core[p, a, group]] + [w_y1[k, p, a] for k in range(groups - 1)])
    x1 = [w_copy(w_y1.at[0, :, lax.rem(s2 + k, S2)], w_x1.at[k - 1], side_peer(k)) for k in range(1, S2)]
    for copy in x2:
        copy.wait()
    for p in range(half):
        for g in range(groups):
            w_x2[0, p, g] = sum_into(bf, [w_core[half + p, s2, g]] + [w_x2[k, p, g] for k in range(S2 - 1)])
    y2 = [w_copy(w_x2.at[0, :, lax.rem(group + k, groups)], w_y2.at[k - 1], group_peer(k)) for k in range(1, groups)]

    j_first.wait()
    for p in range(PLANES):
        for a in range(S2):
            j_core[p, a] = sum_into(bf, [jg[p, a, core], j_core[p, a]])
    j_second = [j_copy(j_core.at[:, lax.rem(s2 + k, S2)], j_side.at[k - 1], side_peer(k)) for k in range(1, S2)]

    local[3].wait()
    local[4].wait()
    for j in range(1, PLANES):
        plane_parts[j].wait()
    strip = 64

    def norm_back(i, carry):
        rows = pl.ds(pl.multiple_of(i * strip, strip), strip)
        grad = z_send[0, rows].astype(f32)
        for j in range(1, PLANES):
            grad = grad + z_got[j - 1, rows].astype(f32)
        values = tokens[rows].astype(f32)
        centred = values - jnp.mean(values, axis=-1, keepdims=True)
        scale = lax.rsqrt(jnp.mean(centred * centred, axis=-1, keepdims=True) + norm_eps)
        normal = centred * scale
        grad = grad * gain_ref[0:1]
        grad = grad - jnp.mean(grad, axis=-1, keepdims=True) - normal * jnp.mean(grad * normal, axis=-1, keepdims=True)
        grad_hidden[rows] = grad_hidden[rows] + grad * scale
        return carry

    lax.fori_loop(0, T // strip, norm_back, 0)

    blocks = T // BLOCK
    piece = BLOCK // n

    def d_copy(source, target, base, k):
        return remote(source.at[lax.rem(me + k, n)], target.at[me], d_sems, base + k, (lax.rem(me + k, n), group))

    for i in range(n):
        d_send[i] = jnp.concatenate(
            [grad_hidden[b * BLOCK + i * piece : b * BLOCK + (i + 1) * piece] for b in range(blocks)], axis=0
        ).astype(bf)
    out_deal = [d_copy(d_send, d_mid, 0, k) for k in range(1, n)]
    for copy in out_deal:
        copy.start()
    d_mid[me] = d_send[me]

    for copy in x1 + y2:
        copy.wait()
    for p in range(half):
        w_plane[p] = sum_into(bf, [w_y1[0, p, s2]] + [w_x1[k, p] for k in range(S2 - 1)])
        w_plane[half + p] = sum_into(bf, [w_x2[0, p, group]] + [w_y2[k, p] for k in range(groups - 1)])
    w_last = [w_copy(w_plane.at[lax.rem(plane + k, PLANES)], w_z.at[k - 1], plane_peer(k)) for k in range(1, PLANES)]
    for copy in j_second:
        copy.wait()
    for p in range(PLANES):
        j_side[0, p] = sum_into(bf, [j_core[p, s2]] + [j_side[k, p] for k in range(S2 - 1)])
    j_third = [j_copy(j_side.at[0, lax.rem(plane + k, PLANES)], j_plane.at[plane], plane_peer(k)) for k in range(1, PLANES)]
    j_plane[plane] = j_side[0, plane]

    for copy in out_deal:
        copy.wait()
    for i in range(n):
        chosen = []
        for b in range(blocks):
            wanted = deal_ref[i * blocks + b]
            held = d_mid[wanted // blocks].astype(f32)
            part = held[:piece]
            for other in range(1, blocks):
                part = jnp.where(lax.rem(wanted, blocks) == other, held[other * piece : (other + 1) * piece], part)
            chosen.append(part)
        d_back[i] = jnp.concatenate(chosen, axis=0).astype(bf)
    back_deal = [d_copy(d_back, d_got, n, k) for k in range(1, n)]
    for copy in back_deal:
        copy.start()
    d_got[me] = d_back[me]

    for copy in w_last:
        copy.wait()
    w_all[group] = sum_into(bf, [w_plane[plane]] + [w_z[k] for k in range(PLANES - 1)])
    w_gather = [w_copy(w_all.at[group], w_all.at[group], group_peer(k)) for k in range(1, groups)]
    for copy in j_third:
        copy.wait()
    j_group[group] = j_plane[...]
    j_last = [j_copy(j_plane, j_group.at[group], group_peer(k)) for k in range(1, groups)]

    for copy in back_deal:
        copy.wait()
    for b in range(blocks):
        for i in range(0, n, 2):
            rows = [d_got[i + e].astype(f32)[b * piece : (b + 1) * piece] for e in range(2)]
            dealt_ref[b * BLOCK + i * piece : b * BLOCK + (i + 2) * piece] = jnp.concatenate(rows, axis=0).astype(bf)
    for copy in w_gather:
        copy.wait()
    for g in range(groups):
        shard_ref[g] = w_all[g].astype(f32)
    for copy in j_last:
        copy.wait()
    for p in range(PLANES):
        total = j_group[0, p].astype(f32)
        for g in range(1, groups):
            total = total + j_group[g, p].astype(f32)
        joint_out_ref[p] = total


def tail(n, groups, deal, dqt, dkv, turn, joint_t, first, tokens, grad_hidden, gain, packed):
    bf, f32 = jnp.bfloat16, jnp.float32
    S2 = n // PLANES // 2
    T, D = tokens.shape
    width = joint_t.shape[0]
    wide = width + 128
    rows = D // n
    part = packed.shape[4]
    piece_rows = T // n
    half = PLANES // 2
    any_, vm, sm = (pl.BlockSpec(memory_space=m) for m in (pl.ANY, pltpu.VMEM, pltpu.SMEM))
    sems = lambda count: pltpu.SemaphoreType.DMA((2, count))
    return pl.pallas_call(
        functools.partial(tail_kernel, n, groups),
        out_shape=(
            jax.ShapeDtypeStruct((T, D), bf),
            jax.ShapeDtypeStruct((groups, part, D), f32),
            jax.ShapeDtypeStruct((PLANES, rows, wide), f32),
        ),
        in_specs=[sm, vm, vm, vm, any_, any_, any_, any_, vm, any_],
        out_specs=(vm, vm, vm),
        scratch_shapes=[
            pltpu.VMEM((width, D), bf),
            pltpu.VMEM((PLANES, T, D), bf),
            pltpu.VMEM((T, D), bf),
            pltpu.VMEM((T, D), f32),
            pltpu.VMEM((PLANES, S2, groups, part, D), bf),
            pltpu.SemaphoreType.DMA((5,)),
            pltpu.VMEM((PLANES, S2, T, 2 * QW), bf),
            pltpu.VMEM((PLANES, S2, T, 2 * QW), bf),
            pltpu.VMEM((PLANES, S2 - 1, T, 2 * QW), bf),
            sems(PLANES * S2),
            pltpu.VMEM((PLANES, width, T), bf),
            pltpu.VMEM((PLANES, T, D), bf),
            pltpu.VMEM((PLANES - 1, T, D), bf),
            sems(PLANES - 1),
            pltpu.VMEM((width, D), f32),
            pltpu.VMEM((PLANES, S2, 2, rows, wide), bf),
            pltpu.VMEM((PLANES, S2, rows, wide), bf),
            pltpu.VMEM((S2 - 1, PLANES, rows, wide), bf),
            pltpu.VMEM((PLANES, rows, wide), bf),
            pltpu.VMEM((groups, PLANES, rows, wide), bf),
            sems(S2 + PLANES + groups - 2),
            pltpu.VMEM((PLANES, S2, groups, part, D), bf),
            pltpu.VMEM((groups - 1, half, S2, part, D), bf),
            pltpu.VMEM((S2 - 1, half, part, D), bf),
            pltpu.VMEM((S2 - 1, half, groups, part, D), bf),
            pltpu.VMEM((groups - 1, half, part, D), bf),
            pltpu.VMEM((PLANES, part, D), bf),
            pltpu.VMEM((PLANES - 1, part, D), bf),
            pltpu.VMEM((groups, part, D), bf),
            sems(2 + 3 * (groups - 1) + 2 * (S2 - 1) + PLANES - 1),
            pltpu.VMEM((n, piece_rows, D), bf),
            pltpu.VMEM((n, piece_rows, D), bf),
            pltpu.VMEM((n, piece_rows, D), bf),
            pltpu.VMEM((n, piece_rows, D), bf),
            sems(2 * n),
        ],
        compiler_params=pltpu.CompilerParams(collective_id=0, has_side_effects=True, vmem_limit_bytes=60 << 20),
    )(deal, dqt, dkv, turn, joint_t, first, tokens, grad_hidden, gain, packed)


def layer_norm(values, weights):
    centred = values - jnp.mean(values, axis=-1, keepdims=True)
    spread = jnp.mean(centred * centred, axis=-1, keepdims=True)
    return centred * lax.rsqrt(spread + norm_eps) * weights


def on_device(
    n,
    groups,
    tokens,
    cotangent,
    lengths,
    deal,
    joint_projection,
    output_projection,
    expand_weight,
    contract_weight,
    gain_first,
    gain_second,
):
    bf, f32 = jnp.bfloat16, jnp.float32
    T, D = tokens.shape[1:]
    S = n // PLANES
    S2 = S // 2
    me = lax.axis_index("ctx")
    plane = me // S

    def over_planes(x, k):
        return lax.ppermute(x, "ctx", [(h * S + s, (h + k) % PLANES * S + s) for h in range(PLANES) for s in range(S)])

    def turned(x, shift):
        return lax.dynamic_slice_in_dim(jnp.concatenate([x, x], axis=0), shift, x.shape[0], 0)

    tokens_own = tokens[0]
    first, qt, kv, joint_t, turn, gains, out_w, exp_w, con_w = front(
        n,
        groups,
        lengths,
        tokens_own,
        joint_projection,
        gain_first,
        gain_second,
        output_projection,
        expand_weight,
        contract_weight,
    )
    out_w, exp_w, con_w = (w.reshape(-1, w.shape[-1]) for w in (out_w, exp_w, con_w))
    gain_one, gain_two = gains[0], gains[1]
    ot, lowt, lse = attn_fwd(n, lengths, qt, kv)

    parts = [lowt[0]] + [over_planes(lowt[k], -k) for k in range(1, PLANES)]
    attended_t = turned(jnp.stack(parts), (PLANES - plane) % PLANES).reshape(D, T)

    x = tokens_own.astype(f32)
    grad_out = cotangent[0]
    hidden = x + jnp.einsum("dt,de->te", attended_t, out_w, preferred_element_type=f32)
    second = layer_norm(hidden, gain_two).astype(bf)
    expanded = jnp.dot(second, exp_w, preferred_element_type=f32)

    def gated(values):
        return jax.nn.gelu(values[:, :FF], approximate=False) * values[:, FF:]

    activated_f, gated_pull = jax.vjp(gated, expanded)
    activated = activated_f.astype(bf)
    output = (hidden + jnp.dot(activated, con_w, preferred_element_type=f32)).astype(bf)

    grad_activated = jnp.einsum("td,fd->tf", grad_out, con_w, preferred_element_type=f32)
    grad_expanded = gated_pull(grad_activated)[0].astype(bf)
    grad_second = jnp.einsum("tf,df->td", grad_expanded, exp_w, preferred_element_type=f32)
    _, second_pull = jax.vjp(layer_norm, hidden, gain_two)
    grad_hidden_norm, grad_gain_two = second_pull(grad_second)
    grad_hidden = grad_out.astype(f32) + grad_hidden_norm
    grad_branch = grad_hidden.astype(bf)
    grad_attended = jnp.einsum("de,te->dt", out_w, grad_branch, preferred_element_type=f32).astype(bf)
    rel = turned(grad_attended.reshape(PLANES, QW, T), plane)
    gt = jnp.stack([rel[0]] + [over_planes(rel[k], k) for k in range(1, PLANES)])

    grad_contract = jnp.einsum("tf,td->fd", activated, grad_out, preferred_element_type=f32)
    grad_expand = jnp.einsum("td,tf->df", second, grad_expanded, preferred_element_type=f32)
    grad_output = jnp.einsum("dt,te->de", attended_t, grad_branch, preferred_element_type=f32)

    dqt, dkv = attn_bwd(n, lengths, qt, kv, ot, lse, gt)

    def sharded(x):
        return x.astype(bf).reshape(n, x.shape[0] // n, x.shape[1])

    gain_rows = jnp.pad(grad_gain_two.reshape(n, 1, D // n), ((0, 0), (0, 7), (0, D - D // n))).astype(bf)
    rows = D // n
    wide = grad_expand.shape[1] // D
    pieces = [sharded(grad_output)]
    pieces += [sharded(grad_expand[:, i * D : (i + 1) * D]) for i in range(wide)]
    pieces += [sharded(grad_contract), gain_rows]
    used = sum(p.shape[1] for p in pieces)
    part = -(-used // (groups * 16)) * 16
    packed = jnp.concatenate(pieces + [jnp.zeros((n, groups * part - used, D), bf)], axis=1)
    packed = packed.reshape(PLANES, S2, 2, groups, part, D)

    dealt, shards, joint_raw = tail(
        n,
        groups,
        deal[0],
        dqt,
        dkv.reshape(PLANES, S2, 2, T, 2 * QW),
        turn,
        joint_t,
        first,
        tokens_own,
        grad_hidden,
        gains,
        packed,
    )
    shards = shards.reshape(groups * part, D)
    shard_output = shards[:rows]
    shard_expand = jnp.concatenate([shards[(1 + i) * rows : (2 + i) * rows] for i in range(wide)], axis=1)
    after = (1 + wide) * rows
    ff_rows = grad_contract.shape[0] // n
    shard_contract = shards[after : after + ff_rows]
    shard_gain_two = shards[after + ff_rows, :rows]
    shard_joint = jnp.transpose(joint_raw[:, :, : 3 * QW].reshape(PLANES, rows, 3, QW), (1, 2, 0, 3))
    shard_joint = shard_joint.reshape(rows, 3 * PLANES * QW)
    shard_gain_one = jnp.sum(joint_raw[:, :, -1], axis=0) / lax.dynamic_slice_in_dim(gain_one, me * rows, rows)
    return (
        output[None],
        dealt[None],
        shard_joint,
        shard_output,
        shard_expand,
        shard_contract,
        shard_gain_one,
        shard_gain_two,
    )


def solution(mesh):
    return jax.shard_map(
        functools.partial(on_device, mesh.shape["ctx"], mesh.shape["fsdp"]),
        mesh=mesh,
        in_specs=(
            P("fsdp", "ctx", None),
            P("fsdp", "ctx", None),
            P("fsdp", None),
            P("fsdp", None),
            P("fsdp", None),
            P("fsdp", None),
            P("fsdp", None),
            P("fsdp", None),
            P("fsdp"),
            P("fsdp"),
        ),
        out_specs=(
            P("fsdp", "ctx", None),
            P("fsdp", "ctx", None),
            P("ctx", None),
            P("ctx", None),
            P("ctx", None),
            P("ctx", None),
            P("ctx"),
            P("ctx"),
        ),
        check_vma=False,
    )
```

profile of v0, /device:TPU:0, one launch (start us, length us, event | category | flops | bytes accessed | tf_op | source)
XLA Modules:
  0.0 259.3 jit_solution(15629024417569329745)
XLA Ops:
  0.6 0.6 multiply_power_fusion.freq_ref
  1.3 1.2 broadcast_in_dim.26.gain_one_ref
  2.5 1.2 broadcast_in_dim.27.gain_two_ref
  3.7 56.7 %shard_map.161 = (bf16[4,256,768]{2,1,0:T(8,128)(2,1)}, bf16[4,192,256]{2,1,0:T(8,128)(2,1)}, bf16[16,256,384]{2,1,0:T(8,128)(2,1)}, bf16[640,768]{1,0:T(8,128)(...) custom-call(s32[1,3]{1,0:T(1,128)} %lengths_ref.5, ...), custom_call_target="tpu_custom_call" | custom-call | tf_op jit(solution)/shard_map/pallas_call | solution.py:546
  60.5 14.1 %shard_map.162 = (f32[4,192,256]{2,1,0:T(8,128)}, bf16[4,192,256]{2,1,0:T(8,128)(2,1)}, f32[4,8,256]{2,1,0:T(8,128)}) custom-call(s32[1,3]{1,0:T(1,128)} %lengths_ref.5, bf16[4,192,256]{2,1,0:T(8,128)(2,1)} %get-tuple-element.25.qt_ref, bf16[16,256,384]{2,1,0:T(8,128)(2,1)} %get-tuple-element.26.kv_ref), custom_call_target="tpu_custom_call" | custom-call | tf_op jit(solution)/shard_map/pallas_call | solution.py:147
  74.6 1.1 slice_bitcast_fusion.3
  75.7 1.5 collective-permute-start
  77.2 1.4 collective-permute-start.1
  78.6 0.6 collective-permute-start.2
  79.3 0.8 fusion.27
  80.3 7.6 %collective-permute-done.1 = bf16[192,256]{1,0:T(8,128)(2,1)S(1)} collective-permute-done((bf16[192,256]{1,0:T(8,128)(2,1)S(1)}, bf16[192,256]{1,0:T(8,128)(2,1)S(1)}, u32[]{:S(2)}, u32[]{:S(2)}) %collective-permute-start.1) | collective-permute-done | bytes 98336 | tf_op jit(solution)/shard_map/ppermute | solution.py:1028
  87.9 0.9 slice_dynamic-update-slice_fusion.1
  89.0 0.6 fusion.28
  89.8 1.2 copy-done.3
  90.9 1.1 fusion.21
  92.5 2.8 %fusion.12 = (f32[256,1152]{1,0:T(8,128)S(1)}, f32[256,1152]{1,0:T(8,128)S(1)}, f32[256,1152]{1,0:T(8,128)S(1)}) fusion(f32[256,2304]{1,0:T(8,128)S(1)} %fusion.21, bf16[1152,768]{1,0:T(8,128)(2,1)S(1)} %bitcast.90, bf16[1,256,768]{2,1,0:T(8,128)(2,1)S(1)} %copy-done.6), kind=kOutput, calls=%fused_computation.42 | convolution fusion | flops 472154112 | bytes 6881280 | tf_op jit(solution)/shard_map/td,fd->tf/dot_general | solution.py:1066
  95.3 0.6 multiply_add_fusion
  95.9 1.2 multiply_reduce_fusion
  97.2 0.3 fusion.22
  97.7 0.5 convolution_convert_fusion.3
  98.2 0.4 copy-done
  98.6 0.5 convolution_convert_fusion.2
  99.0 1.3 convolution_convert_fusion
  100.3 1.4 fusion.1
  101.7 0.7 convolution_convert_fusion.1
  102.6 0.6 collective-permute-start.5
  103.2 1.3 collective-permute-start.4
  104.4 1.9 collective-permute-start.3
  106.4 1.1 constant_dynamic-update-slice_fusion.4
  107.5 1.6 fusion.24
  109.2 2.5 constant_dynamic-update-slice_fusion.3
  111.7 1.2 constant_dynamic-update-slice_fusion.2
  112.9 1.1 constant_dynamic-update-slice_fusion.1
  114.0 1.4 constant_dynamic-update-slice_fusion
  115.4 0.7 pad_dynamic-update-slice_fusion
  116.1 0.8 broadcast_dynamic-update-slice_fusion
  116.9 1.7 pad_maximum_fusion.1.gt_ref
  118.6 21.1 %shard_map.163 = (f32[4,192,256]{2,1,0:T(8,128)}, bf16[16,256,384]{2,1,0:T(8,128)(2,1)}) custom-call(s32[1,3]{1,0:T(1,128)} %lengths_ref.5, bf16[4,192,256]{2,1,0:T(8,128)(2,1)} %get-tuple-element.25.qt_ref, bf16[16,256,384]{2,1,0:T(8,128)(2,1)} %get-tuple-element.26.kv_ref, f32[4,192,256]{2,1,0:T(8,128)} %get-tuple-element.32.ot_ref, ...), custom_call_target="tpu_custom_call" | custom-call | tf_op jit(solution)/shard_map/pallas_call | solution.py:230
  139.7 110.7 %shard_map.164 = (bf16[256,768]{1,0:T(8,128)(2,1)}, f32[2,144,768]{2,1,0:T(8,128)}, f32[4,48,768]{2,1,0:T(8,128)}) custom-call(s32[32]{0:T(128)} %bitcast.101, f32[4,192,256]{2,1,0:T(8,128)} %get-tuple-element.34.dq_ref, bf16[4,2,2,256,384]{4,3,2,1,0:T(8,128)(2,1)} %bitcast.87, f32[4,64,256]{2,1,0:T(8,128)} %get-tuple-element.36.turn_ref, ...), custom_call_target="tpu_custom_call" | custom-call | tf_op jit(solution)/shard_map/pallas_call | solution.py:950
  250.4 1.9 fusion.25
  252.3 1.6 slice.108
  254.1 1.2 slice_bitcast_fusion.6
  255.3 0.3 reshape.138
  255.7 0.4 copy.28
  256.1 1.1 reshape.139
  257.2 0.8 pad_maximum_fusion
  258.0 0.6 fusion.18
  258.6 0.7 copy.45
  (39 shorter events, 1.6 us)
Async XLA Ops:
  75.6 13.3 %copy-start.1 = (bf16[2,2,192,768]{3,2,1,0:T(8,128)(2,1)S(1)}, bf16[2,2,192,768]{3,2,1,0:T(8,128)(2,1)}, u32[]{:S(2)}) copy-start(bf16[2,2,192,768]{3,2,1,0:T(8,128)(2,1)} %get-tuple-element.28) | copy-start | bytes 3538948
  75.6 13.3 %copy-start.4 = (bf16[1,256,768]{2,1,0:T(8,128)(2,1)S(1)}, bf16[1,256,768]{2,1,0:T(8,128)(2,1)}, u32[]{:S(2)}) copy-start(bf16[1,256,768]{2,1,0:T(8,128)(2,1)} %param.10) | copy-start | bytes 1179652
  75.7 4.7 %collective-permute-start = (bf16[192,256]{1,0:T(8,128)(2,1)S(1)}, bf16[192,256]{1,0:T(8,128)(2,1)S(1)}, u32[]{:S(2)}, u32[]{:S(2)}) collective-permute-start(bf16[192,256]{1,0:T(8,128)(2,1)S(1)} %get-tuple-element.64), channel_id=1, source_target_pairs={{0,24},{2,26},{4,28},{6,30},{8,0},{10,2},{12,4},{14,6},{16,8},{18,... | collective-permute-start | bytes 294920 | tf_op jit(solution)/shard_map/ppermute | solution.py:1028
  77.2 10.7 %collective-permute-start.1 = (bf16[192,256]{1,0:T(8,128)(2,1)S(1)}, bf16[192,256]{1,0:T(8,128)(2,1)S(1)}, u32[]{:S(2)}, u32[]{:S(2)}) collective-permute-start(bf16[192,256]{1,0:T(8,128)(2,1)S(1)} %get-tuple-element.63), channel_id=1, source_target_pairs={{0,16},{2,18},{4,20},{6,22},{8,24},{10,26},{12,28},{14,30},{16,0},... | collective-permute-start | bytes 294920 | tf_op jit(solution)/shard_map/ppermute | solution.py:1028
  78.6 9.3 %collective-permute-start.2 = (bf16[192,256]{1,0:T(8,128)(2,1)S(1)}, bf16[192,256]{1,0:T(8,128)(2,1)S(1)}, u32[]{:S(2)}, u32[]{:S(2)}) collective-permute-start(bf16[192,256]{1,0:T(8,128)(2,1)S(1)} %get-tuple-element.61), channel_id=1, source_target_pairs={{0,8},{2,10},{4,12},{6,14},{8,16},{10,18},{12,20},{14,22},{16,24},... | collective-permute-start | bytes 294920 | tf_op jit(solution)/shard_map/ppermute | solution.py:1028
  88.9 2.0 copy-start.3
  90.9 1.5 copy-start.5
  90.9 1.5 copy-start.6
  97.7 0.9 copy-start
  102.6 14.3 %collective-permute-start.5 = (bf16[192,256]{1,0:T(8,128)(2,1)S(1)}, bf16[192,256]{1,0:T(8,128)(2,1)S(1)}, u32[]{:S(2)}, u32[]{:S(2)}) collective-permute-start(bf16[192,256]{1,0:T(8,128)(2,1)S(1)} %get-tuple-element.60), channel_id=1, source_target_pairs={{0,24},{2,26},{4,28},{6,30},{8,0},{10,2},{12,4},{14,6},{16,8},{18,... | collective-permute-start | bytes 294920 | tf_op jit(solution)/shard_map/ppermute | solution.py:1028
  103.2 13.7 %collective-permute-start.4 = (bf16[192,256]{1,0:T(8,128)(2,1)S(1)}, bf16[192,256]{1,0:T(8,128)(2,1)S(1)}, u32[]{:S(2)}, u32[]{:S(2)}) collective-permute-start(bf16[192,256]{1,0:T(8,128)(2,1)S(1)} %get-tuple-element.58), channel_id=1, source_target_pairs={{0,16},{2,18},{4,20},{6,22},{8,24},{10,26},{12,28},{14,30},{16,0},... | collective-permute-start | bytes 294920 | tf_op jit(solution)/shard_map/ppermute | solution.py:1028
  104.4 12.5 %collective-permute-start.3 = (bf16[192,256]{1,0:T(8,128)(2,1)S(1)}, bf16[192,256]{1,0:T(8,128)(2,1)}, u32[]{:S(2)}, u32[]{:S(2)}) collective-permute-start(bf16[192,256]{1,0:T(8,128)(2,1)S(1)} %get-tuple-element.59), channel_id=1, source_target_pairs={{0,8},{2,10},{4,12},{6,14},{8,16},{10,18},{12,20},{14,22},{16,24},... | collective-permute-start | bytes 294920 | tf_op jit(solution)/shard_map/ppermute | solution.py:1028
  109.2 2.5 copy-start.2
  250.4 3.5 %copy-start.7 = (f32[4,48,768]{2,1,0:T(8,128)S(1)}, f32[4,48,768]{2,1,0:T(8,128)}, u32[]{:S(2)}) copy-start(f32[4,48,768]{2,1,0:T(8,128)} %get-tuple-element.40) | copy-start | bytes 1769476
  256.1 2.5 copy-start.8
where the time goes:
time: 261 us; the launch traced here: 259 us
  Pallas kernels  203 us (78%)
  local copies, waits for them, and re-layouts  25.2 us (10%)
  matrix products  10.1 us (4%)
  waiting for transfers between devices  7.77 us (3%)
  starting transfers between devices  7.37 us (3%)
  other arithmetic  5.42 us (2%)
    pallas_call x1, Pallas kernels, tail(): pl.pallas_call(functools.partial(tail_kernel, n, groups), out_shape=(jax....  111 us
    pallas_call x1, Pallas kernels, front(): pl.pallas_call(functools.partial(front_kernel, n, groups, lengths.shape[1...  56.7 us
    pallas_call x1, Pallas kernels, attn_bwd(): pl.pallas_call(functools.partial(bwd_kernel, n, lengths.shape[1]), out_sh...  21.1 us
    pallas_call x1, Pallas kernels, attn_fwd(): pl.pallas_call(functools.partial(fwd_kernel, n, lengths.shape[1]), out_sh...  14.1 us
    unnamed x31, local copies, waits for them, and re-layouts  11.6 us
    ppermute x6, waiting for transfers between devices, over_planes(): lax.ppermute(x, 'ctx', [(h * S + s, (h + k) % PLANES * S + s) for h in ra...  7.77 us
    ppermute x6, starting transfers between devices, over_planes(): lax.ppermute(x, 'ctx', [(h * S + s, (h + k) % PLANES * S + s) for h in ra...  7.37 us
  transfers between devices with their start and end apart: 6, of which 2 were waited for; matrix products, arithmetic and copies ran while one was open for 4% of the time, Pallas kernels for 0%

commit v1 on v0

--- a/solution.py
+++ b/solution.py
@@ -1,4 +1,5 @@
 import functools
+import math
 
 import jax
 import jax.numpy as jnp
@@ -583,79 +584,59 @@
     )
 
 
-def tail_kernel(
+def middle_kernel(
     n,
     groups,
-    deal_ref,
-    dq_ref,
-    dkv_ref,
-    turn_ref,
-    joint_t_hbm,
-    first_hbm,
-    tokens_hbm,
-    grad_hidden_hbm,
+    low_ref,
+    tokens_ref,
+    cot_ref,
+    gains_ref,
+    out_hbm,
+    exp_hbm,
+    con_hbm,
+    output_ref,
+    grad_hidden_ref,
+    gt_ref,
     gain_ref,
-    packed_hbm,
-    dealt_ref,
-    shard_ref,
-    joint_out_ref,
-    joint_t,
-    first,
-    tokens,
-    grad_hidden,
+    y_keep,
+    y_send,
+    x_keep,
+    x_send,
+    z_keep,
+    z_send,
+    out_w,
+    exp_w,
+    con_w,
+    local_sems,
+    att,
+    a_sems,
+    g_send,
+    g_sems,
+    hidden,
+    second,
+    branch,
+    ga,
+    act,
+    gexp,
+    acc,
     w_own,
-    local_sems,
-    kv_near,
-    kv_send,
-    kv_far,
-    kv_sems,
-    mixed,
-    z_send,
-    z_got,
-    z_sems,
-    jg_t,
-    jg,
-    j_core,
-    j_side,
-    j_plane,
-    j_group,
-    j_sems,
-    w_core,
-    w_y1,
-    w_x1,
-    w_x2,
-    w_y2,
-    w_plane,
-    w_z,
-    w_all,
+    w_other,
+    w_got,
     w_sems,
-    d_send,
-    d_mid,
-    d_back,
-    d_got,
-    d_sems,
 ):
     bf, f32 = jnp.bfloat16, jnp.float32
     S = n // PLANES
     S2 = S // 2
-    T, D = tokens.shape
+    T, D = tokens_ref.shape
+    FFN = act.shape[1]
     me, group = lax.axis_index("ctx"), lax.axis_index("fsdp")
     plane, side = me // S, lax.rem(me, S)
     s2, core = side // 2, lax.rem(side, 2)
 
-    def at(p, a, c, g):
-        return (p * S + a * 2 + c, g)
-
     def plane_peer(k):
-        return at(lax.rem(plane + k, PLANES), s2, core, group)
-
-    def side_peer(k):
-        return at(plane, lax.rem(s2 + k, S2), core, group)
-
-    def group_peer(k):
-        return at(plane, s2, core, lax.rem(group + k, groups))
-
-    core_peer = at(plane, s2, 1 - core, group)
+        return (lax.rem(plane + k, PLANES) * S + side, group)
+
+    core_peer = (plane * S + s2 * 2 + 1 - core, group)
 
     def remote(source, target, sems, index, device):
         return pltpu.make_async_remote_copy(
@@ -667,31 +648,338 @@
             device_id_type=pl.DeviceIdType.MESH,
         )
 
+    local = [
+        pltpu.make_async_copy(source, target, local_sems.at[i])
+        for i, (source, target) in enumerate([(con_hbm, con_w), (out_hbm, out_w), (exp_hbm, exp_w)])
+    ]
+    for copy in local:
+        copy.start()
     barrier = pltpu.get_barrier_semaphore()
-
-    def greet(k, carry):
-        pl.semaphore_signal(
-            barrier, inc=1, device_id=(lax.rem(me + k, n), group), device_id_type=pl.DeviceIdType.MESH
+    for k in range(1, PLANES):
+        pl.semaphore_signal(barrier, inc=1, device_id=plane_peer(k), device_id_type=pl.DeviceIdType.MESH)
+    pl.semaphore_signal(barrier, inc=1, device_id=core_peer, device_id_type=pl.DeviceIdType.MESH)
+    pl.semaphore_wait(barrier, PLANES)
+
+    home = [remote(low_ref.at[j], att.at[plane], a_sems, j - 1, plane_peer(PLANES - j)) for j in range(1, PLANES)]
+    for copy in home:
+        copy.start()
+    att[plane] = low_ref[0]
+
+    def nt(a, b):
+        return lax.dot_general(a, b, (((1,), (1,)), ((), ())), preferred_element_type=f32)
+
+    chunk = 384
+    local[0].wait()
+    cot = cot_ref[...]
+    for c in range(0, FFN, chunk):
+        ga[:, c : c + chunk] = nt(cot, con_w[c : c + chunk])
+    local[1].wait()
+    for copy in home:
+        copy.wait()
+    attended = att[...].reshape(D, T)
+    hidden[...] = tokens_ref[...].astype(f32) + jnp.dot(attended.T, out_w[...], preferred_element_type=f32)
+
+    strip = 64
+
+    def norm(i, carry):
+        rows = pl.ds(pl.multiple_of(i * strip, strip), strip)
+        values = hidden[rows]
+        centred = values - jnp.mean(values, axis=-1, keepdims=True)
+        spread = jnp.mean(centred * centred, axis=-1, keepdims=True)
+        second[rows] = (centred * lax.rsqrt(spread + norm_eps) * gains_ref[1:2]).astype(bf)
+        return carry
+
+    lax.fori_loop(0, T // strip, norm, 0)
+    local[2].wait()
+    for c in range(0, FFN, chunk):
+        cols, gate_cols = slice(c, c + chunk), slice(FFN + c, FFN + c + chunk)
+        inner = jnp.dot(second[...], exp_w[:, cols], preferred_element_type=f32)
+        gate = jnp.dot(second[...], exp_w[:, gate_cols], preferred_element_type=f32)
+        share = 0.5 * (1.0 + lax.erf(inner * (0.5**0.5)))
+        bent = inner * share
+        act[:, cols] = (bent * gate).astype(bf)
+        grad = ga[:, cols]
+        slope = share + inner * jnp.exp(-0.5 * inner * inner) * ((2.0 * math.pi) ** -0.5)
+        gexp[:, cols] = (grad * gate * slope).astype(bf)
+        gexp[:, gate_cols] = (grad * bent).astype(bf)
+    output_ref[...] = (hidden[...] + jnp.dot(act[...], con_w[...], preferred_element_type=f32)).astype(bf)
+    acc[:T] = nt(gexp[...], exp_w[...])
+
+    def norm_back(i, total):
+        rows = pl.ds(pl.multiple_of(i * strip, strip), strip)
+        values = hidden[rows]
+        centred = values - jnp.mean(values, axis=-1, keepdims=True)
+        scale = lax.rsqrt(jnp.mean(centred * centred, axis=-1, keepdims=True) + norm_eps)
+        normal = centred * scale
+        grad = acc[rows]
+        total = total + jnp.sum(grad * normal, axis=0, keepdims=True)
+        grad = grad * gains_ref[1:2]
+        grad = grad - jnp.mean(grad, axis=-1, keepdims=True) - normal * jnp.mean(grad * normal, axis=-1, keepdims=True)
+        back = cot_ref[rows].astype(f32) + grad * scale
+        grad_hidden_ref[rows] = back
+        branch[rows] = back.astype(bf)
+        return total
+
+    total = lax.fori_loop(0, T // strip, norm_back, jnp.zeros((1, D), f32))
+    gain_ref[...] = jnp.broadcast_to(total, gain_ref.shape)
+    for p in range(PLANES):
+        g_send[p] = nt(out_w[p * QW : (p + 1) * QW], branch[...]).astype(bf)
+    away = [
+        remote(g_send.at[lax.rem(plane + k, PLANES)], gt_ref.at[k], g_sems, k - 1, plane_peer(k))
+        for k in range(1, PLANES)
+    ]
+    for copy in away:
+        copy.start()
+    gt_ref[0] = g_send[plane]
+
+    sent = []
+
+    def place(rows, offset, height):
+        for target, parity in ((w_other, 1 - core), (w_own, core)):
+
+            def body(m, carry):
+                if rows % 8:
+                    pair = acc[pl.ds(pl.multiple_of(2 * m * rows, 8), 2 * rows)]
+                    value = jnp.where(parity == 0, pair[:rows], pair[rows:])
+                else:
+                    value = acc[pl.ds(pl.multiple_of((2 * m + parity) * rows, 8), rows)]
+                if height > rows:
+                    value = jnp.concatenate([value, jnp.zeros((height - rows, D), f32)], axis=0)
+                value = value.astype(bf)
+                target[m, offset : offset + height] = value
+                return carry
+
+            lax.fori_loop(0, n // 2, body, 0)
+        part = pl.ds(offset, height)
+        sent.append(remote(w_other.at[:, part], w_got.at[:, part], w_sems, len(sent), core_peer))
+        sent[-1].start()
+
+    rows = D // n
+    acc[:D] = jnp.dot(attended, branch[...], preferred_element_type=f32)
+    place(rows, 0, rows)
+    second_t = second[...].T
+    wide = 2 * FFN // D
+    for i in range(wide):
+        acc[:D] = jnp.dot(second_t, gexp[:, i * D : (i + 1) * D], preferred_element_type=f32)
+        place(rows, (1 + i) * rows, rows)
+    for c in range(0, FFN, chunk):
+        acc[c : c + chunk] = jnp.dot(act[:, c : c + chunk].T, cot_ref[...], preferred_element_type=f32)
+    used = (1 + wide) * rows
+    place(FFN // n, used, w_own.shape[1] - used)
+
+    for copy in sent:
+        copy.wait()
+    height = y_keep.shape[2]
+    third = lambda g, i: pl.ds(pl.multiple_of((3 * g + i) * height, 16), height)
+
+    def summed(m, part):
+        return (w_own[m, part].astype(f32) + w_got[m, part].astype(f32)).astype(bf)
+
+    def each(count, body):
+        def step(i, carry):
+            body(i)
+            return carry
+
+        lax.fori_loop(0, count, step, 0)
+
+    for k in range(groups):
+        g = lax.rem(group + k, groups)
+
+        def first(m, k=k, g=g):
+            (y_send.at[k - 1] if k else y_keep)[m // S2, lax.rem(m, S2)] = summed(m, third(g, 0))
+
+        each(PLANES * S2, first)
+    for k in range(S2):
+        a = lax.rem(s2 + k, S2)
+
+        def second_part(i, k=k, a=a):
+            p, g = i // groups, lax.rem(i, groups)
+            (x_send.at[k - 1] if k else x_keep)[p, g] = summed(p * S2 + a, third(g, 1))
+
+        each(PLANES * groups, second_part)
+    for k in range(PLANES):
+        p = lax.rem(plane + k, PLANES)
+
+        def third_part(i, k=k, p=p):
+            a, g = i // groups, lax.rem(i, groups)
+            (z_send.at[k - 1] if k else z_keep)[a, g] = summed(p * S2 + a, third(g, 2))
+
+        each(S2 * groups, third_part)
+    for copy in away:
+        copy.wait()
+
+
+def middle(n, groups, lowt, tokens, cotangent, gains, out_w, exp_w, con_w):
+    bf, f32 = jnp.bfloat16, jnp.float32
+    S2 = n // PLANES // 2
+    T, D = tokens.shape
+    ffn = con_w.shape[0]
+    used = (D + 2 * ffn + ffn) // n
+    height = -(-used // (groups * 48)) * 16
+    any_, vm = pl.BlockSpec(memory_space=pl.ANY), pl.BlockSpec(memory_space=pltpu.VMEM)
+    sems = lambda count: pltpu.SemaphoreType.DMA((2, count))
+    shape = lambda *s: jax.ShapeDtypeStruct(s, bf)
+    half = (n // 2, 3 * groups * height, D)
+    return pl.pallas_call(
+        functools.partial(middle_kernel, n, groups),
+        out_shape=(
+            shape(T, D),
+            jax.ShapeDtypeStruct((T, D), f32),
+            shape(PLANES, QW, T),
+            jax.ShapeDtypeStruct((8, D), f32),
+            shape(PLANES, S2, height, D),
+            shape(groups - 1, PLANES, S2, height, D),
+            shape(PLANES, groups, height, D),
+            shape(S2 - 1, PLANES, groups, height, D),
+            shape(S2, groups, height, D),
+            shape(PLANES - 1, S2, groups, height, D),
+        ),
+        in_specs=[vm, vm, vm, vm, any_, any_, any_],
+        out_specs=tuple([vm] * 10),
+        scratch_shapes=[
+            pltpu.VMEM(out_w.shape, bf),
+            pltpu.VMEM(exp_w.shape, bf),
+            pltpu.VMEM(con_w.shape, bf),
+            pltpu.SemaphoreType.DMA((3,)),
+            pltpu.VMEM((PLANES, QW, T), bf),
+            sems(PLANES - 1),
+            pltpu.VMEM((PLANES, QW, T), bf),
+            sems(PLANES - 1),
+            pltpu.VMEM((T, D), f32),
+            pltpu.VMEM((T, D), bf),
+            pltpu.VMEM((T, D), bf),
+            pltpu.VMEM((T, ffn), f32),
+            pltpu.VMEM((T, ffn), bf),
+            pltpu.VMEM((T, 2 * ffn), bf),
+            pltpu.VMEM((ffn, D), f32),
+            pltpu.VMEM(half, bf),
+            pltpu.VMEM(half, bf),
+            pltpu.VMEM(half, bf),
+            sems(2 + 2 * ffn // D),
+        ],
+        compiler_params=pltpu.CompilerParams(collective_id=2, has_side_effects=True, vmem_limit_bytes=60 << 20),
+    )(lowt, tokens, cotangent, gains, out_w, exp_w, con_w)
+
+
+def tail_kernel(
+    n,
+    groups,
+    deal_ref,
+    dq_ref,
+    dkv_ref,
+    turn_ref,
+    gains_ref,
+    gain_two_ref,
+    joint_t_hbm,
+    first_hbm,
+    tokens_hbm,
+    grad_hidden_hbm,
+    y_keep_hbm,
+    y_got_hbm,
+    x_keep_hbm,
+    x_got_hbm,
+    z_keep_hbm,
+    z_got_hbm,
+    d_got,
+    w_all,
+    jq_all,
+    jk_all,
+    gain_all,
+    joint_t,
+    first,
+    tokens,
+    grad_hidden,
+    y_keep,
+    y_got,
+    x_keep,
+    x_got,
+    z_keep,
+    z_came,
+    local_sems,
+    kv_near,
+    kv_send,
+    kv_far,
+    kv_sems,
+    mixed_q,
+    mixed_kv,
+    part,
+    part_got,
+    part_send_sems,
+    part_recv_sems,
+    j_acc,
+    jq,
+    jq_core,
+    jq_side,
+    jq_plane,
+    jk,
+    jk_core,
+    jk_side,
+    jk_plane,
+    j_sems,
+    x1_got,
+    y2_got,
+    y3_got,
+    x3_got,
+    w_plane,
+    w_plane_got,
+    w_sems,
+    d_send,
+    d_mid,
+    d_back,
+    d_sems,
+    gain_part,
+    gain_got,
+    gain_sems,
+):
+    bf, f32 = jnp.bfloat16, jnp.float32
+    S = n // PLANES
+    S2 = S // 2
+    T, D = tokens.shape
+    me, group = lax.axis_index("ctx"), lax.axis_index("fsdp")
+    plane, side = me // S, lax.rem(me, S)
+    s2, core = side // 2, lax.rem(side, 2)
+    MESH = pl.DeviceIdType.MESH
+
+    def at(p, a, c, g):
+        return (p * S + a * 2 + c, g)
+
+    def plane_peer(k):
+        return at(lax.rem(plane + k, PLANES), s2, core, group)
+
+    def side_peer(k):
+        return at(plane, lax.rem(s2 + k, S2), core, group)
+
+    def group_peer(k):
+        return at(plane, s2, core, lax.rem(group + k, groups))
+
+    core_peer = at(plane, s2, 1 - core, group)
+
+    def send(source, target, send_sem, recv_sem, device):
+        return pltpu.make_async_remote_copy(
+            src_ref=source, dst_ref=target, send_sem=send_sem, recv_sem=recv_sem, device_id=device, device_id_type=MESH
         )
-        return carry
-
-    lax.fori_loop(1, n, greet, 0)
-    for k in range(1, groups):
-        pl.semaphore_signal(barrier, inc=1, device_id=group_peer(k), device_id_type=pl.DeviceIdType.MESH)
-    pl.semaphore_wait(barrier, n - 1 + groups - 1)
-
-    order = [*range(1, PLANES), 0]
-    planes = [lax.rem(plane + PLANES - j, PLANES) for j in range(PLANES)]
-    core_kv = [remote(dkv_ref.at[planes[j], :, 1 - core], kv_near.at[j], kv_sems, j, core_peer) for j in range(PLANES)]
-    for j in order:
-        core_kv[j].start()
+
+    def remote(source, target, sems, index, device):
+        return send(source, target, sems.at[0, index], sems.at[1, index], device)
+
+    def total_of(terms):
+        total = terms[0].astype(f32)
+        for term in terms[1:]:
+            total = total + term.astype(f32)
+        return total
+
     local = [
         pltpu.make_async_copy(source, target, local_sems.at[i])
         for i, (source, target) in enumerate(
             [
+                (first_hbm, first),
                 (joint_t_hbm, joint_t),
-                (first_hbm, first),
-                (packed_hbm.at[:, :, core], w_own),
+                (y_keep_hbm, y_keep),
+                (y_got_hbm, y_got),
+                (x_keep_hbm, x_keep),
+                (x_got_hbm, x_got),
+                (z_keep_hbm, z_keep),
+                (z_got_hbm, z_came),
                 (tokens_hbm, tokens),
                 (grad_hidden_hbm, grad_hidden),
             ]
@@ -699,112 +987,86 @@
     ]
     for copy in local:
         copy.start()
-    half = PLANES // 2
-    core_w = [
-        remote(
-            packed_hbm.at[pl.ds(i * half, half), :, 1 - core],
-            w_core.at[pl.ds(i * half, half)],
-            w_sems,
-            i,
-            core_peer,
-        )
-        for i in range(2)
+    barrier = pltpu.get_barrier_semaphore()
+
+    def greet(k, carry):
+        pl.semaphore_signal(barrier, inc=1, device_id=(lax.rem(me + k, n), group), device_id_type=MESH)
+        return carry
+
+    lax.fori_loop(1, n, greet, 0)
+    for k in range(1, groups):
+        pl.semaphore_signal(barrier, inc=1, device_id=group_peer(k), device_id_type=MESH)
+    pl.semaphore_wait(barrier, n - 1 + groups - 1)
+
+    lower = plane < 2
+    middle = (plane == 1) | (plane == 2)
+    order = [
+        jnp.where(lower, 3, 0),
+        jnp.where(plane == 0, 2, jnp.where(plane == 1, 0, jnp.where(plane == 2, 3, 1))),
+        jnp.where((plane == 0) | (plane == 2), 1, 2),
+        plane,
     ]
-    for copy in core_w:
+    steps = range(PLANES)
+    back = [lax.rem(plane + PLANES - p, PLANES) for p in order]
+    main = jnp.where(lower, 0, 1)
+    main_plane = plane + 1 - 2 * main
+
+    core_kv = [remote(dkv_ref.at[order[t], :, 1 - core], kv_near.at[t], kv_sems, t, core_peer) for t in steps]
+    for copy in core_kv:
         copy.start()
 
+    def turned_back(x, t):
+        cos, sin = turn_ref[back[t], :HALF], turn_ref[back[t], HALF:]
+        rows = []
+        for h in range(HP):
+            upper, lower = x[h * HD : h * HD + HALF], x[h * HD + HALF : (h + 1) * HD]
+            rows += [upper * cos + lower * sin, lower * cos - upper * sin]
+        return jnp.concatenate(rows, axis=0)
+
     side_kv = {}
-    for j in order:
-        core_kv[j].wait()
-        for k in range(S2):
-            total = dkv_ref[planes[j], k, core].astype(f32) + kv_near[j, k].astype(f32)
-            kv_send[j, k] = total.astype(bf)
+    for t in steps:
+        core_kv[t].wait()
+        for a in range(S2):
+            kv_send[t, a] = total_of([dkv_ref[order[t], a, core], kv_near[t, a]]).astype(bf)
         for k in range(1, S2):
-            side_kv[j, k] = remote(
-                kv_send.at[j, lax.rem(s2 + S2 - k, S2)],
-                kv_far.at[j, k - 1],
+            side_kv[t, k] = remote(
+                kv_send.at[t, lax.rem(s2 + S2 - k, S2)],
+                kv_far.at[t, k - 1],
                 kv_sems,
-                PLANES + j * (S2 - 1) + k - 1,
+                PLANES + t * (S2 - 1) + k - 1,
                 side_peer(S2 - k),
             )
-            side_kv[j, k].start()
+            side_kv[t, k].start()
+    for t in steps:
+        mixed_q[t] = turned_back(dq_ref[back[t]], t).astype(bf)
 
     w_moves = []
 
     def w_copy(source, target, device):
-        copy = remote(source, target, w_sems, 2 + len(w_moves), device)
+        copy = remote(source, target, w_sems, len(w_moves), device)
         w_moves.append(copy)
         copy.start()
         return copy
 
-    def add_core(i):
-        core_w[i].wait()
-        if i == 0:
-            local[2].wait()
-
-        def body(step, carry):
-            p, a, g = i * half + step // (S2 * groups), lax.rem(step // groups, S2), lax.rem(step, groups)
-            w_core[p, a, g] = (w_own[p, a, g].astype(f32) + w_core[p, a, g].astype(f32)).astype(bf)
-            return carry
-
-        lax.fori_loop(0, half * S2 * groups, body, 0)
-
-    plane_parts = {}
-    local[0].wait()
-    for j in order:
-        dk = kv_send[j, s2].astype(f32)
-        for k in range(1, S2):
-            side_kv[j, k].wait()
-            dk = dk + kv_far[j, k - 1].astype(f32)
-        dk = dk.T
-        cos, sin = turn_ref[j, :HALF], turn_ref[j, HALF:]
-        rows = []
-        for part in (dq_ref[j], dk[:QW]):
-            for h in range(HP):
-                upper, lower = part[h * HD : h * HD + HALF], part[h * HD + HALF : (h + 1) * HD]
-                rows += [upper * cos + lower * sin, lower * cos - upper * sin]
-        rows += [dk[QW:], jnp.zeros((mixed.shape[1] - 3 * QW, T), f32)]
-        turned = jnp.concatenate(rows, axis=0)
-        mixed[j] = turned.astype(bf)
-        part = jnp.dot(turned.T.astype(bf), joint_t[...], preferred_element_type=f32)
-        z_send[j] = part.astype(bf)
-        if j:
-            plane_parts[j] = remote(z_send.at[j], z_got.at[j - 1], z_sems, j - 1, plane_peer(PLANES - j))
-            plane_parts[j].start()
-        if j == order[0]:
-            add_core(0)
-            y1 = [
-                w_copy(w_core.at[pl.ds(0, half), :, lax.rem(group + k, groups)], w_y1.at[k - 1], group_peer(k))
-                for k in range(1, groups)
-            ]
-        elif j == order[1]:
-            add_core(1)
-            x2 = [
-                w_copy(w_core.at[pl.ds(half, half), lax.rem(s2 + k, S2)], w_x2.at[k - 1], side_peer(k))
-                for k in range(1, S2)
-            ]
-
-    local[1].wait()
-    jg_t[...] = jnp.dot(mixed[0], first[0], preferred_element_type=f32)
-    for j in range(1, PLANES):
-        jg_t[...] += jnp.dot(mixed[j], first[j], preferred_element_type=f32)
-    width = jg_t.shape[0]
-    shard_rows = jg.shape[3]
-    per = 128
-    for i in range(D // per):
-        block = jg_t[:, i * per : (i + 1) * per]
-        gain_part = jnp.sum(block * joint_t[:, i * per : (i + 1) * per].astype(f32), axis=0, keepdims=True)
-        whole = jnp.concatenate([block, jnp.broadcast_to(gain_part, (per, per))], axis=0).T.astype(bf)
-        j_rows = whole.astype(f32)
-        first_row = i * per
-        row = first_row
-        while row < first_row + per:
-            shard, offset = divmod(row, shard_rows)
-            count = min(shard_rows - offset, first_row + per - row)
-            jg[shard // S, shard % S // 2, shard % 2, offset : offset + count] = j_rows[
-                row - first_row : row - first_row + count
-            ].astype(bf)
-            row += count
+    local[4].wait()
+    local[5].wait()
+    for p in range(PLANES):
+        for g in range(groups):
+            x_keep[p, g] = total_of([x_keep[p, g]] + [x_got[k, p, g] for k in range(S2 - 1)]).astype(bf)
+    y2 = [w_copy(x_keep.at[:, lax.rem(group + k, groups)], y2_got.at[k - 1], group_peer(k)) for k in range(1, groups)]
+    local[2].wait()
+    local[3].wait()
+    for p in range(PLANES):
+        for a in range(S2):
+            y_keep[p, a] = total_of([y_keep[p, a]] + [y_got[k, p, a] for k in range(groups - 1)]).astype(bf)
+    x1 = [w_copy(y_keep.at[:, lax.rem(s2 + k, S2)], x1_got.at[k - 1], side_peer(k)) for k in range(1, S2)]
+    local[6].wait()
+    local[7].wait()
+    for a in range(S2):
+        for g in range(groups):
+            z_keep[a, g] = total_of([z_keep[a, g]] + [z_came[k, a, g] for k in range(PLANES - 1)]).astype(bf)
+    y3 = [w_copy(z_keep.at[:, lax.rem(group + k, groups)], y3_got.at[k - 1], group_peer(k)) for k in range(1, groups)]
+
     j_moves = []
 
     def j_copy(source, target, device):
@@ -813,54 +1075,164 @@
         copy.start()
         return copy
 
-    j_first = j_copy(jg.at[:, :, 1 - core], j_core, core_peer)
-
-    def sum_into(target, terms):
-        total = terms[0].astype(f32)
-        for term in terms[1:]:
-            total = total + term.astype(f32)
-        return total.astype(target)
-
-    for copy in y1:
+    def j_core_stage(mixed, grads, near):
+        height = mixed.shape[1]
+        j_acc[:height] = total_of(
+            [jnp.dot(mixed[t], first[back[t]], preferred_element_type=f32) for t in steps]
+        )
+        shard_rows = D // n
+        for i in range(D // 128):
+            block = j_acc[:height, i * 128 : (i + 1) * 128].T
+            row = i * 128
+            while row < (i + 1) * 128:
+                shard, offset = divmod(row, shard_rows)
+                count = min(shard_rows - offset, (i + 1) * 128 - row)
+                begin = row - i * 128
+                grads[shard // S, shard % S // 2, shard % 2, offset : offset + count] = block[
+                    begin : begin + count
+                ].astype(bf)
+                row += count
+        return [j_copy(grads.at[:, :, 1 - core], near, core_peer)]
+
+    def j_side_stage(moves, grads, near, far):
+        for copy in moves:
+            copy.wait()
+        for p in range(PLANES):
+            for a in range(S2):
+                near[p, a] = total_of([grads[p, a, core], near[p, a]]).astype(bf)
+        return [j_copy(near.at[:, lax.rem(s2 + k, S2)], far.at[k - 1], side_peer(k)) for k in range(1, S2)]
+
+    def j_plane_stage(moves, near, far, gathered):
+        for copy in moves:
+            copy.wait()
+        for p in range(PLANES):
+            far[0, p] = total_of([near[p, s2]] + [far[k, p] for k in range(S2 - 1)]).astype(bf)
+        gathered[plane] = far[0, plane]
+        return [
+            j_copy(far.at[0, lax.rem(plane + k, PLANES)], gathered.at[plane], plane_peer(k)) for k in range(1, PLANES)
+        ]
+
+    def j_group_stage(moves, gathered, every):
+        for copy in moves:
+            copy.wait()
+        every[group] = gathered[...]
+        return [j_copy(gathered, every.at[group], group_peer(k)) for k in range(1, groups)]
+
+    local[0].wait()
+    jq_moves = j_core_stage(mixed_q, jq, jq_core)
+
+    local[1].wait()
+
+    def main_send(t):
+        return send(
+            part.at[t],
+            part_got.at[main, order[t]],
+            part_send_sems.at[t],
+            part_recv_sems.at[main * PLANES + order[t]],
+            at(main_plane, s2, core, group),
+        )
+
+    def other_send(t):
+        return send(
+            part.at[t],
+            part_got.at[1 - main, order[t]],
+            part_send_sems.at[t],
+            part_recv_sems.at[(1 - main) * PLANES + order[t]],
+            at(2 * plane - main_plane, s2, core, group),
+        )
+
+    def came(direction, p):
+        return send(
+            part.at[0],
+            part_got.at[direction, p],
+            part_send_sems.at[0],
+            part_recv_sems.at[direction * PLANES + p],
+            core_peer,
+        )
+
+    strip = 64
+
+    def add_part(t, direction, p):
+        def body(i, carry):
+            rows = pl.ds(pl.multiple_of(i * strip, strip), strip)
+            part[t, rows] = total_of([part[t, rows], part_got[direction, p, rows]]).astype(bf)
+            return carry
+
+        lax.fori_loop(0, T // strip, body, 0)
+
+    def relay(t, secondary):
+        @pl.when(middle)
+        def _():
+            direction = 1 - main if secondary else main
+            came(direction, order[t]).wait_recv()
+            add_part(t, direction, order[t])
+            (other_send if secondary else main_send)(t).start()
+
+    def key_step(t):
+        for k in range(1, S2):
+            side_kv[t, k].wait()
+        dk = total_of([kv_send[t, s2]] + [kv_far[t, k] for k in range(S2 - 1)]).T
+        mixed_kv[t, :QW] = turned_back(dk[:QW], t).astype(bf)
+        mixed_kv[t, QW:] = dk[QW:].astype(bf)
+        grads = jnp.concatenate([mixed_q[t], mixed_kv[t]], axis=0)
+        part[t] = jnp.dot(grads.T, joint_t[: 3 * QW], preferred_element_type=f32).astype(bf)
+        if t < PLANES - 1:
+
+            @pl.when(jnp.logical_not(middle))
+            def _():
+                main_send(t).start()
+
+    key_step(0)
+    jq_moves = j_side_stage(jq_moves, jq, jq_core, jq_side)
+    key_step(1)
+    key_step(2)
+    relay(0, False)
+    jq_moves = j_plane_stage(jq_moves, jq_core, jq_side, jq_plane)
+    key_step(3)
+    relay(2, False)
+    jk_moves = j_core_stage(mixed_kv, jk, jk_core)
+
+    for copy in y3:
         copy.wait()
-    for p in range(half):
-        for a in range(S2):
-            w_y1[0, p, a] = sum_into(bf, [w_core[p, a, group]] + [w_y1[k, p, a] for k in range(groups - 1)])
-    x1 = [w_copy(w_y1.at[0, :, lax.rem(s2 + k, S2)], w_x1.at[k - 1], side_peer(k)) for k in range(1, S2)]
-    for copy in x2:
+    for a in range(S2):
+        z_keep[a, group] = total_of([z_keep[a, group]] + [y3_got[k, a] for k in range(groups - 1)]).astype(bf)
+    x3 = [w_copy(z_keep.at[lax.rem(s2 + k, S2), group], x3_got.at[k - 1], side_peer(k)) for k in range(1, S2)]
+    relay(1, True)
+    for copy in y2 + x1:
         copy.wait()
-    for p in range(half):
-        for g in range(groups):
-            w_x2[0, p, g] = sum_into(bf, [w_core[half + p, s2, g]] + [w_x2[k, p, g] for k in range(S2 - 1)])
-    y2 = [w_copy(w_x2.at[0, :, lax.rem(group + k, groups)], w_y2.at[k - 1], group_peer(k)) for k in range(1, groups)]
-
-    j_first.wait()
     for p in range(PLANES):
-        for a in range(S2):
-            j_core[p, a] = sum_into(bf, [jg[p, a, core], j_core[p, a]])
-    j_second = [j_copy(j_core.at[:, lax.rem(s2 + k, S2)], j_side.at[k - 1], side_peer(k)) for k in range(1, S2)]
-
-    local[3].wait()
-    local[4].wait()
-    for j in range(1, PLANES):
-        plane_parts[j].wait()
-    strip = 64
-
-    def norm_back(i, carry):
+        w_plane[p, 0] = total_of([y_keep[p, s2]] + [x1_got[k, p] for k in range(S2 - 1)]).astype(bf)
+        w_plane[p, 1] = total_of([x_keep[p, group]] + [y2_got[k, p] for k in range(groups - 1)]).astype(bf)
+    jk_moves = j_side_stage(jk_moves, jk, jk_core, jk_side)
+    w_last = [
+        w_copy(w_plane.at[lax.rem(plane + k, PLANES)], w_plane_got.at[k - 1], plane_peer(k)) for k in range(1, PLANES)
+    ]
+    jq_moves = j_group_stage(jq_moves, jq_plane, jq_all)
+
+    local[8].wait()
+    local[9].wait()
+    came(1 - main, plane).wait_recv()
+    add_part(PLANES - 1, 1 - main, plane)
+
+    @pl.when(middle)
+    def _():
+        came(main, plane).wait_recv()
+        add_part(PLANES - 1, main, plane)
+
+    def norm_back(i, total):
         rows = pl.ds(pl.multiple_of(i * strip, strip), strip)
-        grad = z_send[0, rows].astype(f32)
-        for j in range(1, PLANES):
-            grad = grad + z_got[j - 1, rows].astype(f32)
+        grad = part[PLANES - 1, rows].astype(f32)
         values = tokens[rows].astype(f32)
         centred = values - jnp.mean(values, axis=-1, keepdims=True)
         scale = lax.rsqrt(jnp.mean(centred * centred, axis=-1, keepdims=True) + norm_eps)
         normal = centred * scale
-        grad = grad * gain_ref[0:1]
+        total = total + jnp.sum(grad * normal, axis=0, keepdims=True)
+        grad = grad * gains_ref[0:1]
         grad = grad - jnp.mean(grad, axis=-1, keepdims=True) - normal * jnp.mean(grad * normal, axis=-1, keepdims=True)
         grad_hidden[rows] = grad_hidden[rows] + grad * scale
-        return carry
-
-    lax.fori_loop(0, T // strip, norm_back, 0)
+        return total
+
+    gain_one = lax.fori_loop(0, T // strip, norm_back, jnp.zeros((1, D), f32))
 
     blocks = T // BLOCK
     piece = BLOCK // n
@@ -877,18 +1249,18 @@
         copy.start()
     d_mid[me] = d_send[me]
 
-    for copy in x1 + y2:
-        copy.wait()
-    for p in range(half):
-        w_plane[p] = sum_into(bf, [w_y1[0, p, s2]] + [w_x1[k, p] for k in range(S2 - 1)])
-        w_plane[half + p] = sum_into(bf, [w_x2[0, p, group]] + [w_y2[k, p] for k in range(groups - 1)])
-    w_last = [w_copy(w_plane.at[lax.rem(plane + k, PLANES)], w_z.at[k - 1], plane_peer(k)) for k in range(1, PLANES)]
-    for copy in j_second:
-        copy.wait()
-    for p in range(PLANES):
-        j_side[0, p] = sum_into(bf, [j_core[p, s2]] + [j_side[k, p] for k in range(S2 - 1)])
-    j_third = [j_copy(j_side.at[0, lax.rem(plane + k, PLANES)], j_plane.at[plane], plane_peer(k)) for k in range(1, PLANES)]
-    j_plane[plane] = j_side[0, plane]
+    per = D // 128
+    gain_part[...] = jnp.zeros_like(gain_part)
+    for i in range(per):
+        gain_part[i : i + 1] = gain_one[:, i * 128 : (i + 1) * 128]
+        gain_part[per + i : per + i + 1] = gain_two_ref[0:1, i * 128 : (i + 1) * 128]
+    gain_moves = [
+        remote(gain_part, gain_got.at[me], gain_sems, k - 1, (lax.rem(me + k, n), group)) for k in range(1, n)
+    ]
+    for copy in gain_moves:
+        copy.start()
+    gain_got[me] = gain_part[...]
+    jk_moves = j_plane_stage(jk_moves, jk_core, jk_side, jk_plane)
 
     for copy in out_deal:
         copy.wait()
@@ -897,110 +1269,170 @@
         for b in range(blocks):
             wanted = deal_ref[i * blocks + b]
             held = d_mid[wanted // blocks].astype(f32)
-            part = held[:piece]
+            rows = held[:piece]
             for other in range(1, blocks):
-                part = jnp.where(lax.rem(wanted, blocks) == other, held[other * piece : (other + 1) * piece], part)
-            chosen.append(part)
+                rows = jnp.where(lax.rem(wanted, blocks) == other, held[other * piece : (other + 1) * piece], rows)
+            chosen.append(rows)
         d_back[i] = jnp.concatenate(chosen, axis=0).astype(bf)
     back_deal = [d_copy(d_back, d_got, n, k) for k in range(1, n)]
     for copy in back_deal:
         copy.start()
     d_got[me] = d_back[me]
 
-    for copy in w_last:
+    for copy in gain_moves:
         copy.wait()
-    w_all[group] = sum_into(bf, [w_plane[plane]] + [w_z[k] for k in range(PLANES - 1)])
+    gain_part[...] = total_of([gain_got[i] for i in range(n)])
+    gain_all[group] = gain_part[...]
+    gain_last = [
+        remote(gain_part, gain_all.at[group], gain_sems, n - 1 + k - 1, group_peer(k)) for k in range(1, groups)
+    ]
+    for copy in gain_last:
+        copy.start()
+    for copy in w_last + x3:
+        copy.wait()
+    height = w_plane.shape[2]
+    for i in range(2):
+        w_all[group, i * height : (i + 1) * height] = total_of(
+            [w_plane[plane, i]] + [w_plane_got[k, i] for k in range(PLANES - 1)]
+        ).astype(bf)
+    w_all[group, 2 * height :] = total_of([z_keep[s2, group]] + [x3_got[k] for k in range(S2 - 1)]).astype(bf)
     w_gather = [w_copy(w_all.at[group], w_all.at[group], group_peer(k)) for k in range(1, groups)]
-    for copy in j_third:
+    jk_moves = j_group_stage(jk_moves, jk_plane, jk_all)
+
+    for copy in back_deal + gain_last + w_gather + jq_moves + jk_moves:
         copy.wait()
-    j_group[group] = j_plane[...]
-    j_last = [j_copy(j_plane, j_group.at[group], group_peer(k)) for k in range(1, groups)]
-
-    for copy in back_deal:
-        copy.wait()
-    for b in range(blocks):
-        for i in range(0, n, 2):
-            rows = [d_got[i + e].astype(f32)[b * piece : (b + 1) * piece] for e in range(2)]
-            dealt_ref[b * BLOCK + i * piece : b * BLOCK + (i + 2) * piece] = jnp.concatenate(rows, axis=0).astype(bf)
-    for copy in w_gather:
-        copy.wait()
-    for g in range(groups):
-        shard_ref[g] = w_all[g].astype(f32)
-    for copy in j_last:
-        copy.wait()
-    for p in range(PLANES):
-        total = j_group[0, p].astype(f32)
-        for g in range(1, groups):
-            total = total + j_group[g, p].astype(f32)
-        joint_out_ref[p] = total
-
-
-def tail(n, groups, deal, dqt, dkv, turn, joint_t, first, tokens, grad_hidden, gain, packed):
+    for t in range(PLANES - 1):
+        came_from = send(part.at[t], part.at[t], part_send_sems.at[t], part_recv_sems.at[0], core_peer)
+        came_from.wait_send()
+
+
+def tail(n, groups, deal, dqt, dkv, turn, gains, gain_two, joint_t, first, tokens, grad_hidden, pieces):
     bf, f32 = jnp.bfloat16, jnp.float32
     S2 = n // PLANES // 2
     T, D = tokens.shape
-    width = joint_t.shape[0]
-    wide = width + 128
     rows = D // n
-    part = packed.shape[4]
+    height = pieces[0].shape[2]
     piece_rows = T // n
-    half = PLANES // 2
+    gain_rows = -(-2 * D // 128 // 8) * 8
     any_, vm, sm = (pl.BlockSpec(memory_space=m) for m in (pl.ANY, pltpu.VMEM, pltpu.SMEM))
     sems = lambda count: pltpu.SemaphoreType.DMA((2, count))
+    small = lambda *s: pltpu.VMEM(s, bf)
+    j_buffers = lambda w: [
+        small(PLANES, S2, 2, rows, w),
+        small(PLANES, S2, rows, w),
+        small(S2 - 1, PLANES, rows, w),
+        small(PLANES, rows, w),
+    ]
     return pl.pallas_call(
         functools.partial(tail_kernel, n, groups),
         out_shape=(
-            jax.ShapeDtypeStruct((T, D), bf),
-            jax.ShapeDtypeStruct((groups, part, D), f32),
-            jax.ShapeDtypeStruct((PLANES, rows, wide), f32),
+            jax.ShapeDtypeStruct((n, piece_rows, D), bf),
+            jax.ShapeDtypeStruct((groups, 3 * height, D), bf),
+            jax.ShapeDtypeStruct((groups, PLANES, rows, QW), bf),
+            jax.ShapeDtypeStruct((groups, PLANES, rows, 2 * QW), bf),
+            jax.ShapeDtypeStruct((groups, gain_rows, 128), f32),
         ),
-        in_specs=[sm, vm, vm, vm, any_, any_, any_, any_, vm, any_],
-        out_specs=(vm, vm, vm),
+        in_specs=[sm, vm, vm, vm, vm, vm] + [any_] * 10,
+        out_specs=tuple([vm] * 5),
         scratch_shapes=[
-            pltpu.VMEM((width, D), bf),
+            pltpu.VMEM(joint_t.shape, bf),
             pltpu.VMEM((PLANES, T, D), bf),
             pltpu.VMEM((T, D), bf),
             pltpu.VMEM((T, D), f32),
-            pltpu.VMEM((PLANES, S2, groups, part, D), bf),
-            pltpu.SemaphoreType.DMA((5,)),
-            pltpu.VMEM((PLANES, S2, T, 2 * QW), bf),
-            pltpu.VMEM((PLANES, S2, T, 2 * QW), bf),
-            pltpu.VMEM((PLANES, S2 - 1, T, 2 * QW), bf),
+            *[pltpu.VMEM(p.shape, bf) for p in pieces],
+            pltpu.SemaphoreType.DMA((10,)),
+            small(PLANES, S2, T, 2 * QW),
+            small(PLANES, S2, T, 2 * QW),
+            small(PLANES, S2 - 1, T, 2 * QW),
             sems(PLANES * S2),
-            pltpu.VMEM((PLANES, width, T), bf),
-            pltpu.VMEM((PLANES, T, D), bf),
-            pltpu.VMEM((PLANES - 1, T, D), bf),
-            sems(PLANES - 1),
-            pltpu.VMEM((width, D), f32),
-            pltpu.VMEM((PLANES, S2, 2, rows, wide), bf),
-            pltpu.VMEM((PLANES, S2, rows, wide), bf),
-            pltpu.VMEM((S2 - 1, PLANES, rows, wide), bf),
-            pltpu.VMEM((PLANES, rows, wide), bf),
-            pltpu.VMEM((groups, PLANES, rows, wide), bf),
-            sems(S2 + PLANES + groups - 2),
-            pltpu.VMEM((PLANES, S2, groups, part, D), bf),
-            pltpu.VMEM((groups - 1, half, S2, part, D), bf),
-            pltpu.VMEM((S2 - 1, half, part, D), bf),
-            pltpu.VMEM((S2 - 1, half, groups, part, D), bf),
-            pltpu.VMEM((groups - 1, half, part, D), bf),
-            pltpu.VMEM((PLANES, part, D), bf),
-            pltpu.VMEM((PLANES - 1, part, D), bf),
-            pltpu.VMEM((groups, part, D), bf),
-            sems(2 + 3 * (groups - 1) + 2 * (S2 - 1) + PLANES - 1),
-            pltpu.VMEM((n, piece_rows, D), bf),
-            pltpu.VMEM((n, piece_rows, D), bf),
-            pltpu.VMEM((n, piece_rows, D), bf),
-            pltpu.VMEM((n, piece_rows, D), bf),
+            small(PLANES, QW, T),
+            small(PLANES, 2 * QW, T),
+            small(PLANES, T, D),
+            small(2, PLANES, T, D),
+            pltpu.SemaphoreType.DMA((PLANES - 1,)),
+            pltpu.SemaphoreType.DMA((2 * PLANES,)),
+            pltpu.VMEM((2 * QW, D), f32),
+            *j_buffers(QW),
+            *j_buffers(2 * QW),
+            sems(2 * (1 + S2 - 1 + PLANES - 1 + groups - 1)),
+            small(S2 - 1, PLANES, height, D),
+            small(groups - 1, PLANES, height, D),
+            small(groups - 1, S2, height, D),
+            small(S2 - 1, height, D),
+            small(PLANES, 2, height, D),
+            small(PLANES - 1, 2, height, D),
+            sems(3 * (groups - 1) + 2 * (S2 - 1) + PLANES - 1),
+            small(n, piece_rows, D),
+            small(n, piece_rows, D),
+            small(n, piece_rows, D),
             sems(2 * n),
+            pltpu.VMEM((gain_rows, 128), f32),
+            pltpu.VMEM((n, gain_rows, 128), f32),
+            sems(n - 1 + groups - 1),
         ],
         compiler_params=pltpu.CompilerParams(collective_id=0, has_side_effects=True, vmem_limit_bytes=60 << 20),
-    )(deal, dqt, dkv, turn, joint_t, first, tokens, grad_hidden, gain, packed)
-
-
-def layer_norm(values, weights):
-    centred = values - jnp.mean(values, axis=-1, keepdims=True)
-    spread = jnp.mean(centred * centred, axis=-1, keepdims=True)
-    return centred * lax.rsqrt(spread + norm_eps) * weights
+    )(deal, dqt, dkv, turn, gains, gain_two, joint_t, first, tokens, grad_hidden, *pieces)
+
+
+def finish_kernel(n, d_ref, w_ref, jq_ref, jk_ref, dealt_ref, joint_ref, output_ref, expand_ref, contract_ref):
+    f32 = jnp.float32
+    T, D = dealt_ref.shape
+    blocks = T // BLOCK
+    piece = BLOCK // n
+    for b in range(blocks):
+        for i in range(0, n, 2):
+            rows = [d_ref[i + e].astype(f32)[b * piece : (b + 1) * piece] for e in range(2)]
+            dealt_ref[b * BLOCK + i * piece : b * BLOCK + (i + 2) * piece] = jnp.concatenate(rows, axis=0).astype(
+                dealt_ref.dtype
+            )
+
+    def summed(ref, p):
+        total = ref[0, p].astype(f32)
+        for g in range(1, ref.shape[0]):
+            total = total + ref[g, p].astype(f32)
+        return total.T
+
+    for i in range(PLANES // 2):
+        pair = [summed(jq_ref, 2 * i + e) for e in range(2)]
+        joint_ref[:, i * 2 * QW : (i + 1) * 2 * QW] = jnp.concatenate(pair, axis=0).T
+        pair = [summed(jk_ref, 2 * i + e) for e in range(2)]
+        for part in range(2):
+            cols = (part + 1) * D + i * 2 * QW
+            rows = [x[part * QW : (part + 1) * QW] for x in pair]
+            joint_ref[:, cols : cols + 2 * QW] = jnp.concatenate(rows, axis=0).T
+    height = w_ref.shape[1]
+    rows = D // n
+    targets = [(output_ref, 0, rows)]
+    targets += [(expand_ref, i * D, rows) for i in range(expand_ref.shape[1] // D)]
+    targets += [(contract_ref, 0, contract_ref.shape[0])]
+    row = 0
+    for target, column, count in targets:
+        done = 0
+        while done < count:
+            g, offset = divmod(row, height)
+            part = min(count - done, height - offset)
+            target[done : done + part, column : column + D] = w_ref[g, offset : offset + part].astype(f32)
+            done += part
+            row += part
+
+
+def finish(n, T, wide, contract_rows, d_got, w_all, jq_all, jk_all):
+    D = d_got.shape[-1]
+    rows = D // n
+    f32 = jnp.float32
+    vm = pl.BlockSpec(memory_space=pltpu.VMEM)
+    return pl.pallas_call(
+        functools.partial(finish_kernel, n),
+        out_shape=(
+            jax.ShapeDtypeStruct((T, D), jnp.bfloat16),
+            jax.ShapeDtypeStruct((rows, 3 * D), f32),
+            jax.ShapeDtypeStruct((rows, D), f32),
+            jax.ShapeDtypeStruct((rows, wide), f32),
+            jax.ShapeDtypeStruct((contract_rows, D), f32),
+        ),
+        in_specs=[vm] * 4,
+        out_specs=tuple([vm] * 5),
+    )(d_got, w_all, jq_all, jk_all)
 
 
 def on_device(
@@ -1017,25 +1449,33 @@
     gain_first,
     gain_second,
 ):
-    bf, f32 = jnp.bfloat16, jnp.float32
     T, D = tokens.shape[1:]
     S = n // PLANES
     S2 = S // 2
     me = lax.axis_index("ctx")
-    plane = me // S
 
     def over_planes(x, k):
         return lax.ppermute(x, "ctx", [(h * S + s, (h + k) % PLANES * S + s) for h in range(PLANES) for s in range(S)])
 
-    def turned(x, shift):
-        return lax.dynamic_slice_in_dim(jnp.concatenate([x, x], axis=0), shift, x.shape[0], 0)
-
-    tokens_own = tokens[0]
+    def over_sides(x, k):
+        pairs = [
+            (h * S + a * 2 + c, h * S + (a + k) % S2 * 2 + c) for h in range(PLANES) for a in range(S2) for c in range(2)
+        ]
+        return lax.ppermute(x, "ctx", pairs)
+
+    def over_groups(x, k):
+        return lax.ppermute(x, "fsdp", [(f, (f + k) % groups) for f in range(groups)])
+
+    def moved(x, over):
+        if x.shape[0] == 1:
+            return over(x, 1)
+        return jnp.stack([over(x[k], k + 1) for k in range(x.shape[0])])
+
     first, qt, kv, joint_t, turn, gains, out_w, exp_w, con_w = front(
         n,
         groups,
         lengths,
-        tokens_own,
+        tokens[0],
         joint_projection,
         gain_first,
         gain_second,
@@ -1044,80 +1484,33 @@
         contract_weight,
     )
     out_w, exp_w, con_w = (w.reshape(-1, w.shape[-1]) for w in (out_w, exp_w, con_w))
-    gain_one, gain_two = gains[0], gains[1]
     ot, lowt, lse = attn_fwd(n, lengths, qt, kv)
-
-    parts = [lowt[0]] + [over_planes(lowt[k], -k) for k in range(1, PLANES)]
-    attended_t = turned(jnp.stack(parts), (PLANES - plane) % PLANES).reshape(D, T)
-
-    x = tokens_own.astype(f32)
-    grad_out = cotangent[0]
-    hidden = x + jnp.einsum("dt,de->te", attended_t, out_w, preferred_element_type=f32)
-    second = layer_norm(hidden, gain_two).astype(bf)
-    expanded = jnp.dot(second, exp_w, preferred_element_type=f32)
-
-    def gated(values):
-        return jax.nn.gelu(values[:, :FF], approximate=False) * values[:, FF:]
-
-    activated_f, gated_pull = jax.vjp(gated, expanded)
-    activated = activated_f.astype(bf)
-    output = (hidden + jnp.dot(activated, con_w, preferred_element_type=f32)).astype(bf)
-
-    grad_activated = jnp.einsum("td,fd->tf", grad_out, con_w, preferred_element_type=f32)
-    grad_expanded = gated_pull(grad_activated)[0].astype(bf)
-    grad_second = jnp.einsum("tf,df->td", grad_expanded, exp_w, preferred_element_type=f32)
-    _, second_pull = jax.vjp(layer_norm, hidden, gain_two)
-    grad_hidden_norm, grad_gain_two = second_pull(grad_second)
-    grad_hidden = grad_out.astype(f32) + grad_hidden_norm
-    grad_branch = grad_hidden.astype(bf)
-    grad_attended = jnp.einsum("de,te->dt", out_w, grad_branch, preferred_element_type=f32).astype(bf)
-    rel = turned(grad_attended.reshape(PLANES, QW, T), plane)
-    gt = jnp.stack([rel[0]] + [over_planes(rel[k], k) for k in range(1, PLANES)])
-
-    grad_contract = jnp.einsum("tf,td->fd", activated, grad_out, preferred_element_type=f32)
-    grad_expand = jnp.einsum("td,tf->df", second, grad_expanded, preferred_element_type=f32)
-    grad_output = jnp.einsum("dt,te->de", attended_t, grad_branch, preferred_element_type=f32)
-
+    output, grad_hidden, gt, gain_two, y_keep, y_send, x_keep, x_send, z_keep, z_send = middle(
+        n, groups, lowt, tokens[0], cotangent[0], gains, out_w, exp_w, con_w
+    )
+    y_got, x_got, z_got = moved(y_send, over_groups), moved(x_send, over_sides), moved(z_send, over_planes)
     dqt, dkv = attn_bwd(n, lengths, qt, kv, ot, lse, gt)
-
-    def sharded(x):
-        return x.astype(bf).reshape(n, x.shape[0] // n, x.shape[1])
-
-    gain_rows = jnp.pad(grad_gain_two.reshape(n, 1, D // n), ((0, 0), (0, 7), (0, D - D // n))).astype(bf)
-    rows = D // n
-    wide = grad_expand.shape[1] // D
-    pieces = [sharded(grad_output)]
-    pieces += [sharded(grad_expand[:, i * D : (i + 1) * D]) for i in range(wide)]
-    pieces += [sharded(grad_contract), gain_rows]
-    used = sum(p.shape[1] for p in pieces)
-    part = -(-used // (groups * 16)) * 16
-    packed = jnp.concatenate(pieces + [jnp.zeros((n, groups * part - used, D), bf)], axis=1)
-    packed = packed.reshape(PLANES, S2, 2, groups, part, D)
-
-    dealt, shards, joint_raw = tail(
+    d_got, w_all, jq_all, jk_all, gain_all = tail(
         n,
         groups,
         deal[0],
         dqt,
         dkv.reshape(PLANES, S2, 2, T, 2 * QW),
         turn,
+        gains,
+        gain_two,
         joint_t,
         first,
-        tokens_own,
+        tokens[0],
         grad_hidden,
-        gains,
-        packed,
+        [y_keep, y_got, x_keep, x_got, z_keep, z_got],
     )
-    shards = shards.reshape(groups * part, D)
-    shard_output = shards[:rows]
-    shard_expand = jnp.concatenate([shards[(1 + i) * rows : (2 + i) * rows] for i in range(wide)], axis=1)
-    after = (1 + wide) * rows
-    ff_rows = grad_contract.shape[0] // n
-    shard_contract = shards[after : after + ff_rows]
-    shard_gain_two = shards[after + ff_rows, :rows]
-    shard_joint = jnp.transpose(joint_raw[:, :, : 3 * QW].reshape(PLANES, rows, 3, QW), (1, 2, 0, 3))
-    shard_joint = shard_joint.reshape(rows, 3 * PLANES * QW)
-    shard_gain_one = jnp.sum(joint_raw[:, :, -1], axis=0) / lax.dynamic_slice_in_dim(gain_one, me * rows, rows)
+    dealt, shard_joint, shard_output, shard_expand, shard_contract = finish(
+        n, T, exp_w.shape[1], con_w.shape[0] // n, d_got, w_all, jq_all, jk_all
+    )
+    width = D // n
+    gain_grads = jnp.sum(gain_all, axis=0).reshape(-1)[: 2 * D].reshape(2, D)
+    gain_grads = lax.dynamic_slice_in_dim(gain_grads, me * width, width, axis=1)
     return (
         output[None],
         dealt[None],
@@ -1125,8 +1518,8 @@
         shard_output,
         shard_expand,
         shard_contract,
-        shard_gain_one,
-        shard_gain_two,
+        gain_grads[0],
+        gain_grads[1],
     )
 
 

time: 261 us -> 236 us (0.904); the launches traced: 259 us -> 232 us
  local copies, waits for them, and re-layouts: 25.2 us -> 6.03 us
  Pallas kernels: 203 us -> 215 us
  matrix products: 10.1 us -> 0 us
  waiting for transfers between devices: 7.77 us -> 0.01 us
  other arithmetic: 5.42 us -> 2.39 us
    pallas_call x0 -> x2, Pallas kernels: none -> 33.6 us  [the longest x1 30.5 us: middle(): pl.pallas_call(functools.partial(middle_kernel, n, groups), out_shape=(sh...]
    pallas_call x1, Pallas kernels: 111 us -> 85.2 us  [tail(): pl.pallas_call(functools.partial(tail_kernel, n, groups), out_shape=(jax....]
    dot_general x9 -> x0, matrix products: 10.1 us -> none  [the longest x1 2.81 us: on_device(): jnp.einsum('td,fd->tf', grad_out, con_w, preferred_element_type=f32)]
    unnamed x31 -> x7, local copies, waits for them, and re-layouts: 11.6 us -> 1.74 us
    ppermute x6 -> x3, waiting for transfers between devices: 7.77 us -> 0.01 us  [over_planes(): lax.ppermute(x, 'ctx', [(h * S + s, (h + k) % PLANES * S + s) for h in ra...]
    slice x6 -> x0, local copies, waits for them, and re-layouts: 6.04 us -> none  [the longest x1 1.88 us: on_device(): shards[(1 + i) * rows:(2 + i) * rows]]
    ppermute x6 -> x3, starting transfers between devices: 7.37 us -> 3.88 us  [over_planes(): lax.ppermute(x, 'ctx', [(h * S + s, (h + k) % PLANES * S + s) for h in ra...]
    ppermute x0 -> x2, starting transfers between devices: none -> 3.37 us  [the longest x1 1.99 us: over_sides(): return lax.ppermute(x, 'ctx', pairs)]
  transfers between devices with their start and end apart: 6 -> 5, of which waited for: 2 -> 0; matrix products, arithmetic and copies ran while one was open for 4% -> 1% of each run, Pallas kernels for 0% -> 10%
where the time goes in v1:
time: 236 us; the launch traced here: 232 us
  Pallas kernels  215 us (91%)
  starting transfers between devices  7.25 us (3%)
  local copies, waits for them, and re-layouts  6.03 us (3%)
  other arithmetic  2.39 us (1%)
    pallas_call x1, Pallas kernels, tail(): pl.pallas_call(functools.partial(tail_kernel, n, groups), out_shape=(jax....  85.2 us
    pallas_call x1, Pallas kernels, front(): pl.pallas_call(functools.partial(front_kernel, n, groups, lengths.shape[1...  56.7 us
    pallas_call x1, Pallas kernels, middle(): pl.pallas_call(functools.partial(middle_kernel, n, groups), out_shape=(sh...  30.5 us
    pallas_call x1, Pallas kernels, attn_bwd(): pl.pallas_call(functools.partial(bwd_kernel, n, lengths.shape[1]), out_sh...  23.7 us
    pallas_call x1, Pallas kernels, attn_fwd(): pl.pallas_call(functools.partial(fwd_kernel, n, lengths.shape[1]), out_sh...  16 us
  transfers between devices with their start and end apart: 5, of which 0 were waited for; matrix products, arithmetic and copies ran while one was open for 1% of the time, Pallas kernels for 10%

profile of v1, /device:TPU:0, one launch (start us, length us, event | category | flops | bytes accessed | tf_op | source)
XLA Modules:
  0.0 231.6 jit_solution(1337156295583933112)
XLA Ops:
  0.6 0.6 multiply_power_fusion.freq_ref
  1.3 1.2 broadcast_in_dim.13.gain_one_ref
  2.5 1.2 broadcast_in_dim.14.gain_two_ref
  3.7 56.7 %shard_map.161 = (bf16[4,256,768]{2,1,0:T(8,128)(2,1)}, bf16[4,192,256]{2,1,0:T(8,128)(2,1)}, bf16[16,256,384]{2,1,0:T(8,128)(2,1)}, bf16[640,768]{1,0:T(8,128)(...) custom-call(s32[1,3]{1,0:T(1,128)} %lengths_ref.5, ...), custom_call_target="tpu_custom_call" | custom-call | tf_op jit(solution)/shard_map/pallas_call | solution.py:547
  60.5 16.0 %shard_map.162 = (f32[4,192,256]{2,1,0:T(8,128)}, bf16[4,192,256]{2,1,0:T(8,128)(2,1)}, f32[4,8,256]{2,1,0:T(8,128)}) custom-call(s32[1,3]{1,0:T(1,128)} %lengths_ref.5, bf16[4,192,256]{2,1,0:T(8,128)(2,1)} %get-tuple-element.42.qt_ref, bf16[16,256,384]{2,1,0:T(8,128)(2,1)} %get-tuple-element.43.kv_ref), custom_call_target="tpu_custom_call" | custom-call | tf_op jit(solution)/shard_map/pallas_call | solution.py:148
  76.4 30.5 %shard_map.163 = (bf16[256,768]{1,0:T(8,128)(2,1)}, f32[256,768]{1,0:T(8,128)}, bf16[4,192,256]{2,1,0:T(8,128)(2,1)}, f32[8,768]{1,0:T(8,128)}, bf16[4,2,48,768]...) custom-call(bf16[4,192,256]{2,1,0:T(8,128)(2,1)} %get-tuple-element., ...), custom_call_target="tpu_custom_call" | custom-call | tf_op jit(solution)/shard_map/pallas_call | solution.py:823
  106.9 1.4 collective-permute-start
  108.3 2.0 collective-permute-start.1
  110.3 1.2 slice_bitcast_fusion.2
  111.5 1.2 collective-permute-start.2
  112.7 2.4 %collective-permute-start.3 = (bf16[2,2,48,768]{3,2,1,0:T(8,128)(2,1)S(1)}, bf16[2,2,48,768]{3,2,1,0:T(8,128)(2,1)S(1)}, u32[]{:S(2)}, u32[]{:S(2)}) collective-permute-start(bf16[2,2,48,768]{3,2,1,0:T(8,128)(2,1)S(1)} %get-tuple-element.78), channel_id=1, source_target_pairs={{0,16},{2,18},{4,20},{6,22},{8,24},{10,26},{12,28},{14,30},{16,0},... | collective-permute-start | bytes 884744 | tf_op jit(solution)/shard_map/ppermute | solution.py:1458
  115.1 0.3 collective-permute-start.4
  115.4 23.7 %shard_map.164 = (f32[4,192,256]{2,1,0:T(8,128)}, bf16[16,256,384]{2,1,0:T(8,128)(2,1)}) custom-call(s32[1,3]{1,0:T(1,128)} %lengths_ref.5, bf16[4,192,256]{2,1,0:T(8,128)(2,1)} %get-tuple-element.42.qt_ref, bf16[16,256,384]{2,1,0:T(8,128)(2,1)} %get-tuple-element.43.kv_ref, f32[4,192,256]{2,1,0:T(8,128)} %get-tuple-element.50.ot_ref, ...), custom_call_target="tpu_custom_call" | custom-call | tf_op jit(solution)/shard_map/pallas_call | solution.py:231
  139.1 0.0 collective-permute-done.2
  139.1 0.0 collective-permute-done.3
  139.1 0.0 collective-permute-done.4
  139.1 1.0 pad_maximum_fusion.z_got_hbm
  140.1 0.0 collective-permute-done.y_got_hbm
  140.1 0.0 copy-start
  140.1 0.0 collective-permute-done.1.x_got_hbm
  140.1 0.0 copy-start.1
  140.1 0.8 copy-done
  140.9 0.2 copy-done.1
  141.1 0.0 copy-start.2
  141.1 85.2 %shard_map.165 = (bf16[16,16,768]{2,1,0:T(8,128)(2,1)}, bf16[2,144,768]{2,1,0:T(8,128)(2,1)}, bf16[2,4,48,192]{3,2,1,0:T(8,128)(2,1)}, bf16[2,4,48,384]{3,2,1,0:T(8,128)(2,1)}, f32[2,16,128]{2,1,0:T(8,128)}) custom-call(s32[32]{0:T(128)} %bitcast.42, f32[4,192,256]{2,1,0:T(8,128)} %get-tuple-element.53.dq_ref, bf16[4,2,2,256,384]{4,3,2,1,0:T(8,128)(2,1)} %bitcast.30, ...), custom_call_target="tpu_custom_call" | custom-call | tf_op jit(solution)/shard_map/pallas_call | solution.py:1326
  226.4 0.7 reduce_sum.9
  227.1 0.1 constant_dynamic-slice_fusion
  227.2 0.5 slice_bitcast_fusion.3
  227.7 3.1 %shard_map.166 = (bf16[256,768]{1,0:T(8,128)(2,1)}, f32[48,2304]{1,0:T(8,128)}, f32[48,768]{1,0:T(8,128)}, f32[48,2304]{1,0:T(8,128)}, f32[72,768]{1,0:T(8,128)}) custom-call(bf16[16,16,768]{2,1,0:T(8,128)(2,1)} %get-tuple-element.66.d_ref, bf16[2,144,768]{2,1,0:T(8,128)(2,1)} %get-tuple-element.67.w_ref, bf16[2,4,48,192]{3,2,1,0:T(8,128)(2,1)} %get-tuple-element.68.jq_ref, ...), custom_call_target="tpu_custom_call" | custom-call | tf_op jit(solution)/shard_map/pallas_call | solution.py:1424
  230.8 0.0 copy-done.2
  230.8 0.7 copy.20
  (1 shorter events, 0.0 us)
Async XLA Ops:
  106.9 33.2 %collective-permute-start = (bf16[1,4,2,48,768]{4,3,2,1,0:T(8,128)(2,1)}, bf16[1,4,2,48,768]{4,3,2,1,0:T(8,128)(2,1)S(1)}, u32[]{:S(2)}, u32[]{:S(2)}) collective-permute-start(bf16[1,4,2,48,768]{4,3,2,1,0:T(8,128)(2,1)} %get-tuple-element.61), channel_id=1, source_target_pairs={{0,1},{1,0},{2,3},{3,2},{4,5},{5,4},{6,7},{7,6},{8,9},{9,8},{10,11... | collective-permute-start | bytes 1769480 | tf_op jit(solution)/shard_map/ppermute | solution.py:1467
  108.3 31.8 %collective-permute-start.1 = (bf16[1,4,2,48,768]{4,3,2,1,0:T(8,128)(2,1)}, bf16[1,4,2,48,768]{4,3,2,1,0:T(8,128)(2,1)S(1)}, u32[]{:S(2)}, u32[]{:S(2)}) collective-permute-start(bf16[1,4,2,48,768]{4,3,2,1,0:T(8,128)(2,1)} %get-tuple-element.63), channel_id=1, source_target_pairs={{0,4},{2,6},{4,0},{6,2},{8,12},{10,14},{12,8},{14,10},{16,20},{18,... | collective-permute-start | bytes 1769480 | tf_op jit(solution)/shard_map/ppermute | solution.py:1464
  111.5 27.6 %collective-permute-start.2 = (bf16[2,2,48,768]{3,2,1,0:T(8,128)(2,1)S(1)}, bf16[2,2,48,768]{3,2,1,0:T(8,128)(2,1)S(1)}, u32[]{:S(2)}, u32[]{:S(2)}) collective-permute-start(bf16[2,2,48,768]{3,2,1,0:T(8,128)(2,1)S(1)} %get-tuple-element.76), channel_id=1, source_target_pairs={{0,8},{2,10},{4,12},{6,14},{8,16},{10,18},{12,20},{14,22},{16,24},... | collective-permute-start | bytes 884744 | tf_op jit(solution)/shard_map/ppermute | solution.py:1458
  112.7 26.3 %collective-permute-start.3 = (bf16[2,2,48,768]{3,2,1,0:T(8,128)(2,1)S(1)}, bf16[2,2,48,768]{3,2,1,0:T(8,128)(2,1)S(1)}, u32[]{:S(2)}, u32[]{:S(2)}) collective-permute-start(bf16[2,2,48,768]{3,2,1,0:T(8,128)(2,1)S(1)} %get-tuple-element.78), channel_id=1, source_target_pairs={{0,16},{2,18},{4,20},{6,22},{8,24},{10,26},{12,28},{14,30},{16,0},... | collective-permute-start | bytes 884744 | tf_op jit(solution)/shard_map/ppermute | solution.py:1458
  115.1 23.9 %collective-permute-start.4 = (bf16[2,2,48,768]{3,2,1,0:T(8,128)(2,1)S(1)}, bf16[2,2,48,768]{3,2,1,0:T(8,128)(2,1)S(1)}, u32[]{:S(2)}, u32[]{:S(2)}) collective-permute-start(bf16[2,2,48,768]{3,2,1,0:T(8,128)(2,1)S(1)} %get-tuple-element.77), channel_id=1, source_target_pairs={{0,24},{2,26},{4,28},{6,30},{8,0},{10,2},{12,4},{14,6},{16,8},{18,... | collective-permute-start | bytes 884744 | tf_op jit(solution)/shard_map/ppermute | solution.py:1458
  140.1 0.8 copy-start
  140.1 1.0 copy-start.1
  141.1 89.7 %copy-start.2 = (bf16[256,768]{1,0:T(8,128)(2,1)S(1)}, bf16[256,768]{1,0:T(8,128)(2,1)}, u32[]{:S(2)}) copy-start(bf16[256,768]{1,0:T(8,128)(2,1)} %get-tuple-element.49) | copy-start | bytes 1179652

commit v2 on v1

--- a/solution.py
+++ b/solution.py
@@ -3,6 +3,7 @@
 
 import jax
 import jax.numpy as jnp
+import numpy as np
 from jax import lax
 from jax.experimental import pallas as pl
 from jax.experimental.pallas import tpu as pltpu
@@ -250,7 +251,6 @@
     joint_ref,
     gain_one_ref,
     gain_two_ref,
-    freq_ref,
     out_hbm,
     exp_hbm,
     con_hbm,
@@ -349,8 +349,8 @@
             if begin < end:
                 cols[c, begin - c * half : end - c * half] = chosen[begin - low : end - low].astype(bf)
     gain_held[group] = jnp.zeros_like(gain_held[group])
-    gain_held[group, 0:1] = gain_one_ref[...].astype(f32)
-    gain_held[group, 1:2] = gain_two_ref[...].astype(f32)
+    gain_held[group, 0:1] = gain_one_ref[...].astype(f32).reshape(1, -1)
+    gain_held[group, 1:2] = gain_two_ref[...].astype(f32).reshape(1, -1)
     col_moves = [
         remote(cols.at[core], cols_all.at[group, core], g_sems, k - 1, group_peer(k)) for k in range(1, groups)
     ]
@@ -380,11 +380,15 @@
         copy.start()
 
     ends = ends_of(lengths_ref, count)
+    row = lax.broadcasted_iota(jnp.int32, (HALF, T), 0)
+    frequencies = jnp.zeros((HALF, T), f32)
+    for i in range(HALF):
+        frequencies = jnp.where(row == i, float(np.float32(rope_base ** (-2.0 * i / HEAD_DIM))), frequencies)
     for j in range(PLANES):
         base = (lax.rem(plane + PLANES - j, PLANES) * S + side) * T
         index = base + lax.broadcasted_iota(jnp.int32, (8, T), 1)
         begin, _ = span_of(index, ends)
-        angles = (index - begin)[0:1].astype(f32) * freq_ref[...]
+        angles = (index - begin)[0:1].astype(f32) * frequencies
         turn_ref[j, :HALF] = jnp.cos(angles)
         turn_ref[j, HALF:] = jnp.sin(angles)
 
@@ -542,7 +546,6 @@
     any_, vm, sm = (pl.BlockSpec(memory_space=m) for m in (pl.ANY, pltpu.VMEM, pltpu.SMEM))
     sems = lambda count: pltpu.SemaphoreType.DMA((2, count))
     halves = lambda w: w.reshape(2, w.shape[0] // 2, w.shape[1])
-    frequencies = rope_base ** (-jnp.arange(0, HEAD_DIM, 2).astype(f32) / HEAD_DIM)
     weights = [halves(w) for w in (out_w, exp_w, con_w)]
     return pl.pallas_call(
         functools.partial(front_kernel, n, groups, lengths.shape[1]),
@@ -555,7 +558,7 @@
             jax.ShapeDtypeStruct((8, D), f32),
             *[jax.ShapeDtypeStruct((groups, *w.shape), bf) for w in weights],
         ),
-        in_specs=[sm, vm, vm, vm, vm, vm, any_, any_, any_],
+        in_specs=[sm, vm, vm, vm, vm, any_, any_, any_],
         out_specs=(vm, vm, any_, vm, vm, vm, any_, any_, any_),
         scratch_shapes=[
             pltpu.VMEM((PLANES, T, D), bf),
@@ -577,9 +580,8 @@
         lengths,
         tokens,
         joint_shard,
-        gain_first[None],
-        gain_second[None],
-        frequencies[:, None],
+        gain_first,
+        gain_second,
         *weights,
     )
 
@@ -597,13 +599,14 @@
     output_ref,
     grad_hidden_ref,
     gt_ref,
-    gain_ref,
     y_keep,
     y_send,
     x_keep,
     x_send,
     z_keep,
-    z_send,
+    z_send_1,
+    z_send_2,
+    z_send_3,
     out_w,
     exp_w,
     con_w,
@@ -721,7 +724,7 @@
         return total
 
     total = lax.fori_loop(0, T // strip, norm_back, jnp.zeros((1, D), f32))
-    gain_ref[...] = jnp.broadcast_to(total, gain_ref.shape)
+    gain_two = jnp.broadcast_to(total, (8, D))
     for p in range(PLANES):
         g_send[p] = nt(out_w[p * QW : (p + 1) * QW], branch[...]).astype(bf)
     away = [
@@ -744,7 +747,8 @@
                 else:
                     value = acc[pl.ds(pl.multiple_of((2 * m + parity) * rows, 8), rows)]
                 if height > rows:
-                    value = jnp.concatenate([value, jnp.zeros((height - rows, D), f32)], axis=0)
+                    rest = jnp.zeros((height - rows - 8, D), f32)
+                    value = jnp.concatenate([value, gain_two, rest], axis=0)
                 value = value.astype(bf)
                 target[m, offset : offset + height] = value
                 return carry
@@ -797,12 +801,13 @@
             (x_send.at[k - 1] if k else x_keep)[p, g] = summed(p * S2 + a, third(g, 1))
 
         each(PLANES * groups, second_part)
+    z_parts = [z_keep, z_send_1, z_send_2, z_send_3]
     for k in range(PLANES):
         p = lax.rem(plane + k, PLANES)
 
         def third_part(i, k=k, p=p):
             a, g = i // groups, lax.rem(i, groups)
-            (z_send.at[k - 1] if k else z_keep)[a, g] = summed(p * S2 + a, third(g, 2))
+            z_parts[k][a, g] = summed(p * S2 + a, third(g, 2))
 
         each(S2 * groups, third_part)
     for copy in away:
@@ -814,7 +819,7 @@
     S2 = n // PLANES // 2
     T, D = tokens.shape
     ffn = con_w.shape[0]
-    used = (D + 2 * ffn + ffn) // n
+    used = (D + 2 * ffn + ffn) // n + 8
     height = -(-used // (groups * 48)) * 16
     any_, vm = pl.BlockSpec(memory_space=pl.ANY), pl.BlockSpec(memory_space=pltpu.VMEM)
     sems = lambda count: pltpu.SemaphoreType.DMA((2, count))
@@ -826,16 +831,15 @@
             shape(T, D),
             jax.ShapeDtypeStruct((T, D), f32),
             shape(PLANES, QW, T),
-            jax.ShapeDtypeStruct((8, D), f32),
             shape(PLANES, S2, height, D),
             shape(groups - 1, PLANES, S2, height, D),
             shape(PLANES, groups, height, D),
             shape(S2 - 1, PLANES, groups, height, D),
             shape(S2, groups, height, D),
-            shape(PLANES - 1, S2, groups, height, D),
+            *[shape(S2, groups, height, D)] * (PLANES - 1),
         ),
         in_specs=[vm, vm, vm, vm, any_, any_, any_],
-        out_specs=tuple([vm] * 10),
+        out_specs=tuple([vm] * 11),
         scratch_shapes=[
             pltpu.VMEM(out_w.shape, bf),
             pltpu.VMEM(exp_w.shape, bf),
@@ -869,7 +873,7 @@
     dkv_ref,
     turn_ref,
     gains_ref,
-    gain_two_ref,
+    joint_hbm,
     joint_t_hbm,
     first_hbm,
     tokens_hbm,
@@ -879,12 +883,14 @@
     x_keep_hbm,
     x_got_hbm,
     z_keep_hbm,
-    z_got_hbm,
+    z_got_1,
+    z_got_2,
+    z_got_3,
     d_got,
     w_all,
     jq_all,
     jk_all,
-    gain_all,
+    joint_rows,
     joint_t,
     first,
     tokens,
@@ -919,6 +925,7 @@
     x1_got,
     y2_got,
     y3_got,
+    z1_got,
     x3_got,
     w_plane,
     w_plane_got,
@@ -927,9 +934,8 @@
     d_mid,
     d_back,
     d_sems,
-    gain_part,
-    gain_got,
-    gain_sems,
+    row_sems,
+    row_local,
 ):
     bf, f32 = jnp.bfloat16, jnp.float32
     S = n // PLANES
@@ -979,7 +985,9 @@
                 (x_keep_hbm, x_keep),
                 (x_got_hbm, x_got),
                 (z_keep_hbm, z_keep),
-                (z_got_hbm, z_came),
+                (z_got_1, z_came.at[0]),
+                (z_got_2, z_came.at[1]),
+                (z_got_3, z_came.at[2]),
                 (tokens_hbm, tokens),
                 (grad_hidden_hbm, grad_hidden),
             ]
@@ -1014,6 +1022,42 @@
     core_kv = [remote(dkv_ref.at[order[t], :, 1 - core], kv_near.at[t], kv_sems, t, core_peer) for t in steps]
     for copy in core_kv:
         copy.start()
+
+    per_group = joint_hbm.shape[0]
+    index = me - group * per_group
+    held_here = (index >= 0) & (index < per_group)
+    row_own = pltpu.make_async_copy(joint_hbm.at[jnp.clip(index, 0, per_group - 1)], joint_rows, row_local.at[0])
+    row_moves = [
+        send(
+            joint_hbm.at[jnp.clip(index, 0, per_group - 1)],
+            joint_rows,
+            row_sems.at[k - 1],
+            row_sems.at[groups - 1],
+            group_peer(k),
+        )
+        for k in range(1, groups)
+    ]
+
+    @pl.when(held_here)
+    def _():
+        row_own.start()
+        for copy in row_moves:
+            copy.start()
+
+    w_moves = []
+
+    def w_copy(source, target, device):
+        copy = remote(source, target, w_sems, len(w_moves), device)
+        w_moves.append(copy)
+        copy.start()
+        return copy
+
+    local[2].wait()
+    local[3].wait()
+    for p in range(PLANES):
+        for a in range(S2):
+            y_keep[p, a] = total_of([y_keep[p, a]] + [y_got[k, p, a] for k in range(groups - 1)]).astype(bf)
+    z1 = [w_copy(y_keep.at[lax.rem(plane + k, PLANES)], z1_got.at[k - 1], plane_peer(k)) for k in range(1, PLANES)]
 
     def turned_back(x, t):
         cos, sin = turn_ref[back[t], :HALF], turn_ref[back[t], HALF:]
@@ -1040,28 +1084,14 @@
     for t in steps:
         mixed_q[t] = turned_back(dq_ref[back[t]], t).astype(bf)
 
-    w_moves = []
-
-    def w_copy(source, target, device):
-        copy = remote(source, target, w_sems, len(w_moves), device)
-        w_moves.append(copy)
-        copy.start()
-        return copy
-
     local[4].wait()
     local[5].wait()
     for p in range(PLANES):
         for g in range(groups):
             x_keep[p, g] = total_of([x_keep[p, g]] + [x_got[k, p, g] for k in range(S2 - 1)]).astype(bf)
     y2 = [w_copy(x_keep.at[:, lax.rem(group + k, groups)], y2_got.at[k - 1], group_peer(k)) for k in range(1, groups)]
-    local[2].wait()
-    local[3].wait()
-    for p in range(PLANES):
-        for a in range(S2):
-            y_keep[p, a] = total_of([y_keep[p, a]] + [y_got[k, p, a] for k in range(groups - 1)]).astype(bf)
-    x1 = [w_copy(y_keep.at[:, lax.rem(s2 + k, S2)], x1_got.at[k - 1], side_peer(k)) for k in range(1, S2)]
-    local[6].wait()
-    local[7].wait()
+    for i in range(6, 10):
+        local[i].wait()
     for a in range(S2):
         for g in range(groups):
             z_keep[a, g] = total_of([z_keep[a, g]] + [z_came[k, a, g] for k in range(PLANES - 1)]).astype(bf)
@@ -1197,20 +1227,24 @@
     for a in range(S2):
         z_keep[a, group] = total_of([z_keep[a, group]] + [y3_got[k, a] for k in range(groups - 1)]).astype(bf)
     x3 = [w_copy(z_keep.at[lax.rem(s2 + k, S2), group], x3_got.at[k - 1], side_peer(k)) for k in range(1, S2)]
-    relay(1, True)
-    for copy in y2 + x1:
+    for copy in y2:
         copy.wait()
     for p in range(PLANES):
-        w_plane[p, 0] = total_of([y_keep[p, s2]] + [x1_got[k, p] for k in range(S2 - 1)]).astype(bf)
-        w_plane[p, 1] = total_of([x_keep[p, group]] + [y2_got[k, p] for k in range(groups - 1)]).astype(bf)
-    jk_moves = j_side_stage(jk_moves, jk, jk_core, jk_side)
+        w_plane[p] = total_of([x_keep[p, group]] + [y2_got[k, p] for k in range(groups - 1)]).astype(bf)
     w_last = [
         w_copy(w_plane.at[lax.rem(plane + k, PLANES)], w_plane_got.at[k - 1], plane_peer(k)) for k in range(1, PLANES)
     ]
+    for copy in z1:
+        copy.wait()
+    for a in range(S2):
+        y_keep[plane, a] = total_of([y_keep[plane, a]] + [z1_got[k, a] for k in range(PLANES - 1)]).astype(bf)
+    x1 = [w_copy(y_keep.at[plane, lax.rem(s2 + k, S2)], x1_got.at[k - 1], side_peer(k)) for k in range(1, S2)]
+    relay(1, True)
+    jk_moves = j_side_stage(jk_moves, jk, jk_core, jk_side)
     jq_moves = j_group_stage(jq_moves, jq_plane, jq_all)
 
-    local[8].wait()
-    local[9].wait()
+    local[10].wait()
+    local[11].wait()
     came(1 - main, plane).wait_recv()
     add_part(PLANES - 1, 1 - main, plane)
 
@@ -1219,20 +1253,19 @@
         came(main, plane).wait_recv()
         add_part(PLANES - 1, main, plane)
 
-    def norm_back(i, total):
+    def norm_back(i, carry):
         rows = pl.ds(pl.multiple_of(i * strip, strip), strip)
         grad = part[PLANES - 1, rows].astype(f32)
         values = tokens[rows].astype(f32)
         centred = values - jnp.mean(values, axis=-1, keepdims=True)
         scale = lax.rsqrt(jnp.mean(centred * centred, axis=-1, keepdims=True) + norm_eps)
         normal = centred * scale
-        total = total + jnp.sum(grad * normal, axis=0, keepdims=True)
         grad = grad * gains_ref[0:1]
         grad = grad - jnp.mean(grad, axis=-1, keepdims=True) - normal * jnp.mean(grad * normal, axis=-1, keepdims=True)
         grad_hidden[rows] = grad_hidden[rows] + grad * scale
-        return total
-
-    gain_one = lax.fori_loop(0, T // strip, norm_back, jnp.zeros((1, D), f32))
+        return carry
+
+    lax.fori_loop(0, T // strip, norm_back, 0)
 
     blocks = T // BLOCK
     piece = BLOCK // n
@@ -1249,17 +1282,6 @@
         copy.start()
     d_mid[me] = d_send[me]
 
-    per = D // 128
-    gain_part[...] = jnp.zeros_like(gain_part)
-    for i in range(per):
-        gain_part[i : i + 1] = gain_one[:, i * 128 : (i + 1) * 128]
-        gain_part[per + i : per + i + 1] = gain_two_ref[0:1, i * 128 : (i + 1) * 128]
-    gain_moves = [
-        remote(gain_part, gain_got.at[me], gain_sems, k - 1, (lax.rem(me + k, n), group)) for k in range(1, n)
-    ]
-    for copy in gain_moves:
-        copy.start()
-    gain_got[me] = gain_part[...]
     jk_moves = j_plane_stage(jk_moves, jk_core, jk_side, jk_plane)
 
     for copy in out_deal:
@@ -1279,41 +1301,42 @@
         copy.start()
     d_got[me] = d_back[me]
 
-    for copy in gain_moves:
+    for copy in x1 + w_last + x3:
         copy.wait()
-    gain_part[...] = total_of([gain_got[i] for i in range(n)])
-    gain_all[group] = gain_part[...]
-    gain_last = [
-        remote(gain_part, gain_all.at[group], gain_sems, n - 1 + k - 1, group_peer(k)) for k in range(1, groups)
-    ]
-    for copy in gain_last:
-        copy.start()
-    for copy in w_last + x3:
-        copy.wait()
-    height = w_plane.shape[2]
-    for i in range(2):
-        w_all[group, i * height : (i + 1) * height] = total_of(
-            [w_plane[plane, i]] + [w_plane_got[k, i] for k in range(PLANES - 1)]
-        ).astype(bf)
+    height = w_plane.shape[1]
+    w_all[group, :height] = total_of([y_keep[plane, s2]] + [x1_got[k] for k in range(S2 - 1)]).astype(bf)
+    w_all[group, height : 2 * height] = total_of(
+        [w_plane[plane]] + [w_plane_got[k] for k in range(PLANES - 1)]
+    ).astype(bf)
     w_all[group, 2 * height :] = total_of([z_keep[s2, group]] + [x3_got[k] for k in range(S2 - 1)]).astype(bf)
     w_gather = [w_copy(w_all.at[group], w_all.at[group], group_peer(k)) for k in range(1, groups)]
     jk_moves = j_group_stage(jk_moves, jk_plane, jk_all)
 
-    for copy in back_deal + gain_last + w_gather + jq_moves + jk_moves:
+    for copy in back_deal + w_gather + jq_moves + jk_moves:
         copy.wait()
     for t in range(PLANES - 1):
         came_from = send(part.at[t], part.at[t], part_send_sems.at[t], part_recv_sems.at[0], core_peer)
         came_from.wait_send()
 
-
-def tail(n, groups, deal, dqt, dkv, turn, gains, gain_two, joint_t, first, tokens, grad_hidden, pieces):
+    @pl.when(held_here)
+    def _():
+        row_own.wait()
+        for copy in row_moves:
+            copy.wait_send()
+
+    @pl.when(jnp.logical_not(held_here))
+    def _():
+        row_moves[0].wait_recv()
+
+
+def tail(n, groups, deal, dqt, dkv, turn, gains, joint_shard, joint_t, first, tokens, grad_hidden, pieces):
     bf, f32 = jnp.bfloat16, jnp.float32
     S2 = n // PLANES // 2
     T, D = tokens.shape
     rows = D // n
     height = pieces[0].shape[2]
     piece_rows = T // n
-    gain_rows = -(-2 * D // 128 // 8) * 8
+    joint_shard = joint_shard.reshape(-1, rows, joint_shard.shape[1])
     any_, vm, sm = (pl.BlockSpec(memory_space=m) for m in (pl.ANY, pltpu.VMEM, pltpu.SMEM))
     sems = lambda count: pltpu.SemaphoreType.DMA((2, count))
     small = lambda *s: pltpu.VMEM(s, bf)
@@ -1330,17 +1353,18 @@
             jax.ShapeDtypeStruct((groups, 3 * height, D), bf),
             jax.ShapeDtypeStruct((groups, PLANES, rows, QW), bf),
             jax.ShapeDtypeStruct((groups, PLANES, rows, 2 * QW), bf),
-            jax.ShapeDtypeStruct((groups, gain_rows, 128), f32),
+            jax.ShapeDtypeStruct(joint_shard.shape[1:], bf),
         ),
-        in_specs=[sm, vm, vm, vm, vm, vm] + [any_] * 10,
-        out_specs=tuple([vm] * 5),
+        in_specs=[sm, vm, vm, vm, vm] + [any_] * 13,
+        out_specs=tuple([vm] * 4) + (any_,),
         scratch_shapes=[
             pltpu.VMEM(joint_t.shape, bf),
             pltpu.VMEM((PLANES, T, D), bf),
             pltpu.VMEM((T, D), bf),
             pltpu.VMEM((T, D), f32),
-            *[pltpu.VMEM(p.shape, bf) for p in pieces],
-            pltpu.SemaphoreType.DMA((10,)),
+            *[pltpu.VMEM(p.shape, bf) for p in pieces[:5]],
+            pltpu.VMEM((PLANES - 1, *pieces[5].shape), bf),
+            pltpu.SemaphoreType.DMA((12,)),
             small(PLANES, S2, T, 2 * QW),
             small(PLANES, S2, T, 2 * QW),
             small(PLANES, S2 - 1, T, 2 * QW),
@@ -1355,26 +1379,40 @@
             *j_buffers(QW),
             *j_buffers(2 * QW),
             sems(2 * (1 + S2 - 1 + PLANES - 1 + groups - 1)),
-            small(S2 - 1, PLANES, height, D),
+            small(S2 - 1, height, D),
             small(groups - 1, PLANES, height, D),
             small(groups - 1, S2, height, D),
+            small(PLANES - 1, S2, height, D),
             small(S2 - 1, height, D),
-            small(PLANES, 2, height, D),
-            small(PLANES - 1, 2, height, D),
-            sems(3 * (groups - 1) + 2 * (S2 - 1) + PLANES - 1),
+            small(PLANES, height, D),
+            small(PLANES - 1, height, D),
+            sems(3 * (groups - 1) + 2 * (S2 - 1) + 2 * (PLANES - 1)),
             small(n, piece_rows, D),
             small(n, piece_rows, D),
             small(n, piece_rows, D),
             sems(2 * n),
-            pltpu.VMEM((gain_rows, 128), f32),
-            pltpu.VMEM((n, gain_rows, 128), f32),
-            sems(n - 1 + groups - 1),
+            pltpu.SemaphoreType.DMA((groups,)),
+            pltpu.SemaphoreType.DMA((1,)),
         ],
         compiler_params=pltpu.CompilerParams(collective_id=0, has_side_effects=True, vmem_limit_bytes=60 << 20),
-    )(deal, dqt, dkv, turn, gains, gain_two, joint_t, first, tokens, grad_hidden, *pieces)
-
-
-def finish_kernel(n, d_ref, w_ref, jq_ref, jk_ref, dealt_ref, joint_ref, output_ref, expand_ref, contract_ref):
+    )(deal, dqt, dkv, turn, gains, joint_shard, joint_t, first, tokens, grad_hidden, *pieces)
+
+
+def finish_kernel(
+    n,
+    d_ref,
+    w_ref,
+    jq_ref,
+    jk_ref,
+    rows_ref,
+    dealt_ref,
+    joint_ref,
+    output_ref,
+    expand_ref,
+    contract_ref,
+    gain_one_ref,
+    gain_two_ref,
+):
     f32 = jnp.float32
     T, D = dealt_ref.shape
     blocks = T // BLOCK
@@ -1400,6 +1438,8 @@
             cols = (part + 1) * D + i * 2 * QW
             rows = [x[part * QW : (part + 1) * QW] for x in pair]
             joint_ref[:, cols : cols + 2 * QW] = jnp.concatenate(rows, axis=0).T
+    product = jnp.sum(joint_ref[...] * rows_ref[...].astype(f32), axis=1, keepdims=True)
+    gain_one_ref[...] = jnp.broadcast_to(product, gain_one_ref.shape)
     height = w_ref.shape[1]
     rows = D // n
     targets = [(output_ref, 0, rows)]
@@ -1414,9 +1454,11 @@
             target[done : done + part, column : column + D] = w_ref[g, offset : offset + part].astype(f32)
             done += part
             row += part
-
-
-def finish(n, T, wide, contract_rows, d_got, w_all, jq_all, jk_all):
+    g, offset = divmod(row, height)
+    gain_two_ref[...] = w_ref[g, offset : offset + 1].astype(f32)
+
+
+def finish(n, T, wide, contract_rows, d_got, w_all, jq_all, jk_all, joint_rows):
     D = d_got.shape[-1]
     rows = D // n
     f32 = jnp.float32
@@ -1429,10 +1471,12 @@
             jax.ShapeDtypeStruct((rows, D), f32),
             jax.ShapeDtypeStruct((rows, wide), f32),
             jax.ShapeDtypeStruct((contract_rows, D), f32),
+            jax.ShapeDtypeStruct((rows, 128), f32),
+            jax.ShapeDtypeStruct((1, D), f32),
         ),
-        in_specs=[vm] * 4,
-        out_specs=tuple([vm] * 5),
-    )(d_got, w_all, jq_all, jk_all)
+        in_specs=[vm] * 5,
+        out_specs=tuple([vm] * 7),
+    )(d_got, w_all, jq_all, jk_all, joint_rows)
 
 
 def on_device(
@@ -1485,12 +1529,13 @@
     )
     out_w, exp_w, con_w = (w.reshape(-1, w.shape[-1]) for w in (out_w, exp_w, con_w))
     ot, lowt, lse = attn_fwd(n, lengths, qt, kv)
-    output, grad_hidden, gt, gain_two, y_keep, y_send, x_keep, x_send, z_keep, z_send = middle(
+    output, grad_hidden, gt, y_keep, y_send, x_keep, x_send, z_keep, *z_send = middle(
         n, groups, lowt, tokens[0], cotangent[0], gains, out_w, exp_w, con_w
     )
-    y_got, x_got, z_got = moved(y_send, over_groups), moved(x_send, over_sides), moved(z_send, over_planes)
+    y_got, x_got = moved(y_send, over_groups), moved(x_send, over_sides)
+    z_got = [over_planes(part, k + 1) for k, part in enumerate(z_send)]
     dqt, dkv = attn_bwd(n, lengths, qt, kv, ot, lse, gt)
-    d_got, w_all, jq_all, jk_all, gain_all = tail(
+    d_got, w_all, jq_all, jk_all, joint_rows = tail(
         n,
         groups,
         deal[0],
@@ -1498,19 +1543,19 @@
         dkv.reshape(PLANES, S2, 2, T, 2 * QW),
         turn,
         gains,
-        gain_two,
+        joint_projection,
         joint_t,
         first,
         tokens[0],
         grad_hidden,
-        [y_keep, y_got, x_keep, x_got, z_keep, z_got],
+        [y_keep, y_got, x_keep, x_got, z_keep, *z_got],
     )
-    dealt, shard_joint, shard_output, shard_expand, shard_contract = finish(
-        n, T, exp_w.shape[1], con_w.shape[0] // n, d_got, w_all, jq_all, jk_all
+    dealt, shard_joint, shard_output, shard_expand, shard_contract, gain_one, gain_two = finish(
+        n, T, exp_w.shape[1], con_w.shape[0] // n, d_got, w_all, jq_all, jk_all, joint_rows
     )
     width = D // n
-    gain_grads = jnp.sum(gain_all, axis=0).reshape(-1)[: 2 * D].reshape(2, D)
-    gain_grads = lax.dynamic_slice_in_dim(gain_grads, me * width, width, axis=1)
+    gain_one = gain_one[:, 0] / lax.dynamic_slice_in_dim(gains[0], me * width, width)
+    gain_two = lax.dynamic_slice_in_dim(gain_two[0], me * width, width)
     return (
         output[None],
         dealt[None],
@@ -1518,8 +1563,8 @@
         shard_output,
         shard_expand,
         shard_contract,
-        gain_grads[0],
-        gain_grads[1],
+        gain_one,
+        gain_two,
     )
 
 

time: 236 us -> 227 us (0.962); the launches traced: 232 us -> 227 us
  Pallas kernels: 215 us -> 210 us
  starting transfers between devices: 7.25 us -> 10.3 us
    pallas_call x1, Pallas kernels: 85.2 us -> 77.5 us  [tail(): pl.pallas_call(functools.partial(tail_kernel, n, groups), out_shape=(jax....]
    ppermute x1, starting transfers between devices: 1.99 us -> 5.63 us  [over_sides(): return lax.ppermute(x, 'ctx', pairs)]
    broadcast_in_dim x2 -> x0, local copies, waits for them, and re-layouts: 2.49 us -> none  [the longest x1 1.24 us: front(): gain_first[None]]
  transfers between devices with their start and end apart: 5 -> 5, of which waited for: 0 -> 0; matrix products, arithmetic and copies ran while one was open for 1% -> 0% of each run, Pallas kernels for 10% -> 11%
where the time goes in v2:
time: 227 us
  Pallas kernels  210 us (93%)
  starting transfers between devices  10.3 us (5%)
  local copies, waits for them, and re-layouts  4.82 us (2%)
    pallas_call x1, Pallas kernels, tail(): pl.pallas_call(functools.partial(tail_kernel, n, groups), out_shape=(jax....  77.5 us
    pallas_call x1, Pallas kernels, front(): pl.pallas_call(functools.partial(front_kernel, n, groups, lengths.shape[1...  56.7 us
    pallas_call x1, Pallas kernels, middle(): pl.pallas_call(functools.partial(middle_kernel, n, groups), out_shape=(sh...  30.4 us
    pallas_call x1, Pallas kernels, attn_bwd(): pl.pallas_call(functools.partial(bwd_kernel, n, lengths.shape[1]), out_sh...  25.2 us
    pallas_call x1, Pallas kernels, attn_fwd(): pl.pallas_call(functools.partial(fwd_kernel, n, lengths.shape[1]), out_sh...  17.3 us
    ppermute x1, starting transfers between devices, over_sides(): return lax.ppermute(x, 'ctx', pairs)  5.63 us
    ppermute x3, starting transfers between devices, over_planes(): lax.ppermute(x, 'ctx', [(h * S + s, (h + k) % PLANES * S + s) for h in ra...  4.55 us
  transfers between devices with their start and end apart: 5, of which 0 were waited for; matrix products, arithmetic and copies ran while one was open for 0% of the time, Pallas kernels for 11%

profile of v2, /device:TPU:0, one launch (start us, length us, event | category | flops | bytes accessed | tf_op | source)
XLA Modules:
  0.0 226.9 jit_solution(2440727664135778909)
XLA Ops:
  0.6 56.7 %shard_map.161 = (bf16[4,256,768]{2,1,0:T(8,128)(2,1)}, bf16[4,192,256]{2,1,0:T(8,128)(2,1)}, bf16[16,256,384]{2,1,0:T(8,128)(2,1)}, bf16[640,768]{1,0:T(8,128)(...) custom-call(s32[1,3]{1,0:T(1,128)} %lengths_ref.5, ...), custom_call_target="tpu_custom_call" | custom-call | tf_op jit(solution)/shard_map/pallas_call | solution.py:550
  57.4 17.3 %shard_map.162 = (f32[4,192,256]{2,1,0:T(8,128)}, bf16[4,192,256]{2,1,0:T(8,128)(2,1)}, f32[4,8,256]{2,1,0:T(8,128)}) custom-call(s32[1,3]{1,0:T(1,128)} %lengths_ref.5, bf16[4,192,256]{2,1,0:T(8,128)(2,1)} %get-tuple-element.45.qt_ref, bf16[16,256,384]{2,1,0:T(8,128)(2,1)} %get-tuple-element.46.kv_ref), custom_call_target="tpu_custom_call" | custom-call | tf_op jit(solution)/shard_map/pallas_call | solution.py:149
  74.7 30.4 %shard_map.163 = (bf16[256,768]{1,0:T(8,128)(2,1)}, f32[256,768]{1,0:T(8,128)}, bf16[4,192,256]{2,1,0:T(8,128)(2,1)}, bf16[4,2,48,768]{3,2,1,0:T(8,128)(2,1)}, b...) custom-call(bf16[4,192,256]{2,1,0:T(8,128)(2,1)} %get-tuple-element., ...), custom_call_target="tpu_custom_call" | custom-call | tf_op jit(solution)/shard_map/pallas_call | solution.py:828
  105.1 0.1 collective-permute-start
  105.2 5.6 %collective-permute-start.1 = (bf16[1,4,2,48,768]{4,3,2,1,0:T(8,128)(2,1)}, bf16[1,4,2,48,768]{4,3,2,1,0:T(8,128)(2,1)S(1)}, u32[]{:S(2)}, u32[]{:S(2)}) collective-permute-start(bf16[1,4,2,48,768]{4,3,2,1,0:T(8,128)(2,1)} %get-tuple-element.65), channel_id=1, source_target_pairs={{0,4},{2,6},{4,0},{6,2},{8,12},{10,14},{12,8},{14,10},{16,20},{18,... | collective-permute-start | bytes 1769480 | tf_op jit(solution)/shard_map/ppermute | solution.py:1508
  110.8 2.2 collective-permute-start.2
  113.0 1.6 collective-permute-start.3
  114.6 0.8 collective-permute-start.4
  115.4 0.7 slice.7
  116.1 25.2 %shard_map.164 = (f32[4,192,256]{2,1,0:T(8,128)}, bf16[16,256,384]{2,1,0:T(8,128)(2,1)}) custom-call(s32[1,3]{1,0:T(1,128)} %lengths_ref.5, bf16[4,192,256]{2,1,0:T(8,128)(2,1)} %get-tuple-element.45.qt_ref, bf16[16,256,384]{2,1,0:T(8,128)(2,1)} %get-tuple-element.46.kv_ref, f32[4,192,256]{2,1,0:T(8,128)} %get-tuple-element.53.ot_ref, ...), custom_call_target="tpu_custom_call" | custom-call | tf_op jit(solution)/shard_map/pallas_call | solution.py:232
  141.3 0.0 collective-permute-done.2.z_got_1
  141.3 0.0 copy-start.3
  141.3 0.0 collective-permute-done.3.z_got_2
  141.3 0.0 copy-start.4
  141.3 0.0 collective-permute-done.4.z_got_3
  141.3 0.0 copy-start.5
  141.4 0.0 collective-permute-done.y_got_hbm
  141.4 0.0 copy-start
  141.4 0.0 collective-permute-done.1.x_got_hbm
  141.4 0.0 copy-start.1
  141.4 0.6 copy-done.3
  142.0 0.1 copy-done.4
  142.1 0.1 copy-done.5
  142.2 0.2 copy-done
  142.5 0.2 copy-done.1
  142.6 77.5 %shard_map.165 = (bf16[16,16,768]{2,1,0:T(8,128)(2,1)}, bf16[2,144,768]{2,1,0:T(8,128)(2,1)}, bf16[2,4,48,192]{3,2,1,0:T(8,128)(2,1)}, bf16[2,4,48,384]{3,2,1,0:T(8,128)(2,1)}, bf16[48,2304]{1,0:T(8,128)(2,1)}) custom-call(s32[32]{0:T(128)} %bitcast.30, f32[4,192,256]{2,1,0:T(8,128)} %get-tuple-element.56.dq_ref, bf16[4,2,2,256,384]{4,3,2,1,0:T(8,128)(2,1)} %bitcast.22, ...), custom_call_target="tpu_custom_call" | custom-call | tf_op jit(solution)/shard_map/pallas_call | solution.py:1349
  220.2 0.0 copy-start.2
  220.2 3.3 %shard_map.166 = (bf16[256,768]{1,0:T(8,128)(2,1)}, f32[48,2304]{1,0:T(8,128)}, f32[48,768]{1,0:T(8,128)}, f32[48,2304]{1,0:T(8,128)}, f32[72,768]{1,0:T(8,128)}, /*index=5*/f32[48,128]{1,0:T(8,128)}, f32[1,768]{1,0:T(1,128)}) custom-call(bf16[16,16,768]{2,1,0:T(8,128)(2,1)} %get-tuple-element.70.d_ref, bf16[2,144,768]{2,1,0:T(8,128)(2,1)} %get-tuple-element.71.w_ref, ...), custom_call_target="tpu_custom_call" | custom-call | tf_op jit(solution)/shard_map/pallas_call | solution.py:1466
  223.5 0.8 slice_reduce_fusion
  224.3 1.3 dynamic-slice_bitcast_fusion
  225.6 0.6 bitcast_divide_fusion
  226.2 0.0 copy-done.2
  226.2 0.7 copy.19
Async XLA Ops:
  105.1 36.3 %collective-permute-start = (bf16[1,4,2,48,768]{4,3,2,1,0:T(8,128)(2,1)}, bf16[1,4,2,48,768]{4,3,2,1,0:T(8,128)(2,1)S(1)}, u32[]{:S(2)}, u32[]{:S(2)}) collective-permute-start(bf16[1,4,2,48,768]{4,3,2,1,0:T(8,128)(2,1)} %get-tuple-element.63), channel_id=1, source_target_pairs={{0,1},{1,0},{2,3},{3,2},{4,5},{5,4},{6,7},{7,6},{8,9},{9,8},{10,11... | collective-permute-start | bytes 1769480 | tf_op jit(solution)/shard_map/ppermute | solution.py:1511
  105.2 36.2 %collective-permute-start.1 = (bf16[1,4,2,48,768]{4,3,2,1,0:T(8,128)(2,1)}, bf16[1,4,2,48,768]{4,3,2,1,0:T(8,128)(2,1)S(1)}, u32[]{:S(2)}, u32[]{:S(2)}) collective-permute-start(bf16[1,4,2,48,768]{4,3,2,1,0:T(8,128)(2,1)} %get-tuple-element.65), channel_id=1, source_target_pairs={{0,4},{2,6},{4,0},{6,2},{8,12},{10,14},{12,8},{14,10},{16,20},{18,... | collective-permute-start | bytes 1769480 | tf_op jit(solution)/shard_map/ppermute | solution.py:1508
  110.8 30.5 %collective-permute-start.2 = (bf16[2,2,48,768]{3,2,1,0:T(8,128)(2,1)}, bf16[2,2,48,768]{3,2,1,0:T(8,128)(2,1)S(1)}, u32[]{:S(2)}, u32[]{:S(2)}) collective-permute-start(bf16[2,2,48,768]{3,2,1,0:T(8,128)(2,1)} %get-tuple-element.67), channel_id=1, source_target_pairs={{0,8},{2,10},{4,12},{6,14},{8,16},{10,18},{12,20},{14,22},{16,24},... | collective-permute-start | bytes 884744 | tf_op jit(solution)/shard_map/ppermute | solution.py:1502
  113.0 28.3 %collective-permute-start.3 = (bf16[2,2,48,768]{3,2,1,0:T(8,128)(2,1)}, bf16[2,2,48,768]{3,2,1,0:T(8,128)(2,1)S(1)}, u32[]{:S(2)}, u32[]{:S(2)}) collective-permute-start(bf16[2,2,48,768]{3,2,1,0:T(8,128)(2,1)} %get-tuple-element.68), channel_id=1, source_target_pairs={{0,16},{2,18},{4,20},{6,22},{8,24},{10,26},{12,28},{14,30},{16,0},... | collective-permute-start | bytes 884744 | tf_op jit(solution)/shard_map/ppermute | solution.py:1502
  114.6 26.7 %collective-permute-start.4 = (bf16[2,2,48,768]{3,2,1,0:T(8,128)(2,1)}, bf16[2,2,48,768]{3,2,1,0:T(8,128)(2,1)S(1)}, u32[]{:S(2)}, u32[]{:S(2)}) collective-permute-start(bf16[2,2,48,768]{3,2,1,0:T(8,128)(2,1)} %get-tuple-element.69), channel_id=1, source_target_pairs={{0,24},{2,26},{4,28},{6,30},{8,0},{10,2},{12,4},{14,6},{16,8},{18,... | collective-permute-start | bytes 884744 | tf_op jit(solution)/shard_map/ppermute | solution.py:1502
  141.3 0.7 copy-start.3
  141.3 0.8 copy-start.4
  141.3 0.9 copy-start.5
  141.4 1.1 copy-start
  141.4 1.2 copy-start.1
  220.2 6.0 %copy-start.2 = (bf16[256,768]{1,0:T(8,128)(2,1)S(1)}, bf16[256,768]{1,0:T(8,128)(2,1)}, u32[]{:S(2)}) copy-start(bf16[256,768]{1,0:T(8,128)(2,1)} %get-tuple-element.52) | copy-start | bytes 1179652

commit v3 on v2

--- a/solution.py
+++ b/solution.py
@@ -57,7 +57,7 @@
     return (low, full_low, full_high, high), begin[0:1], end[0:1]
 
 
-def over_units(bounds, step):
+def over_units(bounds, step, sizes):
     low, full_low, full_high, high = bounds
 
     def run(begin, end, masked):
@@ -68,24 +68,21 @@
         lax.fori_loop(begin, end, body, 0)
 
     run(low, full_low, True)
-    in_pairs(full_low, full_high, lambda u: step(u, False))
+    in_groups(full_low, full_high, lambda u: step(u, False), sizes)
     run(full_high, high, True)
 
 
-def in_pairs(begin, end, step):
-    pairs = (end - begin) // 2
-
-    def two(i, carry):
-        step(begin + 2 * i)
-        step(begin + 2 * i + 1)
-        return carry
-
-    def one(u, carry):
-        step(u)
-        return carry
-
-    lax.fori_loop(0, pairs, two, 0)
-    lax.fori_loop(begin + 2 * pairs, end, one, 0)
+def in_groups(begin, end, step, sizes):
+    for size in sizes:
+        count = (end - begin) // size
+
+        def some(i, carry, size=size, begin=begin):
+            for e in range(size):
+                step(begin + size * i + e)
+            return carry
+
+        lax.fori_loop(0, count, some, 0)
+        begin = begin + size * count
 
 
 def fwd_kernel(n, count, lengths_ref, qt_ref, kv_ref, ot_ref, lowt_ref, lse_ref, values, scores, top, total, acc):
@@ -117,7 +114,7 @@
                 scores[u, h] = st[h]
                 top[h] = jnp.maximum(top[h], jnp.max(st[h].reshape(T // 8, 8, T), axis=0))
 
-        over_units(bounds, score)
+        over_units(bounds, score, (2, 1))
         m = [jnp.max(top[h], axis=0, keepdims=True) for h in range(HP)]
 
         def gather(u):
@@ -129,7 +126,7 @@
                     values[u, pl.ds(HD + h * HD, HD), :], p[h].astype(jnp.bfloat16), preferred_element_type=jnp.float32
                 )
 
-        in_pairs(bounds[0], bounds[3], gather)
+        in_groups(bounds[0], bounds[3], gather, (4, 2, 1))
         for h in range(HP):
             rows = pl.ds(h * HD, HD)
             l = jnp.sum(total[h], axis=0, keepdims=True)
@@ -210,7 +207,7 @@
                 rows = pl.ds(h * HD, HD)
                 dq[rows, :] += jnp.dot(keys[u, rows, :], ds[h], preferred_element_type=jnp.float32)
 
-        over_units(bounds, one_unit)
+        over_units(bounds, one_unit, (4, 2, 1))
         dqt_ref[b] = dq[...] * (HD**-0.5)
         return carry
 
@@ -262,7 +259,7 @@
     gains_ref,
     out_all,
     exp_all,
-    con_all,
+    con_ref,
     held,
     t_sems,
     cols,
@@ -366,8 +363,11 @@
         copy.start()
     cols_all[group] = cols[...]
 
-    weights = [(out_hbm, out_all, out_held), (exp_hbm, exp_all, exp_held), (con_hbm, con_all, con_held)]
-    w_in, w_own, w_first, w_second = [], [], [], []
+    weights = [(out_hbm, out_all, out_held), (exp_hbm, exp_all, exp_held)]
+    part = core if con_hbm.shape[0] == 2 else 0
+    w_in = [pltpu.make_async_copy(con_hbm.at[part], con_held, w_local.at[0, len(weights)])]
+    w_own = [pltpu.make_async_copy(con_held, con_ref, w_local.at[1, len(weights)])]
+    w_first, w_second = [], []
     for i, (source, target, bounce) in enumerate(weights):
         w_in.append(pltpu.make_async_copy(source, bounce, w_local.at[0, i]))
         w_own.append(pltpu.make_async_copy(bounce, target.at[group], w_local.at[1, i]))
@@ -546,7 +546,8 @@
     any_, vm, sm = (pl.BlockSpec(memory_space=m) for m in (pl.ANY, pltpu.VMEM, pltpu.SMEM))
     sems = lambda count: pltpu.SemaphoreType.DMA((2, count))
     halves = lambda w: w.reshape(2, w.shape[0] // 2, w.shape[1])
-    weights = [halves(w) for w in (out_w, exp_w, con_w)]
+    weights = [halves(w) for w in (out_w, exp_w)]
+    con_w = con_w.reshape(2 if con_w.shape[0] % 32 == 0 else 1, -1, D)
     return pl.pallas_call(
         functools.partial(front_kernel, n, groups, lengths.shape[1]),
         out_shape=(
@@ -557,6 +558,7 @@
             jax.ShapeDtypeStruct((PLANES, 2 * HALF, T), f32),
             jax.ShapeDtypeStruct((8, D), f32),
             *[jax.ShapeDtypeStruct((groups, *w.shape), bf) for w in weights],
+            jax.ShapeDtypeStruct(con_w.shape[1:], bf),
         ),
         in_specs=[sm, vm, vm, vm, vm, any_, any_, any_],
         out_specs=(vm, vm, any_, vm, vm, vm, any_, any_, any_),
@@ -571,9 +573,10 @@
             sems(PLANES * (2 * S2 - 1)),
             pltpu.SemaphoreType.DMA((PLANES,)),
             sems(2 * len(weights) * (groups - 1)),
-            pltpu.SemaphoreType.DMA((2, len(weights))),
+            pltpu.SemaphoreType.DMA((2, len(weights) + 1)),
             pltpu.VMEM((D, width), bf),
             *[pltpu.VMEM(w.shape, bf) for w in weights],
+            pltpu.VMEM(con_w.shape[1:], bf),
         ],
         compiler_params=pltpu.CompilerParams(collective_id=1, has_side_effects=True, vmem_limit_bytes=60 << 20),
     )(
@@ -583,6 +586,7 @@
         gain_first,
         gain_second,
         *weights,
+        con_w,
     )
 
 
@@ -596,37 +600,42 @@
     out_hbm,
     exp_hbm,
     con_hbm,
-    output_ref,
-    grad_hidden_ref,
-    gt_ref,
-    y_keep,
-    y_send,
-    x_keep,
-    x_send,
-    z_keep,
-    z_send_1,
-    z_send_2,
-    z_send_3,
-    out_w,
-    exp_w,
-    con_w,
-    local_sems,
-    att,
-    a_sems,
-    g_send,
-    g_sems,
-    hidden,
-    second,
-    branch,
-    ga,
-    act,
-    gexp,
-    acc,
-    w_own,
-    w_other,
-    w_got,
-    w_sems,
+    *refs,
 ):
+    con_got, refs = refs[: groups - 1], refs[groups - 1 :]
+    (
+        output_ref,
+        grad_hidden_ref,
+        gt_ref,
+        y_keep,
+        y_send,
+        x_keep,
+        x_send,
+        z_keep,
+        z_send_1,
+        z_send_2,
+        z_send_3,
+        out_w,
+        exp_w,
+        con_w,
+        local_sems,
+        c_sems,
+        att,
+        a_sems,
+        g_send,
+        g_sems,
+        hidden,
+        second,
+        branch,
+        ga,
+        act,
+        gexp,
+        acc,
+        w_own,
+        w_other,
+        w_got,
+        w_sems,
+    ) = refs
     bf, f32 = jnp.bfloat16, jnp.float32
     S = n // PLANES
     S2 = S // 2
@@ -640,6 +649,10 @@
         return (lax.rem(plane + k, PLANES) * S + side, group)
 
     core_peer = (plane * S + s2 * 2 + 1 - core, group)
+
+    def group_peer(k):
+        return (me, lax.rem(group + k, groups))
+
 
     def remote(source, target, sems, index, device):
         return pltpu.make_async_remote_copy(
@@ -651,11 +664,28 @@
             device_id_type=pl.DeviceIdType.MESH,
         )
 
+    ff_share = con_hbm.shape[0]
+    split = ff_share % 32 == 0
+
+    def rows_of(g):
+        return pl.ds(pl.multiple_of(g * ff_share, 16), ff_share)
+
+    def half_of(g):
+        if not split:
+            return rows_of(g)
+        half = ff_share // 2
+        return pl.ds(pl.multiple_of(g * ff_share + core * half, 16), half)
+
+    came = [half_of(lax.rem(group + groups - k, groups)) for k in range(1, groups)]
+    con_hands = [remote(con_got[k], con_w.at[came[k]], c_sems, k, core_peer) for k in range(groups - 1)]
+    con_local = [
+        pltpu.make_async_copy(con_got[k], con_w.at[came[k]], local_sems.at[3 + k]) for k in range(groups - 1)
+    ]
     local = [
         pltpu.make_async_copy(source, target, local_sems.at[i])
-        for i, (source, target) in enumerate([(con_hbm, con_w), (out_hbm, out_w), (exp_hbm, exp_w)])
+        for i, (source, target) in enumerate([(con_hbm, con_w.at[rows_of(group)]), (out_hbm, out_w), (exp_hbm, exp_w)])
     ]
-    for copy in local:
+    for copy in local + con_local:
         copy.start()
     barrier = pltpu.get_barrier_semaphore()
     for k in range(1, PLANES):
@@ -664,7 +694,7 @@
     pl.semaphore_wait(barrier, PLANES)
 
     home = [remote(low_ref.at[j], att.at[plane], a_sems, j - 1, plane_peer(PLANES - j)) for j in range(1, PLANES)]
-    for copy in home:
+    for copy in home + (con_hands if split else []):
         copy.start()
     att[plane] = low_ref[0]
 
@@ -672,8 +702,10 @@
         return lax.dot_general(a, b, (((1,), (1,)), ((), ())), preferred_element_type=f32)
 
     chunk = 384
+    cot = cot_ref[...]
     local[0].wait()
-    cot = cot_ref[...]
+    for copy in con_local + (con_hands if split else []):
+        copy.wait()
     for c in range(0, FFN, chunk):
         ga[:, c : c + chunk] = nt(cot, con_w[c : c + chunk])
     local[1].wait()
@@ -759,17 +791,17 @@
         sent[-1].start()
 
     rows = D // n
-    acc[:D] = jnp.dot(attended, branch[...], preferred_element_type=f32)
-    place(rows, 0, rows)
-    second_t = second[...].T
     wide = 2 * FFN // D
-    for i in range(wide):
-        acc[:D] = jnp.dot(second_t, gexp[:, i * D : (i + 1) * D], preferred_element_type=f32)
-        place(rows, (1 + i) * rows, rows)
     for c in range(0, FFN, chunk):
         acc[c : c + chunk] = jnp.dot(act[:, c : c + chunk].T, cot_ref[...], preferred_element_type=f32)
     used = (1 + wide) * rows
     place(FFN // n, used, w_own.shape[1] - used)
+    second_t = second[...].T
+    for i in range(wide):
+        acc[:D] = jnp.dot(second_t, gexp[:, i * D : (i + 1) * D], preferred_element_type=f32)
+        place(rows, (1 + i) * rows, rows)
+    acc[:D] = jnp.dot(attended, branch[...], preferred_element_type=f32)
+    place(rows, 0, rows)
 
     for copy in sent:
         copy.wait()
@@ -814,11 +846,11 @@
         copy.wait()
 
 
-def middle(n, groups, lowt, tokens, cotangent, gains, out_w, exp_w, con_w):
+def middle(n, groups, lowt, tokens, cotangent, gains, out_w, exp_w, con_w, con_got):
     bf, f32 = jnp.bfloat16, jnp.float32
     S2 = n // PLANES // 2
     T, D = tokens.shape
-    ffn = con_w.shape[0]
+    ffn = con_w.shape[0] * groups
     used = (D + 2 * ffn + ffn) // n + 8
     height = -(-used // (groups * 48)) * 16
     any_, vm = pl.BlockSpec(memory_space=pl.ANY), pl.BlockSpec(memory_space=pltpu.VMEM)
@@ -838,13 +870,14 @@
             shape(S2, groups, height, D),
             *[shape(S2, groups, height, D)] * (PLANES - 1),
         ),
-        in_specs=[vm, vm, vm, vm, any_, any_, any_],
+        in_specs=[vm, vm, vm, vm, any_, any_, any_] + [any_] * (groups - 1),
         out_specs=tuple([vm] * 11),
         scratch_shapes=[
             pltpu.VMEM(out_w.shape, bf),
             pltpu.VMEM(exp_w.shape, bf),
-            pltpu.VMEM(con_w.shape, bf),
-            pltpu.SemaphoreType.DMA((3,)),
+            pltpu.VMEM((ffn, D), bf),
+            pltpu.SemaphoreType.DMA((3 + groups - 1,)),
+            sems(groups - 1),
             pltpu.VMEM((PLANES, QW, T), bf),
             sems(PLANES - 1),
             pltpu.VMEM((PLANES, QW, T), bf),
@@ -862,7 +895,7 @@
             sems(2 + 2 * ffn // D),
         ],
         compiler_params=pltpu.CompilerParams(collective_id=2, has_side_effects=True, vmem_limit_bytes=60 << 20),
-    )(lowt, tokens, cotangent, gains, out_w, exp_w, con_w)
+    )(lowt, tokens, cotangent, gains, out_w, exp_w, con_w, *con_got)
 
 
 def tail_kernel(
@@ -1405,6 +1438,7 @@
     jq_ref,
     jk_ref,
     rows_ref,
+    gains_ref,
     dealt_ref,
     joint_ref,
     output_ref,
@@ -1438,8 +1472,14 @@
             cols = (part + 1) * D + i * 2 * QW
             rows = [x[part * QW : (part + 1) * QW] for x in pair]
             joint_ref[:, cols : cols + 2 * QW] = jnp.concatenate(rows, axis=0).T
+    shift = D - lax.axis_index("ctx") * (D // n)
+
+    def own_lanes(x):
+        return pltpu.roll(jnp.broadcast_to(x, (8, D)), shift, 1)[0:1, : D // n]
+
     product = jnp.sum(joint_ref[...] * rows_ref[...].astype(f32), axis=1, keepdims=True)
-    gain_one_ref[...] = jnp.broadcast_to(product, gain_one_ref.shape)
+    product = jnp.broadcast_to(product, (D // n, 128)).T[0:1]
+    gain_one_ref[...] = product / own_lanes(gains_ref[0:1])
     height = w_ref.shape[1]
     rows = D // n
     targets = [(output_ref, 0, rows)]
@@ -1455,10 +1495,10 @@
             done += part
             row += part
     g, offset = divmod(row, height)
-    gain_two_ref[...] = w_ref[g, offset : offset + 1].astype(f32)
-
-
-def finish(n, T, wide, contract_rows, d_got, w_all, jq_all, jk_all, joint_rows):
+    gain_two_ref[...] = own_lanes(w_ref[g, offset : offset + 1].astype(f32))
+
+
+def finish(n, T, wide, contract_rows, d_got, w_all, jq_all, jk_all, joint_rows, gains):
     D = d_got.shape[-1]
     rows = D // n
     f32 = jnp.float32
@@ -1471,12 +1511,12 @@
             jax.ShapeDtypeStruct((rows, D), f32),
             jax.ShapeDtypeStruct((rows, wide), f32),
             jax.ShapeDtypeStruct((contract_rows, D), f32),
-            jax.ShapeDtypeStruct((rows, 128), f32),
-            jax.ShapeDtypeStruct((1, D), f32),
+            jax.ShapeDtypeStruct((1, rows), f32),
+            jax.ShapeDtypeStruct((1, rows), f32),
         ),
-        in_specs=[vm] * 5,
+        in_specs=[vm] * 6,
         out_specs=tuple([vm] * 7),
-    )(d_got, w_all, jq_all, jk_all, joint_rows)
+    )(d_got, w_all, jq_all, jk_all, joint_rows, gains)
 
 
 def on_device(
@@ -1496,7 +1536,6 @@
     T, D = tokens.shape[1:]
     S = n // PLANES
     S2 = S // 2
-    me = lax.axis_index("ctx")
 
     def over_planes(x, k):
         return lax.ppermute(x, "ctx", [(h * S + s, (h + k) % PLANES * S + s) for h in range(PLANES) for s in range(S)])
@@ -1515,7 +1554,7 @@
             return over(x, 1)
         return jnp.stack([over(x[k], k + 1) for k in range(x.shape[0])])
 
-    first, qt, kv, joint_t, turn, gains, out_w, exp_w, con_w = front(
+    first, qt, kv, joint_t, turn, gains, out_w, exp_w, con_half = front(
         n,
         groups,
         lengths,
@@ -1527,10 +1566,11 @@
         expand_weight,
         contract_weight,
     )
-    out_w, exp_w, con_w = (w.reshape(-1, w.shape[-1]) for w in (out_w, exp_w, con_w))
+    con_got = [over_groups(con_half, k) for k in range(1, groups)]
+    out_w, exp_w = (w.reshape(-1, w.shape[-1]) for w in (out_w, exp_w))
     ot, lowt, lse = attn_fwd(n, lengths, qt, kv)
     output, grad_hidden, gt, y_keep, y_send, x_keep, x_send, z_keep, *z_send = middle(
-        n, groups, lowt, tokens[0], cotangent[0], gains, out_w, exp_w, con_w
+        n, groups, lowt, tokens[0], cotangent[0], gains, out_w, exp_w, contract_weight, con_got
     )
     y_got, x_got = moved(y_send, over_groups), moved(x_send, over_sides)
     z_got = [over_planes(part, k + 1) for k, part in enumerate(z_send)]
@@ -1551,11 +1591,8 @@
         [y_keep, y_got, x_keep, x_got, z_keep, *z_got],
     )
     dealt, shard_joint, shard_output, shard_expand, shard_contract, gain_one, gain_two = finish(
-        n, T, exp_w.shape[1], con_w.shape[0] // n, d_got, w_all, jq_all, jk_all, joint_rows
+        n, T, exp_w.shape[1], contract_weight.shape[0] * groups // n, d_got, w_all, jq_all, jk_all, joint_rows, gains
     )
-    width = D // n
-    gain_one = gain_one[:, 0] / lax.dynamic_slice_in_dim(gains[0], me * width, width)
-    gain_two = lax.dynamic_slice_in_dim(gain_two[0], me * width, width)
     return (
         output[None],
         dealt[None],
@@ -1563,8 +1600,8 @@
         shard_output,
         shard_expand,
         shard_contract,
-        gain_one,
-        gain_two,
+        gain_one[0],
+        gain_two[0],
     )
 
 

time: 227 us -> 212 us (0.934); the launches traced: 227 us -> 215 us
  Pallas kernels: 210 us -> 203 us
    pallas_call x1, Pallas kernels: 56.7 us -> 50.2 us  [front(): pl.pallas_call(functools.partial(front_kernel, n, groups, lengths.shape[1...]
    ppermute x1, starting transfers between devices: 5.63 us -> 2.58 us  [over_sides(): return lax.ppermute(x, 'ctx', pairs)]
  transfers between devices with their start and end apart: 5 -> 6, of which waited for: 0 -> 0; matrix products, arithmetic and copies ran while one was open for 0% -> 0% of each run, Pallas kernels for 11% -> 20%
where the time goes in v3:
time: 212 us; the launch traced here: 215 us
  Pallas kernels  203 us (96%)
  starting transfers between devices  8.6 us (4%)
  local copies, waits for them, and re-layouts  2.74 us (1%)
    pallas_call x1, Pallas kernels, tail(): pl.pallas_call(functools.partial(tail_kernel, n, groups), out_shape=(jax....  76.3 us
    pallas_call x1, Pallas kernels, front(): pl.pallas_call(functools.partial(front_kernel, n, groups, lengths.shape[1...  50.2 us
    pallas_call x1, Pallas kernels, middle(): pl.pallas_call(functools.partial(middle_kernel, n, groups), out_shape=(sh...  30.3 us
    pallas_call x1, Pallas kernels, attn_bwd(): pl.pallas_call(functools.partial(bwd_kernel, n, lengths.shape[1]), out_sh...  25.7 us
    pallas_call x1, Pallas kernels, attn_fwd(): pl.pallas_call(functools.partial(fwd_kernel, n, lengths.shape[1]), out_sh...  17.1 us
    ppermute x3, starting transfers between devices, over_planes(): lax.ppermute(x, 'ctx', [(h * S + s, (h + k) % PLANES * S + s) for h in ra...  4.28 us
  transfers between devices with their start and end apart: 6, of which 0 were waited for; matrix products, arithmetic and copies ran while one was open for 0% of the time, Pallas kernels for 20%

profile of v3, /device:TPU:0, one launch (start us, length us, event | category | flops | bytes accessed | tf_op | source)
XLA Modules:
  0.0 215.0 jit_solution(6523562422255423072)
XLA Ops:
  0.6 50.2 %shard_map.161 = (bf16[4,256,768]{2,1,0:T(8,128)(2,1)}, bf16[4,192,256]{2,1,0:T(8,128)(2,1)}, bf16[16,256,384]{2,1,0:T(8,128)(2,1)}, bf16[640,768]{1,0:T(8,128)(...) custom-call(s32[1,3]{1,0:T(1,128)} %lengths_ref.5, ...), custom_call_target="tpu_custom_call" | custom-call | tf_op jit(solution)/shard_map/pallas_call | solution.py:551
  50.9 1.7 collective-permute-start
  52.5 17.1 %shard_map.162 = (f32[4,192,256]{2,1,0:T(8,128)}, bf16[4,192,256]{2,1,0:T(8,128)(2,1)}, f32[4,8,256]{2,1,0:T(8,128)}) custom-call(s32[1,3]{1,0:T(1,128)} %lengths_ref.5, bf16[4,192,256]{2,1,0:T(8,128)(2,1)} %get-tuple-element.45.qt_ref, bf16[16,256,384]{2,1,0:T(8,128)(2,1)} %get-tuple-element.46.kv_ref), custom_call_target="tpu_custom_call" | custom-call | tf_op jit(solution)/shard_map/pallas_call | solution.py:146
  69.6 0.0 collective-permute-done.refs_0_
  69.6 0.0 copy-start.2
  69.6 0.8 copy-done.2
  70.4 30.3 %shard_map.163 = (bf16[256,768]{1,0:T(8,128)(2,1)}, f32[256,768]{1,0:T(8,128)}, bf16[4,192,256]{2,1,0:T(8,128)(2,1)}, bf16[4,2,48,768]{3,2,1,0:T(8,128)(2,1)}, b...) custom-call(bf16[4,192,256]{2,1,0:T(8,128)(2,1)} %get-tuple-element., ...), custom_call_target="tpu_custom_call" | custom-call | tf_op jit(solution)/shard_map/pallas_call | solution.py:860
  100.7 0.1 collective-permute-start.1
  100.8 2.6 %collective-permute-start.2 = (bf16[1,4,2,48,768]{4,3,2,1,0:T(8,128)(2,1)}, bf16[1,4,2,48,768]{4,3,2,1,0:T(8,128)(2,1)S(1)}, u32[]{:S(2)}, u32[]{:S(2)}) collective-permute-start(bf16[1,4,2,48,768]{4,3,2,1,0:T(8,128)(2,1)} %get-tuple-element.65), channel_id=1, source_target_pairs={{0,4},{2,6},{4,0},{6,2},{8,12},{10,14},{12,8},{14,10},{16,20},{18,... | collective-permute-start | bytes 1769480 | tf_op jit(solution)/shard_map/ppermute | solution.py:1547
  103.4 0.9 collective-permute-start.3
  104.3 3.4 %collective-permute-start.4 = (bf16[2,2,48,768]{3,2,1,0:T(8,128)(2,1)}, bf16[2,2,48,768]{3,2,1,0:T(8,128)(2,1)S(1)}, u32[]{:S(2)}, u32[]{:S(2)}) collective-permute-start(bf16[2,2,48,768]{3,2,1,0:T(8,128)(2,1)} %get-tuple-element.68), channel_id=1, source_target_pairs={{0,16},{2,18},{4,20},{6,22},{8,24},{10,26},{12,28},{14,30},{16,0},... | collective-permute-start | bytes 884744 | tf_op jit(solution)/shard_map/ppermute | solution.py:1541
  107.6 0.0 collective-permute-start.5
  107.6 25.7 %shard_map.164 = (f32[4,192,256]{2,1,0:T(8,128)}, bf16[16,256,384]{2,1,0:T(8,128)(2,1)}) custom-call(s32[1,3]{1,0:T(1,128)} %lengths_ref.5, bf16[4,192,256]{2,1,0:T(8,128)(2,1)} %get-tuple-element.45.qt_ref, bf16[16,256,384]{2,1,0:T(8,128)(2,1)} %get-tuple-element.46.kv_ref, f32[4,192,256]{2,1,0:T(8,128)} %get-tuple-element.53.ot_ref, ...), custom_call_target="tpu_custom_call" | custom-call | tf_op jit(solution)/shard_map/pallas_call | solution.py:229
  133.4 0.0 collective-permute-done.3.z_got_1
  133.4 0.0 copy-start.4
  133.4 0.0 collective-permute-done.4.z_got_2
  133.4 0.0 copy-start.5
  133.4 0.0 collective-permute-done.5.z_got_3
  133.4 0.0 copy-start.6
  133.4 0.0 collective-permute-done.1.y_got_hbm
  133.4 0.0 copy-start
  133.4 0.0 collective-permute-done.2.x_got_hbm
  133.4 0.0 copy-start.1
  133.4 0.6 copy-done.4
  134.1 0.1 copy-done.5
  134.2 0.1 copy-done.6
  134.3 0.2 copy-done
  134.5 0.2 copy-done.1
  134.7 76.3 %shard_map.165 = (bf16[16,16,768]{2,1,0:T(8,128)(2,1)}, bf16[2,144,768]{2,1,0:T(8,128)(2,1)}, bf16[2,4,48,192]{3,2,1,0:T(8,128)(2,1)}, bf16[2,4,48,384]{3,2,1,0:T(8,128)(2,1)}, bf16[48,2304]{1,0:T(8,128)(2,1)}) custom-call(s32[32]{0:T(128)} %bitcast.26, f32[4,192,256]{2,1,0:T(8,128)} %get-tuple-element.56.dq_ref, bf16[4,2,2,256,384]{4,3,2,1,0:T(8,128)(2,1)} %bitcast.20, ...), custom_call_target="tpu_custom_call" | custom-call | tf_op jit(solution)/shard_map/pallas_call | solution.py:1382
  211.0 0.0 copy-start.3
  211.0 3.3 %shard_map.166 = (bf16[256,768]{1,0:T(8,128)(2,1)}, f32[48,2304]{1,0:T(8,128)}, f32[48,768]{1,0:T(8,128)}, f32[48,2304]{1,0:T(8,128)}, f32[72,768]{1,0:T(8,128)}, /*index=5*/f32[1,48]{1,0:T(1,128)}, f32[1,48]{1,0:T(1,128)}) custom-call(bf16[16,16,768]{2,1,0:T(8,128)(2,1)} %get-tuple-element.70.d_ref, bf16[2,144,768]{2,1,0:T(8,128)(2,1)} %get-tuple-element.71.w_ref, ...), custom_call_target="tpu_custom_call" | custom-call | tf_op jit(solution)/shard_map/pallas_call | solution.py:1506
  214.3 0.0 copy-done.3
  214.3 0.7 copy.19
Async XLA Ops:
  50.9 18.7 %collective-permute-start = (bf16[288,768]{1,0:T(8,128)(2,1)}, bf16[288,768]{1,0:T(8,128)(2,1)S(1)}, u32[]{:S(2)}, u32[]{:S(2)}) collective-permute-start(bf16[288,768]{1,0:T(8,128)(2,1)} %get-tuple-element.51), channel_id=1, source_target_pairs={{0,1},{1,0},{2,3},{3,2},{4,5},{5,4},{6,7},{7,6},{8,9},{9,8},{10,11... | collective-permute-start | bytes 1327112 | tf_op jit(solution)/shard_map/ppermute | solution.py:1550
  69.6 0.8 copy-start.2
  100.7 32.7 %collective-permute-start.1 = (bf16[1,4,2,48,768]{4,3,2,1,0:T(8,128)(2,1)}, bf16[1,4,2,48,768]{4,3,2,1,0:T(8,128)(2,1)S(1)}, u32[]{:S(2)}, u32[]{:S(2)}) collective-permute-start(bf16[1,4,2,48,768]{4,3,2,1,0:T(8,128)(2,1)} %get-tuple-element.63), channel_id=1, source_target_pairs={{0,1},{1,0},{2,3},{3,2},{4,5},{5,4},{6,7},{7,6},{8,9},{9,8},{10,11... | collective-permute-start | bytes 1769480 | tf_op jit(solution)/shard_map/ppermute | solution.py:1550
  100.8 32.6 %collective-permute-start.2 = (bf16[1,4,2,48,768]{4,3,2,1,0:T(8,128)(2,1)}, bf16[1,4,2,48,768]{4,3,2,1,0:T(8,128)(2,1)S(1)}, u32[]{:S(2)}, u32[]{:S(2)}) collective-permute-start(bf16[1,4,2,48,768]{4,3,2,1,0:T(8,128)(2,1)} %get-tuple-element.65), channel_id=1, source_target_pairs={{0,4},{2,6},{4,0},{6,2},{8,12},{10,14},{12,8},{14,10},{16,20},{18,... | collective-permute-start | bytes 1769480 | tf_op jit(solution)/shard_map/ppermute | solution.py:1547
  103.4 30.0 %collective-permute-start.3 = (bf16[2,2,48,768]{3,2,1,0:T(8,128)(2,1)}, bf16[2,2,48,768]{3,2,1,0:T(8,128)(2,1)S(1)}, u32[]{:S(2)}, u32[]{:S(2)}) collective-permute-start(bf16[2,2,48,768]{3,2,1,0:T(8,128)(2,1)} %get-tuple-element.67), channel_id=1, source_target_pairs={{0,8},{2,10},{4,12},{6,14},{8,16},{10,18},{12,20},{14,22},{16,24},... | collective-permute-start | bytes 884744 | tf_op jit(solution)/shard_map/ppermute | solution.py:1541
  104.3 29.1 %collective-permute-start.4 = (bf16[2,2,48,768]{3,2,1,0:T(8,128)(2,1)}, bf16[2,2,48,768]{3,2,1,0:T(8,128)(2,1)S(1)}, u32[]{:S(2)}, u32[]{:S(2)}) collective-permute-start(bf16[2,2,48,768]{3,2,1,0:T(8,128)(2,1)} %get-tuple-element.68), channel_id=1, source_target_pairs={{0,16},{2,18},{4,20},{6,22},{8,24},{10,26},{12,28},{14,30},{16,0},... | collective-permute-start | bytes 884744 | tf_op jit(solution)/shard_map/ppermute | solution.py:1541
  107.6 25.7 %collective-permute-start.5 = (bf16[2,2,48,768]{3,2,1,0:T(8,128)(2,1)}, bf16[2,2,48,768]{3,2,1,0:T(8,128)(2,1)S(1)}, u32[]{:S(2)}, u32[]{:S(2)}) collective-permute-start(bf16[2,2,48,768]{3,2,1,0:T(8,128)(2,1)} %get-tuple-element.69), channel_id=1, source_target_pairs={{0,24},{2,26},{4,28},{6,30},{8,0},{10,2},{12,4},{14,6},{16,8},{18,... | collective-permute-start | bytes 884744 | tf_op jit(solution)/shard_map/ppermute | solution.py:1541
  133.4 0.7 copy-start.4
  133.4 0.8 copy-start.5
  133.4 0.9 copy-start.6
  133.4 1.0 copy-start
  133.4 1.2 copy-start.1
  211.0 3.3 %copy-start.3 = (bf16[256,768]{1,0:T(8,128)(2,1)S(1)}, bf16[256,768]{1,0:T(8,128)(2,1)}, u32[]{:S(2)}) copy-start(bf16[256,768]{1,0:T(8,128)(2,1)} %get-tuple-element.52) | copy-start | bytes 1179652

commit v4 on v3

--- a/solution.py
+++ b/solution.py
@@ -181,8 +181,10 @@
         qheads = [head_rows(qt, h) for h in range(HP)]
         gheads = [head_rows(gt, h) for h in range(HP)]
         gpad = [jnp.concatenate([zero, x], axis=0) for x in gheads]
-        q = jnp.concatenate([jnp.concatenate([x, zero], axis=0).T for x in qheads], axis=0)
-        g = jnp.concatenate([x.T for x in gpad], axis=0)
+        lanes = lax.broadcasted_iota(jnp.int32, (T, 256), 1) // HD
+        q, g = jnp.concatenate([qt, zero], axis=0).T, jnp.concatenate([zero, gt], axis=0).T
+        q = jnp.concatenate([jnp.where(lanes == h, q, jnp.zeros_like(q)) for h in range(HP)], axis=0)
+        g = jnp.concatenate([jnp.where(lanes == h + 1, g, jnp.zeros_like(g)) for h in range(HP)], axis=0)
         bounds, q_start, q_end = query_block(n, b, T, ends)
         prod = gt.astype(jnp.float32) * ot_ref[b]
         delta = [jnp.sum(prod[h * HD : (h + 1) * HD], axis=0, keepdims=True) for h in range(HP)]
@@ -600,6 +602,7 @@
     out_hbm,
     exp_hbm,
     con_hbm,
+    joint_hbm,
     *refs,
 ):
     con_got, refs = refs[: groups - 1], refs[groups - 1 :]
@@ -615,11 +618,17 @@
         z_send_1,
         z_send_2,
         z_send_3,
+        joint_near,
         out_w,
         exp_w,
         con_w,
         local_sems,
         c_sems,
+        joint_shard,
+        cols,
+        cols_all,
+        col_sems,
+        joint_rows,
         att,
         a_sems,
         g_send,
@@ -685,18 +694,43 @@
         pltpu.make_async_copy(source, target, local_sems.at[i])
         for i, (source, target) in enumerate([(con_hbm, con_w.at[rows_of(group)]), (out_hbm, out_w), (exp_hbm, exp_w)])
     ]
-    for copy in local + con_local:
+    joint_local = pltpu.make_async_copy(joint_hbm, joint_shard, local_sems.at[3 + groups - 1])
+    for copy in [joint_local] + local + con_local:
         copy.start()
     barrier = pltpu.get_barrier_semaphore()
     for k in range(1, PLANES):
         pl.semaphore_signal(barrier, inc=1, device_id=plane_peer(k), device_id_type=pl.DeviceIdType.MESH)
     pl.semaphore_signal(barrier, inc=1, device_id=core_peer, device_id_type=pl.DeviceIdType.MESH)
-    pl.semaphore_wait(barrier, PLANES)
+    for k in range(1, groups):
+        pl.semaphore_signal(barrier, inc=1, device_id=group_peer(k), device_id_type=pl.DeviceIdType.MESH)
+    pl.semaphore_wait(barrier, PLANES + groups - 1)
 
     home = [remote(low_ref.at[j], att.at[plane], a_sems, j - 1, plane_peer(PLANES - j)) for j in range(1, PLANES)]
     for copy in home + (con_hands if split else []):
         copy.start()
     att[plane] = low_ref[0]
+
+    joint_local.wait()
+    pair = 2 * QW
+    for part in range(3):
+        window = joint_shard[:, pl.ds(pl.multiple_of(part * D + plane // 2 * pair, 128), pair)].T
+        chosen = jnp.where(lax.rem(plane, 2) == 1, window[:QW].astype(f32), window[QW:].astype(f32))
+        half = 3 * QW // 2
+        low, high = part * QW, (part + 1) * QW
+        for c in range(2):
+            begin, end = max(low, c * half), min(high, (c + 1) * half)
+            if begin < end:
+                cols[c, begin - c * half : end - c * half] = chosen[begin - low : end - low].astype(bf)
+    col_moves = [
+        remote(cols.at[core], cols_all.at[group, core], col_sems, k - 1, group_peer(k)) for k in range(1, groups)
+    ]
+    col_hands = []
+    for k in range(1, groups):
+        col_came = cols_all.at[lax.rem(group + groups - k, groups), core]
+        col_hands.append(remote(col_came, col_came, col_sems, groups - 1 + k - 1, core_peer))
+    for copy in col_moves:
+        copy.start()
+    cols_all[group] = cols[...]
 
     def nt(a, b):
         return lax.dot_general(a, b, (((1,), (1,)), ((), ())), preferred_element_type=f32)
@@ -715,6 +749,10 @@
     hidden[...] = tokens_ref[...].astype(f32) + jnp.dot(attended.T, out_w[...], preferred_element_type=f32)
 
     strip = 64
+
+    for copy, hand in zip(col_moves, col_hands):
+        copy.wait()
+        hand.start()
 
     def norm(i, carry):
         rows = pl.ds(pl.multiple_of(i * strip, strip), strip)
@@ -767,6 +805,19 @@
         copy.start()
     gt_ref[0] = g_send[plane]
 
+    for copy in col_hands:
+        copy.wait()
+    share = D // groups
+    for g in range(groups):
+        whole = jnp.concatenate([cols_all[g, 0], cols_all[g, 1]], axis=0)
+        if share % 128 == 0:
+            joint_near[:, g * share : (g + 1) * share] = whole
+        else:
+            joint_rows[g * share : (g + 1) * share] = whole.T
+    if share % 128:
+        for i in range(D // 128):
+            joint_near[:, i * 128 : (i + 1) * 128] = joint_rows[i * 128 : (i + 1) * 128].T
+
     sent = []
 
     def place(rows, offset, height):
@@ -846,7 +897,7 @@
         copy.wait()
 
 
-def middle(n, groups, lowt, tokens, cotangent, gains, out_w, exp_w, con_w, con_got):
+def middle(n, groups, lowt, tokens, cotangent, gains, out_w, exp_w, con_w, joint_shard, con_got):
     bf, f32 = jnp.bfloat16, jnp.float32
     S2 = n // PLANES // 2
     T, D = tokens.shape
@@ -869,15 +920,21 @@
             shape(S2 - 1, PLANES, groups, height, D),
             shape(S2, groups, height, D),
             *[shape(S2, groups, height, D)] * (PLANES - 1),
+            shape(3 * QW, D),
         ),
-        in_specs=[vm, vm, vm, vm, any_, any_, any_] + [any_] * (groups - 1),
-        out_specs=tuple([vm] * 11),
+        in_specs=[vm, vm, vm, vm, any_, any_, any_, any_] + [any_] * (groups - 1),
+        out_specs=tuple([vm] * 12),
         scratch_shapes=[
             pltpu.VMEM(out_w.shape, bf),
             pltpu.VMEM(exp_w.shape, bf),
             pltpu.VMEM((ffn, D), bf),
-            pltpu.SemaphoreType.DMA((3 + groups - 1,)),
+            pltpu.SemaphoreType.DMA((4 + groups - 1,)),
             sems(groups - 1),
+            pltpu.VMEM(joint_shard.shape, bf),
+            pltpu.VMEM((2, 3 * QW // 2, D // groups), bf),
+            pltpu.VMEM((groups, 2, 3 * QW // 2, D // groups), bf),
+            sems(2 * (groups - 1)),
+            pltpu.VMEM((D, 3 * QW), bf),
             pltpu.VMEM((PLANES, QW, T), bf),
             sems(PLANES - 1),
             pltpu.VMEM((PLANES, QW, T), bf),
@@ -895,19 +952,20 @@
             sems(2 + 2 * ffn // D),
         ],
         compiler_params=pltpu.CompilerParams(collective_id=2, has_side_effects=True, vmem_limit_bytes=60 << 20),
-    )(lowt, tokens, cotangent, gains, out_w, exp_w, con_w, *con_got)
+    )(lowt, tokens, cotangent, gains, out_w, exp_w, con_w, joint_shard, *con_got)
 
 
 def tail_kernel(
     n,
     groups,
     deal_ref,
-    dq_ref,
-    dkv_ref,
+    dq_hbm,
+    dkv_hbm,
     turn_ref,
     gains_ref,
     joint_hbm,
     joint_t_hbm,
+    joint_near_hbm,
     first_hbm,
     tokens_hbm,
     grad_hidden_hbm,
@@ -925,6 +983,7 @@
     jk_all,
     joint_rows,
     joint_t,
+    joint_near,
     first,
     tokens,
     grad_hidden,
@@ -935,12 +994,17 @@
     z_keep,
     z_came,
     local_sems,
+    dq_ref,
+    kv_own,
+    own_sems,
     kv_near,
     kv_send,
     kv_far,
     kv_sems,
-    mixed_q,
-    mixed_kv,
+    mixed,
+    mixed_got,
+    mixed_send_sems,
+    mixed_recv_sems,
     part,
     part_got,
     part_send_sems,
@@ -1007,6 +1071,24 @@
             total = total + term.astype(f32)
         return total
 
+    lower = plane < 2
+    middle = (plane == 1) | (plane == 2)
+    order = [
+        jnp.where(lower, 3, 0),
+        jnp.where(plane == 0, 2, jnp.where(plane == 1, 0, jnp.where(plane == 2, 3, 1))),
+        jnp.where((plane == 0) | (plane == 2), 1, 2),
+        plane,
+    ]
+    steps = range(PLANES)
+    back = [lax.rem(plane + PLANES - p, PLANES) for p in order]
+    main = jnp.where(lower, 0, 1)
+    main_plane = plane + 1 - 2 * main
+
+    own_kv = [
+        pltpu.make_async_copy(dkv_hbm.at[order[t], :, core], kv_own.at[t], own_sems.at[t]) for t in steps
+    ] + [pltpu.make_async_copy(dq_hbm, dq_ref, own_sems.at[PLANES])]
+    for copy in own_kv:
+        copy.start()
     local = [
         pltpu.make_async_copy(source, target, local_sems.at[i])
         for i, (source, target) in enumerate(
@@ -1023,6 +1105,7 @@
                 (z_got_3, z_came.at[2]),
                 (tokens_hbm, tokens),
                 (grad_hidden_hbm, grad_hidden),
+                (joint_near_hbm, joint_near),
             ]
         )
     ]
@@ -1039,20 +1122,7 @@
         pl.semaphore_signal(barrier, inc=1, device_id=group_peer(k), device_id_type=MESH)
     pl.semaphore_wait(barrier, n - 1 + groups - 1)
 
-    lower = plane < 2
-    middle = (plane == 1) | (plane == 2)
-    order = [
-        jnp.where(lower, 3, 0),
-        jnp.where(plane == 0, 2, jnp.where(plane == 1, 0, jnp.where(plane == 2, 3, 1))),
-        jnp.where((plane == 0) | (plane == 2), 1, 2),
-        plane,
-    ]
-    steps = range(PLANES)
-    back = [lax.rem(plane + PLANES - p, PLANES) for p in order]
-    main = jnp.where(lower, 0, 1)
-    main_plane = plane + 1 - 2 * main
-
-    core_kv = [remote(dkv_ref.at[order[t], :, 1 - core], kv_near.at[t], kv_sems, t, core_peer) for t in steps]
+    core_kv = [remote(dkv_hbm.at[order[t], :, 1 - core], kv_near.at[t], kv_sems, t, core_peer) for t in steps]
     for copy in core_kv:
         copy.start()
 
@@ -1102,9 +1172,10 @@
 
     side_kv = {}
     for t in steps:
+        own_kv[t].wait()
         core_kv[t].wait()
         for a in range(S2):
-            kv_send[t, a] = total_of([dkv_ref[order[t], a, core], kv_near[t, a]]).astype(bf)
+            kv_send[t, a] = total_of([kv_own[t, a], kv_near[t, a]]).astype(bf)
         for k in range(1, S2):
             side_kv[t, k] = remote(
                 kv_send.at[t, lax.rem(s2 + S2 - k, S2)],
@@ -1114,8 +1185,9 @@
                 side_peer(S2 - k),
             )
             side_kv[t, k].start()
+    own_kv[PLANES].wait()
     for t in steps:
-        mixed_q[t] = turned_back(dq_ref[back[t]], t).astype(bf)
+        mixed[t, :QW] = turned_back(dq_ref[back[t]], t).astype(bf)
 
     local[4].wait()
     local[5].wait()
@@ -1138,10 +1210,12 @@
         copy.start()
         return copy
 
-    def j_core_stage(mixed, grads, near):
-        height = mixed.shape[1]
+    def j_core_stage(begin, height, grads, near):
         j_acc[:height] = total_of(
-            [jnp.dot(mixed[t], first[back[t]], preferred_element_type=f32) for t in steps]
+            [
+                jnp.dot(mixed[t, begin : begin + height], first[back[t]], preferred_element_type=f32)
+                for t in steps
+            ]
         )
         shard_rows = D // n
         for i in range(D // 128):
@@ -1150,9 +1224,9 @@
             while row < (i + 1) * 128:
                 shard, offset = divmod(row, shard_rows)
                 count = min(shard_rows - offset, (i + 1) * 128 - row)
-                begin = row - i * 128
+                source = row - i * 128
                 grads[shard // S, shard % S // 2, shard % 2, offset : offset + count] = block[
-                    begin : begin + count
+                    source : source + count
                 ].astype(bf)
                 row += count
         return [j_copy(grads.at[:, :, 1 - core], near, core_peer)]
@@ -1182,78 +1256,100 @@
         return [j_copy(gathered, every.at[group], group_peer(k)) for k in range(1, groups)]
 
     local[0].wait()
-    jq_moves = j_core_stage(mixed_q, jq, jq_core)
+    jq_moves = j_core_stage(0, QW, jq, jq_core)
 
     local[1].wait()
 
-    def main_send(t):
+    half = T // 2
+    halves = range(2)
+
+    def mixed_send(t, e):
+        lanes = pl.ds(e * half, half)
         return send(
-            part.at[t],
-            part_got.at[main, order[t]],
-            part_send_sems.at[t],
-            part_recv_sems.at[main * PLANES + order[t]],
+            mixed.at[t, :, lanes],
+            mixed_got.at[t, :, lanes],
+            mixed_send_sems.at[t, e],
+            mixed_recv_sems.at[t, e],
             at(main_plane, s2, core, group),
         )
 
-    def other_send(t):
+    def part_send(t, e, direction, target):
+        rows = pl.ds(e * half, half)
         return send(
-            part.at[t],
-            part_got.at[1 - main, order[t]],
-            part_send_sems.at[t],
-            part_recv_sems.at[(1 - main) * PLANES + order[t]],
-            at(2 * plane - main_plane, s2, core, group),
+            part.at[t, rows],
+            part_got.at[direction, order[t], rows],
+            part_send_sems.at[t, e],
+            part_recv_sems.at[direction * PLANES + order[t], e],
+            at(target, s2, core, group),
         )
 
-    def came(direction, p):
+    def part_came(direction, p, e):
+        rows = pl.ds(e * half, half)
         return send(
-            part.at[0],
-            part_got.at[direction, p],
-            part_send_sems.at[0],
-            part_recv_sems.at[direction * PLANES + p],
+            part.at[0, rows],
+            part_got.at[direction, p, rows],
+            part_send_sems.at[0, e],
+            part_recv_sems.at[direction * PLANES + p, e],
             core_peer,
         )
 
-    strip = 64
-
-    def add_part(t, direction, p):
-        def body(i, carry):
-            rows = pl.ds(pl.multiple_of(i * strip, strip), strip)
-            part[t, rows] = total_of([part[t, rows], part_got[direction, p, rows]]).astype(bf)
-            return carry
-
-        lax.fori_loop(0, T // strip, body, 0)
-
-    def relay(t, secondary):
+    other_plane = 2 * plane - main_plane
+
+    def product(grads, columns):
+        return jnp.dot(grads.T, columns, preferred_element_type=f32)
+
+    def add_mixed(t, slot, e):
+        mixed_send(slot, e).wait_recv()
+        rows = slice(e * half, (e + 1) * half)
+        near = product(mixed_got[slot, :, rows], joint_near[...])
+        part[t, rows] = (part[t, rows].astype(f32) + near).astype(bf)
+
+    def add_part(t, direction, p, e):
+        part_came(direction, p, e).wait_recv()
+        rows = slice(e * half, (e + 1) * half)
+        part[t, rows] = total_of([part[t, rows], part_got[direction, p, rows]]).astype(bf)
+
+    def relay(t, slot):
         @pl.when(middle)
         def _():
-            direction = 1 - main if secondary else main
-            came(direction, order[t]).wait_recv()
-            add_part(t, direction, order[t])
-            (other_send if secondary else main_send)(t).start()
+            for e in halves:
+                if slot is None:
+                    add_part(t, 1 - main, order[t], e)
+                    part_send(t, e, 1 - main, other_plane).start()
+                else:
+                    add_mixed(t, slot, e)
+                    part_send(t, e, main, main_plane).start()
 
     def key_step(t):
         for k in range(1, S2):
             side_kv[t, k].wait()
         dk = total_of([kv_send[t, s2]] + [kv_far[t, k] for k in range(S2 - 1)]).T
-        mixed_kv[t, :QW] = turned_back(dk[:QW], t).astype(bf)
-        mixed_kv[t, QW:] = dk[QW:].astype(bf)
-        grads = jnp.concatenate([mixed_q[t], mixed_kv[t]], axis=0)
-        part[t] = jnp.dot(grads.T, joint_t[: 3 * QW], preferred_element_type=f32).astype(bf)
+        mixed[t, QW : 2 * QW] = turned_back(dk[:QW], t).astype(bf)
+        mixed[t, 2 * QW :] = dk[QW:].astype(bf)
         if t < PLANES - 1:
 
             @pl.when(jnp.logical_not(middle))
             def _():
-                main_send(t).start()
-
+                for e in halves:
+                    mixed_send(t, e).start()
+
+            @pl.when(middle)
+            def _():
+                part[t] = product(mixed[t], joint_t[: 3 * QW]).astype(bf)
+
+        else:
+            part[t] = product(mixed[t], joint_t[: 3 * QW]).astype(bf)
+
+    local[12].wait()
     key_step(0)
     jq_moves = j_side_stage(jq_moves, jq, jq_core, jq_side)
     key_step(1)
     key_step(2)
-    relay(0, False)
+    relay(0, 0)
     jq_moves = j_plane_stage(jq_moves, jq_core, jq_side, jq_plane)
     key_step(3)
-    relay(2, False)
-    jk_moves = j_core_stage(mixed_kv, jk, jk_core)
+    relay(2, 1)
+    jk_moves = j_core_stage(QW, 2 * QW, jk, jk_core)
 
     for copy in y3:
         copy.wait()
@@ -1272,19 +1368,21 @@
     for a in range(S2):
         y_keep[plane, a] = total_of([y_keep[plane, a]] + [z1_got[k, a] for k in range(PLANES - 1)]).astype(bf)
     x1 = [w_copy(y_keep.at[plane, lax.rem(s2 + k, S2)], x1_got.at[k - 1], side_peer(k)) for k in range(1, S2)]
-    relay(1, True)
+    relay(1, None)
     jk_moves = j_side_stage(jk_moves, jk, jk_core, jk_side)
     jq_moves = j_group_stage(jq_moves, jq_plane, jq_all)
 
     local[10].wait()
     local[11].wait()
-    came(1 - main, plane).wait_recv()
-    add_part(PLANES - 1, 1 - main, plane)
-
     @pl.when(middle)
     def _():
-        came(main, plane).wait_recv()
-        add_part(PLANES - 1, main, plane)
+        for e in halves:
+            add_mixed(PLANES - 1, 2, e)
+
+    for e in halves:
+        add_part(PLANES - 1, 1 - main, plane, e)
+
+    strip = 64
 
     def norm_back(i, carry):
         rows = pl.ds(pl.multiple_of(i * strip, strip), strip)
@@ -1348,8 +1446,15 @@
     for copy in back_deal + w_gather + jq_moves + jk_moves:
         copy.wait()
     for t in range(PLANES - 1):
-        came_from = send(part.at[t], part.at[t], part_send_sems.at[t], part_recv_sems.at[0], core_peer)
-        came_from.wait_send()
+        for e in halves:
+
+            @pl.when(middle)
+            def _(t=t, e=e):
+                part_send(t, e, main, main_plane).wait_send()
+
+            @pl.when(jnp.logical_not(middle))
+            def _(t=t, e=e):
+                mixed_send(t, e).wait_send()
 
     @pl.when(held_here)
     def _():
@@ -1362,7 +1467,7 @@
         row_moves[0].wait_recv()
 
 
-def tail(n, groups, deal, dqt, dkv, turn, gains, joint_shard, joint_t, first, tokens, grad_hidden, pieces):
+def tail(n, groups, deal, dqt, dkv, turn, gains, joint_shard, joint_t, joint_near, first, tokens, grad_hidden, pieces):
     bf, f32 = jnp.bfloat16, jnp.float32
     S2 = n // PLANES // 2
     T, D = tokens.shape
@@ -1388,26 +1493,32 @@
             jax.ShapeDtypeStruct((groups, PLANES, rows, 2 * QW), bf),
             jax.ShapeDtypeStruct(joint_shard.shape[1:], bf),
         ),
-        in_specs=[sm, vm, vm, vm, vm] + [any_] * 13,
+        in_specs=[sm, any_, any_, vm, vm] + [any_] * 14,
         out_specs=tuple([vm] * 4) + (any_,),
         scratch_shapes=[
             pltpu.VMEM(joint_t.shape, bf),
+            pltpu.VMEM(joint_near.shape, bf),
             pltpu.VMEM((PLANES, T, D), bf),
             pltpu.VMEM((T, D), bf),
             pltpu.VMEM((T, D), f32),
             *[pltpu.VMEM(p.shape, bf) for p in pieces[:5]],
             pltpu.VMEM((PLANES - 1, *pieces[5].shape), bf),
-            pltpu.SemaphoreType.DMA((12,)),
+            pltpu.SemaphoreType.DMA((13,)),
+            pltpu.VMEM(dqt.shape, f32),
+            small(PLANES, S2, T, 2 * QW),
+            pltpu.SemaphoreType.DMA((PLANES + 1,)),
             small(PLANES, S2, T, 2 * QW),
             small(PLANES, S2, T, 2 * QW),
             small(PLANES, S2 - 1, T, 2 * QW),
             sems(PLANES * S2),
-            small(PLANES, QW, T),
-            small(PLANES, 2 * QW, T),
+            small(PLANES, 3 * QW, T),
+            small(PLANES - 1, 3 * QW, T),
+            pltpu.SemaphoreType.DMA((PLANES - 1, 2)),
+            pltpu.SemaphoreType.DMA((PLANES - 1, 2)),
             small(PLANES, T, D),
             small(2, PLANES, T, D),
-            pltpu.SemaphoreType.DMA((PLANES - 1,)),
-            pltpu.SemaphoreType.DMA((2 * PLANES,)),
+            pltpu.SemaphoreType.DMA((PLANES - 1, 2)),
+            pltpu.SemaphoreType.DMA((2 * PLANES, 2)),
             pltpu.VMEM((2 * QW, D), f32),
             *j_buffers(QW),
             *j_buffers(2 * QW),
@@ -1428,7 +1539,7 @@
             pltpu.SemaphoreType.DMA((1,)),
         ],
         compiler_params=pltpu.CompilerParams(collective_id=0, has_side_effects=True, vmem_limit_bytes=60 << 20),
-    )(deal, dqt, dkv, turn, gains, joint_shard, joint_t, first, tokens, grad_hidden, *pieces)
+    )(deal, dqt, dkv, turn, gains, joint_shard, joint_t, joint_near, first, tokens, grad_hidden, *pieces)
 
 
 def finish_kernel(
@@ -1569,8 +1680,8 @@
     con_got = [over_groups(con_half, k) for k in range(1, groups)]
     out_w, exp_w = (w.reshape(-1, w.shape[-1]) for w in (out_w, exp_w))
     ot, lowt, lse = attn_fwd(n, lengths, qt, kv)
-    output, grad_hidden, gt, y_keep, y_send, x_keep, x_send, z_keep, *z_send = middle(
-        n, groups, lowt, tokens[0], cotangent[0], gains, out_w, exp_w, contract_weight, con_got
+    output, grad_hidden, gt, y_keep, y_send, x_keep, x_send, z_keep, *z_send, joint_near = middle(
+        n, groups, lowt, tokens[0], cotangent[0], gains, out_w, exp_w, contract_weight, joint_projection, con_got
     )
     y_got, x_got = moved(y_send, over_groups), moved(x_send, over_sides)
     z_got = [over_planes(part, k + 1) for k, part in enumerate(z_send)]
@@ -1585,6 +1696,7 @@
         gains,
         joint_projection,
         joint_t,
+        joint_near,
         first,
         tokens[0],
         grad_hidden,

time: 212 us -> 204 us (0.962); the launches traced: 215 us -> 203 us
  Pallas kernels: 203 us -> 192 us
    pallas_call x1, Pallas kernels: 25.7 us -> 19.6 us  [attn_bwd(): pl.pallas_call(functools.partial(bwd_kernel, n, lengths.shape[1]), out_sh...]
    pallas_call x1, Pallas kernels: 17.1 us -> 13.4 us  [attn_fwd(): pl.pallas_call(functools.partial(fwd_kernel, n, lengths.shape[1]), out_sh...]
  transfers between devices with their start and end apart: 6 -> 6, of which waited for: 0 -> 1; matrix products, arithmetic and copies ran while one was open for 0% -> 0% of each run, Pallas kernels for 20% -> 16%
where the time goes in v4:
time: 204 us; the launch traced here: 203 us
  Pallas kernels  192 us (94%)
  starting transfers between devices  7.68 us (4%)
  local copies, waits for them, and re-layouts  2.71 us (1%)
    pallas_call x1, Pallas kernels, tail(): pl.pallas_call(functools.partial(tail_kernel, n, groups), out_shape=(jax....  74.4 us
    pallas_call x1, Pallas kernels, front(): pl.pallas_call(functools.partial(front_kernel, n, groups, lengths.shape[1...  50.2 us
    pallas_call x1, Pallas kernels, middle(): pl.pallas_call(functools.partial(middle_kernel, n, groups), out_shape=(sh...  30.7 us
    pallas_call x1, Pallas kernels, attn_bwd(): pl.pallas_call(functools.partial(bwd_kernel, n, lengths.shape[1]), out_sh...  19.6 us
    pallas_call x1, Pallas kernels, attn_fwd(): pl.pallas_call(functools.partial(fwd_kernel, n, lengths.shape[1]), out_sh...  13.4 us
  transfers between devices with their start and end apart: 6, of which 1 were waited for; matrix products, arithmetic and copies ran while one was open for 0% of the time, Pallas kernels for 16%

profile of v4, /device:TPU:0, one launch (start us, length us, event | category | flops | bytes accessed | tf_op | source)
XLA Modules:
  0.0 202.7 jit_solution(3986042912262208743)
XLA Ops:
  0.6 50.2 %shard_map.161 = (bf16[4,256,768]{2,1,0:T(8,128)(2,1)}, bf16[4,192,256]{2,1,0:T(8,128)(2,1)}, bf16[16,256,384]{2,1,0:T(8,128)(2,1)}, bf16[640,768]{1,0:T(8,128)(...) custom-call(s32[1,3]{1,0:T(1,128)} %lengths_ref.5, ...), custom_call_target="tpu_custom_call" | custom-call | tf_op jit(solution)/shard_map/pallas_call | solution.py:553
  50.9 1.7 collective-permute-start
  52.5 13.4 %shard_map.162 = (f32[4,192,256]{2,1,0:T(8,128)}, bf16[4,192,256]{2,1,0:T(8,128)(2,1)}, f32[4,8,256]{2,1,0:T(8,128)}) custom-call(s32[1,3]{1,0:T(1,128)} %lengths_ref.5, bf16[4,192,256]{2,1,0:T(8,128)(2,1)} %get-tuple-element.46.qt_ref, bf16[16,256,384]{2,1,0:T(8,128)(2,1)} %get-tuple-element.47.kv_ref), custom_call_target="tpu_custom_call" | custom-call | tf_op jit(solution)/shard_map/pallas_call | solution.py:146
  65.9 0.0 collective-permute-done.refs_0_
  65.9 0.0 copy-start.2
  65.9 0.8 copy-done.2
  66.7 30.7 %shard_map.163 = (bf16[256,768]{1,0:T(8,128)(2,1)}, f32[256,768]{1,0:T(8,128)}, bf16[4,192,256]{2,1,0:T(8,128)(2,1)}, bf16[4,2,48,768]{3,2,1,0:T(8,128)(2,1)}, b...) custom-call(bf16[4,192,256]{2,1,0:T(8,128)(2,1)} %get-tuple-element., ...), custom_call_target="tpu_custom_call" | custom-call | tf_op jit(solution)/shard_map/pallas_call | solution.py:911
  97.3 0.6 collective-permute-start.1
  98.0 1.5 collective-permute-start.2
  99.5 1.2 collective-permute-start.3
  100.8 1.6 collective-permute-start.4
  102.4 1.0 collective-permute-start.5
  103.4 19.6 %shard_map.164 = (f32[4,192,256]{2,1,0:T(8,128)}, bf16[16,256,384]{2,1,0:T(8,128)(2,1)}) custom-call(s32[1,3]{1,0:T(1,128)} %lengths_ref.5, bf16[4,192,256]{2,1,0:T(8,128)(2,1)} %get-tuple-element.46.qt_ref, bf16[16,256,384]{2,1,0:T(8,128)(2,1)} %get-tuple-element.47.kv_ref, f32[4,192,256]{2,1,0:T(8,128)} %get-tuple-element.54.ot_ref, ...), custom_call_target="tpu_custom_call" | custom-call | tf_op jit(solution)/shard_map/pallas_call | solution.py:231
  123.0 0.0 collective-permute-done.3.z_got_1
  123.0 0.0 copy-start.4
  123.0 0.1 collective-permute-done.4.z_got_2
  123.0 0.0 copy-start.5
  123.0 0.0 collective-permute-done.5.z_got_3
  123.0 0.0 copy-start.6
  123.0 0.0 collective-permute-done.1.y_got_hbm
  123.0 0.0 copy-start
  123.1 0.0 collective-permute-done.2.x_got_hbm
  123.1 0.0 copy-start.1
  123.1 0.6 copy-done.4
  123.7 0.1 copy-done.5
  123.8 0.1 copy-done.6
  123.9 0.2 copy-done
  124.1 0.2 copy-done.1
  124.3 74.4 %shard_map.165 = (bf16[16,16,768]{2,1,0:T(8,128)(2,1)}, bf16[2,144,768]{2,1,0:T(8,128)(2,1)}, bf16[2,4,48,192]{3,2,1,0:T(8,128)(2,1)}, bf16[2,4,48,384]{3,2,1,0:T(8,128)(2,1)}, bf16[48,2304]{1,0:T(8,128)(2,1)}) custom-call(s32[32]{0:T(128)} %bitcast.26, f32[4,192,256]{2,1,0:T(8,128)} %get-tuple-element.57.dq_hbm, bf16[4,2,2,256,384]{4,3,2,1,0:T(8,128)(2,1)} %bitcast.20, ...), custom_call_target="tpu_custom_call" | custom-call | tf_op jit(solution)/shard_map/pallas_call | solution.py:1487
  198.7 0.0 copy-start.3
  198.7 3.3 %shard_map.166 = (bf16[256,768]{1,0:T(8,128)(2,1)}, f32[48,2304]{1,0:T(8,128)}, f32[48,768]{1,0:T(8,128)}, f32[48,2304]{1,0:T(8,128)}, f32[72,768]{1,0:T(8,128)}, /*index=5*/f32[1,48]{1,0:T(1,128)}, f32[1,48]{1,0:T(1,128)}) custom-call(bf16[16,16,768]{2,1,0:T(8,128)(2,1)} %get-tuple-element.72.d_ref, bf16[2,144,768]{2,1,0:T(8,128)(2,1)} %get-tuple-element.73.w_ref, ...), custom_call_target="tpu_custom_call" | custom-call | tf_op jit(solution)/shard_map/pallas_call | solution.py:1617
  202.0 0.0 copy-done.3
  202.0 0.7 copy.19
Async XLA Ops:
  50.9 15.0 %collective-permute-start = (bf16[288,768]{1,0:T(8,128)(2,1)}, bf16[288,768]{1,0:T(8,128)(2,1)S(1)}, u32[]{:S(2)}, u32[]{:S(2)}) collective-permute-start(bf16[288,768]{1,0:T(8,128)(2,1)} %get-tuple-element.52), channel_id=1, source_target_pairs={{0,1},{1,0},{2,3},{3,2},{4,5},{5,4},{6,7},{7,6},{8,9},{9,8},{10,11... | collective-permute-start | bytes 1327112 | tf_op jit(solution)/shard_map/ppermute | solution.py:1661
  65.9 0.8 copy-start.2
  97.3 25.7 %collective-permute-start.1 = (bf16[1,4,2,48,768]{4,3,2,1,0:T(8,128)(2,1)}, bf16[1,4,2,48,768]{4,3,2,1,0:T(8,128)(2,1)S(1)}, u32[]{:S(2)}, u32[]{:S(2)}) collective-permute-start(bf16[1,4,2,48,768]{4,3,2,1,0:T(8,128)(2,1)} %get-tuple-element.65), channel_id=1, source_target_pairs={{0,1},{1,0},{2,3},{3,2},{4,5},{5,4},{6,7},{7,6},{8,9},{9,8},{10,11... | collective-permute-start | bytes 1769480 | tf_op jit(solution)/shard_map/ppermute | solution.py:1661
  98.0 25.1 %collective-permute-start.2 = (bf16[1,4,2,48,768]{4,3,2,1,0:T(8,128)(2,1)}, bf16[1,4,2,48,768]{4,3,2,1,0:T(8,128)(2,1)S(1)}, u32[]{:S(2)}, u32[]{:S(2)}) collective-permute-start(bf16[1,4,2,48,768]{4,3,2,1,0:T(8,128)(2,1)} %get-tuple-element.67), channel_id=1, source_target_pairs={{0,4},{2,6},{4,0},{6,2},{8,12},{10,14},{12,8},{14,10},{16,20},{18,... | collective-permute-start | bytes 1769480 | tf_op jit(solution)/shard_map/ppermute | solution.py:1658
  99.5 23.4 %collective-permute-start.3 = (bf16[2,2,48,768]{3,2,1,0:T(8,128)(2,1)}, bf16[2,2,48,768]{3,2,1,0:T(8,128)(2,1)S(1)}, u32[]{:S(2)}, u32[]{:S(2)}) collective-permute-start(bf16[2,2,48,768]{3,2,1,0:T(8,128)(2,1)} %get-tuple-element.69), channel_id=1, source_target_pairs={{0,8},{2,10},{4,12},{6,14},{8,16},{10,18},{12,20},{14,22},{16,24},... | collective-permute-start | bytes 884744 | tf_op jit(solution)/shard_map/ppermute | solution.py:1652
  100.8 22.2 %collective-permute-start.4 = (bf16[2,2,48,768]{3,2,1,0:T(8,128)(2,1)}, bf16[2,2,48,768]{3,2,1,0:T(8,128)(2,1)S(1)}, u32[]{:S(2)}, u32[]{:S(2)}) collective-permute-start(bf16[2,2,48,768]{3,2,1,0:T(8,128)(2,1)} %get-tuple-element.70), channel_id=1, source_target_pairs={{0,16},{2,18},{4,20},{6,22},{8,24},{10,26},{12,28},{14,30},{16,0},... | collective-permute-start | bytes 884744 | tf_op jit(solution)/shard_map/ppermute | solution.py:1652
  102.4 20.6 %collective-permute-start.5 = (bf16[2,2,48,768]{3,2,1,0:T(8,128)(2,1)}, bf16[2,2,48,768]{3,2,1,0:T(8,128)(2,1)S(1)}, u32[]{:S(2)}, u32[]{:S(2)}) collective-permute-start(bf16[2,2,48,768]{3,2,1,0:T(8,128)(2,1)} %get-tuple-element.71), channel_id=1, source_target_pairs={{0,24},{2,26},{4,28},{6,30},{8,0},{10,2},{12,4},{14,6},{16,8},{18,... | collective-permute-start | bytes 884744 | tf_op jit(solution)/shard_map/ppermute | solution.py:1652
  123.0 0.7 copy-start.4
  123.0 0.7 copy-start.5
  123.0 0.8 copy-start.6
  123.0 1.0 copy-start
  123.1 1.2 copy-start.1
  198.7 3.3 %copy-start.3 = (bf16[256,768]{1,0:T(8,128)(2,1)S(1)}, bf16[256,768]{1,0:T(8,128)(2,1)}, u32[]{:S(2)}) copy-start(bf16[256,768]{1,0:T(8,128)(2,1)} %get-tuple-element.53) | copy-start | bytes 1179652
